TPU v7x, 32 devices: a whole 2x2x4 slice. The times are simulated.
32 devices in a mesh: tm: 4 (over y, x), space: 8 (over z, core).
Axes of the slice: x: 2, y: 2, z: 4, core: 2. Of those that a mesh axis runs over, the one named last changes fastest.
Arguments:
- source: float32 [8, 2048, 128], P('tm', 'space'), may hold values from -6 to 6
- elem_scale: float32 [2048], P('space'), may hold values from 1 to 2
- diag_block: float32 [128, 128], replicated, as said below
- block_inverse: float32 [128, 128], replicated, as said below
- face_flux: float32 [4, 128, 128], replicated, may hold values from -0.072 to 0.072
- time_trace: float32 [128, 128], replicated, as said below
- neighbours: int32 [2048, 4], P('space'), may hold values from 0 to 287, as said below
- send_rows: int32 [8, 32], P('space'), may hold values from 0 to 255, as said below
Outputs:
- smoothed: float32 [8, 2048, 128], P('tm', 'space')
Inputs may be any that keep to these rules, and one draw needn't show every extreme that they name: `neighbours`: indexes the extended list of the element's own partition, of 288 positions; each of the 32 received positions is named by exactly one face of the partition's elements, and only the partition's sent elements name received positions. `send_rows`: each row holds 32 distinct local positions of its partition's elements. `diag_block`: the identity plus a skew-symmetric matrix plus a positive semidefinite matrix. `block_inverse`: the inverse of diag_block. `time_trace`: its largest singular value is at most 0.9.
All inputs are finite; a program needn't handle non-finite values.
Results may differ from a plain program's by a relative error of at most 0.0001.
Values sent between devices are 32-bit elements; how exact they have to be, the bound alone decides.
No kernel may reach another device: no remote copies, remote signals or barrier semaphores. Data moves between devices by JAX's collectives and lax.ppermute only.
A program may use at most 64 MiB of HBM per device.

v0:
```python
import jax
import jax.numpy as jnp
from jax import lax
from jax.sharding import PartitionSpec as P

DAMPING = 0.7


def with_halo(block, sides, width):
    for axis, dim in sides:
        count = lax.axis_size(axis)
        forward = [(i, i + 1) for i in range(count - 1)]
        forward.append((count - 1, 0))
        backward = [(target, source) for source, target in forward]
        low = lax.ppermute(
            lax.slice_in_dim(block, block.shape[dim] - width, None, axis=dim), axis, forward
        )
        high = lax.ppermute(lax.slice_in_dim(block, 0, width, axis=dim), axis, backward)
        block = jnp.concatenate([low, block, high], axis=dim)
    return block


def passed_along(x, axis, by):
    length = lax.axis_size(axis)
    pairs = [(i, i + by) for i in range(length) if 0 <= i + by < length]
    return lax.ppermute(x, axis, pairs)


def product(left, right):
    return jnp.dot(left, right, precision=lax.Precision.HIGHEST, preferred_element_type=jnp.float32)


def body(
    source, elem_scale, diag_block, block_inverse, face_flux, time_trace, neighbours, send_rows
):
    slab_count, elements, unknowns = source.shape
    send_order = send_rows[0]
    halo_rows = send_order.shape[0] // 2
    inv_scale = 1.0 / elem_scale
    coarse_scale = 1.0 / (2.0 * elem_scale - 1.0)
    coarse_count = slab_count // 2

    def operate(field):
        outgoing = field[:, send_order, :]
        padded = with_halo(outgoing, (("space", 1),), halo_rows)
        extended = jnp.concatenate(
            [field, padded[:, :halo_rows], padded[:, 3 * halo_rows :]], axis=1
        )
        face_term = jnp.zeros((slab_count * elements, unknowns), jnp.float32)
        for face_index in range(4):
            picked = jnp.take(extended, neighbours[:, face_index], axis=1)
            face_term = face_term + product(picked.reshape(-1, unknowns), face_flux[face_index])
        incoming = passed_along(field[-1], "tm", 1)
        earlier = jnp.concatenate([incoming[None], field[:-1]], axis=0)
        diagonal_term = (
            product(field.reshape(-1, unknowns), diag_block).reshape(field.shape)
            * elem_scale[None, :, None]
        )
        time_term = product(earlier.reshape(-1, unknowns), time_trace).reshape(field.shape)
        return diagonal_term - time_term - face_term.reshape(field.shape)

    def precondition(residual):
        return (
            product(residual.reshape(-1, unknowns), block_inverse).reshape(residual.shape)
            * inv_scale[None, :, None]
        )

    def smooth(solution):
        return solution + DAMPING * precondition(source - operate(solution))

    def coarse_step(state, rhs_slab):
        state = coarse_scale[:, None] * product(
            rhs_slab + product(state, time_trace), block_inverse
        )
        return (state, state)

    solution = DAMPING * precondition(source)
    solution = smooth(solution)
    residual = source - operate(solution)
    paired = residual.reshape(coarse_count, 2, elements, unknowns)
    coarse_rhs = paired[:, 0] + paired[:, 1]
    zero_state = jnp.zeros((elements, unknowns), jnp.float32)
    gathered_rhs = lax.all_gather(coarse_rhs, "tm", axis=0, tiled=True)
    final_state, every_state = lax.scan(coarse_step, zero_state, gathered_rhs)
    first_slab = lax.axis_index("tm") * coarse_count
    correction = lax.dynamic_slice_in_dim(every_state, first_slab, coarse_count, 0)
    solution = solution + jnp.repeat(correction, 2, axis=0)
    solution = smooth(solution)
    solution = smooth(solution)
    return solution


def solution(mesh):
    in_specs = (
        P("tm", "space", None),
        P("space"),
        P(),
        P(),
        P(),
        P(),
        P("space", None),
        P("space", None),
    )
    out_specs = P("tm", "space", None)
    return jax.shard_map(body, mesh=mesh, in_specs=in_specs, out_specs=out_specs, check_vma=False)
```

profile of v0, /device:TPU:0, one launch (start us, length us, event | category | flops | bytes accessed | tf_op | source)
XLA Modules:
  0.0 83.8 jit_solution(2443995638531701402)
XLA Ops:
  0.0 0.7 add_divide_fusion
  0.7 1.3 %fusion.19 = f32[2,256,128]{2,1,0:T(8,128)S(1)} fusion(f32[2,256,128]{2,1,0:T(8,128)} %param.12, f32[256]{0:T(256)S(1)} %get-tuple-element.105, f32[128,128]{1,0:T(8,128)} %param.15), kind=kOutput, calls=%fused_computation.66 | convolution fusion | flops 100794368 | bytes 590848 | tf_op jit(solution)/shard_map/dot_general | solution.py:30
  2.3 0.4 copy-done.8
  2.7 0.6 gather_fusion
  3.3 0.5 collective-permute-start.1
  3.9 4.1 %collective-permute-start.2 = (f32[2,16,128]{2,1,0:T(8,128)S(1)}, f32[2,16,128]{2,1,0:T(8,128)S(1)}, u32[]{:S(2)}, u32[]{:S(2)}) collective-permute-start(f32[2,16,128]{2,1,0:T(8,128)S(1)} %get-tuple-element.99), channel_id=1, source_target_pairs={{1,0},{2,1},{3,2},{4,3},{5,4},{6,5},{7,6},{0,7},{9,8},{10,9},{11,1... | collective-permute-start | bytes 49160 | tf_op jit(solution)/shard_map/ppermute | solution.py:18
  8.0 3.8 %collective-permute-start = (f32[256,128]{1,0:T(8,128)S(1)}, f32[256,128]{1,0:T(8,128)S(1)}, u32[]{:S(2)}, u32[]{:S(2)}) collective-permute-start(f32[256,128]{1,0:T(8,128)S(1)} %get-tuple-element.90), channel_id=1, source_target_pairs={{0,8},{8,16},{16,24},{1,9},{9,17},{17,25},{2,10},{10,18},{18,26},{... | collective-permute-start | bytes 393224 | tf_op jit(solution)/shard_map/ppermute | solution.py:26
  12.0 0.6 copy-done.6
  12.7 0.4 convolution_multiply_fusion.7
  13.4 1.0 %gather_fusion.4 = f32[256,2,128]{2,1,0:T(2,128)S(1)} fusion(f32[2,288,128]{2,0,1:T(2,128)S(1)} %copy.75, s32[1024]{0:T(1024)S(1)} %pad_clamp_fusion.3), kind=kCustom, calls=%fused_computation.clone | custom fusion | bytes 525312 | tf_op jit(solution)/shard_map/jit(_take)/gather | solution.py:51
  14.7 1.0 %gather_fusion.5 = f32[256,2,128]{2,1,0:T(2,128)S(1)} fusion(f32[2,288,128]{2,0,1:T(2,128)S(1)} %copy.75, s32[1024]{0:T(1024)S(1)} %pad_clamp_fusion.2), kind=kCustom, calls=%fused_computation.1.clone | custom fusion | bytes 525312 | tf_op jit(solution)/shard_map/jit(_take)/gather | solution.py:51
  16.1 1.0 %gather_fusion.6 = f32[256,2,128]{2,1,0:T(2,128)S(1)} fusion(f32[2,288,128]{2,0,1:T(2,128)S(1)} %copy.75, s32[1024]{0:T(1024)S(1)} %pad_clamp_fusion.1), kind=kCustom, calls=%fused_computation.2.clone | custom fusion | bytes 525312 | tf_op jit(solution)/shard_map/jit(_take)/gather | solution.py:51
  17.4 1.0 %gather_fusion.7 = f32[256,2,128]{2,1,0:T(2,128)S(1)} fusion(f32[2,288,128]{2,0,1:T(2,128)S(1)} %copy.75, s32[1024]{0:T(1024)S(1)} %pad_clamp_fusion), kind=kCustom, calls=%fused_computation.3.clone | custom fusion | bytes 525312 | tf_op jit(solution)/shard_map/jit(_take)/gather | solution.py:51
  18.8 0.9 %copy-done.4 = f32[4,128,128]{2,1,0:T(8,128)S(1)} copy-done((f32[4,128,128]{2,1,0:T(8,128)S(1)}, f32[4,128,128]{2,1,0:T(8,128)}, u32[]{:S(2)}) %copy-start.4) | copy-done | bytes 262168
  19.7 0.4 fusion.50
  20.1 0.4 convolution_add_fusion.12
  20.5 0.4 convolution_add_fusion.11
  20.9 0.4 convolution_add_fusion.10
  21.2 0.5 copy-done.1
  21.8 0.4 fusion.18
  22.2 0.5 copy-done.2
  22.6 0.4 fusion.16
  23.2 0.4 convolution_multiply_fusion.5
  23.6 0.6 gather_fusion.1
  24.3 3.5 %collective-permute-start.5 = (f32[2,16,128]{2,1,0:T(8,128)S(1)}, f32[2,16,128]{2,1,0:T(8,128)S(1)}, u32[]{:S(2)}, u32[]{:S(2)}) collective-permute-start(f32[2,16,128]{2,1,0:T(8,128)S(1)} %get-tuple-element.97), channel_id=1, source_target_pairs={{1,0},{2,1},{3,2},{4,3},{5,4},{6,5},{7,6},{0,7},{9,8},{10,9},{11,1... | collective-permute-start | bytes 49160 | tf_op jit(solution)/shard_map/ppermute | solution.py:18
  27.8 3.6 %collective-permute-start.3 = (f32[256,128]{1,0:T(8,128)S(1)}, f32[256,128]{1,0:T(8,128)S(1)}, u32[]{:S(2)}, u32[]{:S(2)}) collective-permute-start(f32[256,128]{1,0:T(8,128)S(1)} %get-tuple-element.88), channel_id=1, source_target_pairs={{0,8},{8,16},{16,24},{1,9},{9,17},{17,25},{2,10},{10,18},{18,26},{... | collective-permute-start | bytes 393224 | tf_op jit(solution)/shard_map/ppermute | solution.py:26
  31.7 1.0 %gather_fusion.8 = f32[256,2,128]{2,1,0:T(2,128)S(1)} fusion(f32[2,288,128]{2,0,1:T(2,128)S(1)} %copy.85, s32[1024]{0:T(1024)S(1)} %pad_clamp_fusion.3), kind=kCustom, calls=%fused_computation.4.clone | custom fusion | bytes 525312 | tf_op jit(solution)/shard_map/jit(_take)/gather | solution.py:51
  32.7 1.0 %gather_fusion.9 = f32[256,2,128]{2,1,0:T(2,128)S(1)} fusion(f32[2,288,128]{2,0,1:T(2,128)S(1)} %copy.85, s32[1024]{0:T(1024)S(1)} %pad_clamp_fusion.2), kind=kCustom, calls=%fused_computation.5.clone | custom fusion | bytes 525312 | tf_op jit(solution)/shard_map/jit(_take)/gather | solution.py:51
  33.7 1.0 %gather_fusion.10 = f32[256,2,128]{2,1,0:T(2,128)S(1)} fusion(f32[2,288,128]{2,0,1:T(2,128)S(1)} %copy.85, s32[1024]{0:T(1024)S(1)} %pad_clamp_fusion.1), kind=kCustom, calls=%fused_computation.6.clone | custom fusion | bytes 525312 | tf_op jit(solution)/shard_map/jit(_take)/gather | solution.py:51
  34.6 1.0 %gather_fusion.11 = f32[256,2,128]{2,1,0:T(2,128)S(1)} fusion(f32[2,288,128]{2,0,1:T(2,128)S(1)} %copy.85, s32[1024]{0:T(1024)S(1)} %pad_clamp_fusion), kind=kCustom, calls=%fused_computation.7.clone | custom fusion | bytes 525312 | tf_op jit(solution)/shard_map/jit(_take)/gather | solution.py:51
  36.0 0.4 fusion.48
  37.5 0.4 convolution_add_fusion.9
  37.9 0.4 convolution_add_fusion.8
  38.2 0.4 convolution_add_fusion.7
  38.6 0.4 fusion.14
  39.0 10.1 %all-gather = f32[4,1,256,128]{3,2,1,0:T(8,128)S(1)} all-gather(f32[1,1,256,128]{3,2,1,0:T(8,128)S(1)} %slice_add_fusion), channel_id=2, replica_groups=mesh['tm'=4,'space'=8] {'tm'}, dimensions={0}, use_global_device_ids=true | all-gather | bytes 655360 | tf_op jit(solution)/shard_map/all_gather | solution.py:83
  49.2 2.3 %while.13 = (s32[]{:T(128)}, f32[256,128]{1,0:T(8,128)S(1)}, f32[4,256,128]{2,1,0:T(8,128)S(1)}, f32[256]{0:T(256)S(1)}, f32[4,256,128]{2,1,0:T(8,128)S(1)}, /*i...) while((s32[]{:T(128)}, f32[256,128]{1,0:T(8,128)S(1)}, ...), condition=%wide.region_1.3_spmd.clone, body=%wide.region_0.0_spmd.clone.sunk | while | flops 100761600 | bytes 918639 | solution.py:84
  52.1 0.6 gather_fusion.2
  52.8 3.5 %collective-permute-start.8 = (f32[2,16,128]{2,1,0:T(8,128)S(1)}, f32[2,16,128]{2,1,0:T(8,128)S(1)}, u32[]{:S(2)}, u32[]{:S(2)}) collective-permute-start(f32[2,16,128]{2,1,0:T(8,128)S(1)} %get-tuple-element.95), channel_id=1, source_target_pairs={{1,0},{2,1},{3,2},{4,3},{5,4},{6,5},{7,6},{0,7},{9,8},{10,9},{11,1... | collective-permute-start | bytes 49160 | tf_op jit(solution)/shard_map/ppermute | solution.py:18
  56.3 2.7 %collective-permute-start.6 = (f32[256,128]{1,0:T(8,128)S(1)}, f32[256,128]{1,0:T(8,128)S(1)}, u32[]{:S(2)}, u32[]{:S(2)}) collective-permute-start(f32[256,128]{1,0:T(8,128)S(1)} %get-tuple-element.86), channel_id=1, source_target_pairs={{0,8},{8,16},{16,24},{1,9},{9,17},{17,25},{2,10},{10,18},{18,26},{... | collective-permute-start | bytes 393224 | tf_op jit(solution)/shard_map/ppermute | solution.py:26
  59.3 1.0 %gather_fusion.12 = f32[256,2,128]{2,1,0:T(2,128)S(1)} fusion(f32[2,288,128]{2,0,1:T(2,128)S(1)} %copy.95, s32[1024]{0:T(1024)S(1)} %pad_clamp_fusion.3), kind=kCustom, calls=%fused_computation.8.clone | custom fusion | bytes 525312 | tf_op jit(solution)/shard_map/jit(_take)/gather | solution.py:51
  60.3 1.0 %gather_fusion.13 = f32[256,2,128]{2,1,0:T(2,128)S(1)} fusion(f32[2,288,128]{2,0,1:T(2,128)S(1)} %copy.95, s32[1024]{0:T(1024)S(1)} %pad_clamp_fusion.2), kind=kCustom, calls=%fused_computation.9.clone | custom fusion | bytes 525312 | tf_op jit(solution)/shard_map/jit(_take)/gather | solution.py:51
  61.3 1.0 %gather_fusion.14 = f32[256,2,128]{2,1,0:T(2,128)S(1)} fusion(f32[2,288,128]{2,0,1:T(2,128)S(1)} %copy.95, s32[1024]{0:T(1024)S(1)} %pad_clamp_fusion.1), kind=kCustom, calls=%fused_computation.10.clone | custom fusion | bytes 525312 | tf_op jit(solution)/shard_map/jit(_take)/gather | solution.py:51
  62.3 1.0 %gather_fusion.15 = f32[256,2,128]{2,1,0:T(2,128)S(1)} fusion(f32[2,288,128]{2,0,1:T(2,128)S(1)} %copy.95, s32[1024]{0:T(1024)S(1)} %pad_clamp_fusion), kind=kCustom, calls=%fused_computation.11.clone | custom fusion | bytes 525312 | tf_op jit(solution)/shard_map/jit(_take)/gather | solution.py:51
  63.6 0.4 fusion.46
  65.1 0.4 convolution_add_fusion.6
  65.5 0.4 convolution_add_fusion.5
  65.9 0.4 convolution_add_fusion.4
  66.2 0.4 fusion.11
  66.6 0.4 fusion.9
  67.2 0.4 convolution_multiply_fusion.2
  67.6 0.6 gather_fusion.3
  68.3 3.5 %collective-permute-start.11 = (f32[2,16,128]{2,1,0:T(8,128)S(1)}, f32[2,16,128]{2,1,0:T(8,128)S(1)}, u32[]{:S(2)}, u32[]{:S(2)}) collective-permute-start(f32[2,16,128]{2,1,0:T(8,128)S(1)} %get-tuple-element.93), channel_id=1, source_target_pairs={{1,0},{2,1},{3,2},{4,3},{5,4},{6,5},{7,6},{0,7},{9,8},{10,9},{11,1... | collective-permute-start | bytes 49160 | tf_op jit(solution)/shard_map/ppermute | solution.py:18
  71.8 3.4 %collective-permute-start.9 = (f32[256,128]{1,0:T(8,128)S(1)}, f32[256,128]{1,0:T(8,128)S(1)}, u32[]{:S(2)}, u32[]{:S(2)}) collective-permute-start(f32[256,128]{1,0:T(8,128)S(1)} %get-tuple-element.84), channel_id=1, source_target_pairs={{0,8},{8,16},{16,24},{1,9},{9,17},{17,25},{2,10},{10,18},{18,26},{... | collective-permute-start | bytes 393224 | tf_op jit(solution)/shard_map/ppermute | solution.py:26
  75.5 1.0 %gather_fusion.16 = f32[256,2,128]{2,1,0:T(2,128)S(1)} fusion(f32[2,288,128]{2,0,1:T(2,128)S(1)} %copy.105, s32[1024]{0:T(1024)S(1)} %pad_clamp_fusion.3), kind=kCustom, calls=%fused_computation.12.clone | custom fusion | bytes 525312 | tf_op jit(solution)/shard_map/jit(_take)/gather | solution.py:51
  76.4 1.0 %gather_fusion.17 = f32[256,2,128]{2,1,0:T(2,128)S(1)} fusion(f32[2,288,128]{2,0,1:T(2,128)S(1)} %copy.105, s32[1024]{0:T(1024)S(1)} %pad_clamp_fusion.2), kind=kCustom, calls=%fused_computation.13.clone | custom fusion | bytes 525312 | tf_op jit(solution)/shard_map/jit(_take)/gather | solution.py:51
  77.4 1.0 %gather_fusion.18 = f32[256,2,128]{2,1,0:T(2,128)S(1)} fusion(f32[2,288,128]{2,0,1:T(2,128)S(1)} %copy.105, s32[1024]{0:T(1024)S(1)} %pad_clamp_fusion.1), kind=kCustom, calls=%fused_computation.14.clone | custom fusion | bytes 525312 | tf_op jit(solution)/shard_map/jit(_take)/gather | solution.py:51
  78.4 1.0 %gather_fusion.19 = f32[256,2,128]{2,1,0:T(2,128)S(1)} fusion(f32[2,288,128]{2,0,1:T(2,128)S(1)} %copy.105, s32[1024]{0:T(1024)S(1)} %pad_clamp_fusion), kind=kCustom, calls=%fused_computation.15.clone | custom fusion | bytes 525312 | tf_op jit(solution)/shard_map/jit(_take)/gather | solution.py:51
  79.8 0.4 fusion.44
  81.2 0.4 convolution_add_fusion.3
  81.6 0.4 convolution_add_fusion.2
  82.0 0.4 convolution_add_fusion.1
  82.4 0.4 fusion.7
  82.7 1.1 %fusion.5 = f32[2,256,128]{2,1,0:T(8,128)} fusion(f32[2,256,128]{2,1,0:T(8,128)S(1)} %fusion.9, f32[2,256,128]{2,1,0:T(8,128)S(1)} %fusion.7, f32[256]{0:T(256)S(1)} %get-tuple-element.105, f32[128,128]{1,0:T(8,128)S(1)} %get-tuple-element.180), kind=kOutput, calls=%fused_computation.29 | convolution fusion | flops 100859904 | bytes 852992 | tf_op jit(solution)/shard_map/dot_general | solution.py:30
  (113 shorter events, 10.5 us)
Async XLA Ops:
  0.0 12.0 %copy-start = (f32[128,128]{1,0:T(8,128)S(1)}, f32[128,128]{1,0:T(8,128)}, u32[]{:S(2)}) copy-start(f32[128,128]{1,0:T(8,128)} %param.14) | copy-start | bytes 196612
  2.0 0.7 copy-start.8
  3.3 9.7 %collective-permute-start.1 = (f32[2,16,128]{2,1,0:T(8,128)S(1)}, f32[2,16,128]{2,1,0:T(8,128)S(1)}, u32[]{:S(2)}, u32[]{:S(2)}) collective-permute-start(f32[2,16,128]{2,1,0:T(8,128)S(1)} %get-tuple-element.98), channel_id=1, source_target_pairs={{0,1},{1,2},{2,3},{3,4},{4,5},{5,6},{6,7},{7,0},{8,9},{9,10},{10,1... | collective-permute-start | bytes 49160 | tf_op jit(solution)/shard_map/ppermute | solution.py:15
  3.9 9.2 %collective-permute-start.2 = (f32[2,16,128]{2,1,0:T(8,128)S(1)}, f32[2,16,128]{2,1,0:T(8,128)S(1)}, u32[]{:S(2)}, u32[]{:S(2)}) collective-permute-start(f32[2,16,128]{2,1,0:T(8,128)S(1)} %get-tuple-element.99), channel_id=1, source_target_pairs={{1,0},{2,1},{3,2},{4,3},{5,4},{6,5},{7,6},{0,7},{9,8},{10,9},{11,1... | collective-permute-start | bytes 49160 | tf_op jit(solution)/shard_map/ppermute | solution.py:18
  8.0 3.9 %copy-start.7 = (s32[256,4]{0,1:T(4,128)S(1)}, s32[256,4]{0,1:T(4,128)}, u32[]{:S(2)}) copy-start(s32[256,4]{0,1:T(4,128)} %param.18) | copy-start | bytes 12292
  8.0 13.2 %collective-permute-start = (f32[256,128]{1,0:T(8,128)S(1)}, f32[256,128]{1,0:T(8,128)S(1)}, u32[]{:S(2)}, u32[]{:S(2)}) collective-permute-start(f32[256,128]{1,0:T(8,128)S(1)} %get-tuple-element.90), channel_id=1, source_target_pairs={{0,8},{8,16},{16,24},{1,9},{9,17},{17,25},{2,10},{10,18},{18,26},{... | collective-permute-start | bytes 393224 | tf_op jit(solution)/shard_map/ppermute | solution.py:26
  12.0 0.7 copy-start.6
  18.8 1.0 %copy-start.4 = (f32[4,128,128]{2,1,0:T(8,128)S(1)}, f32[4,128,128]{2,1,0:T(8,128)}, u32[]{:S(2)}) copy-start(f32[4,128,128]{2,1,0:T(8,128)} %param.16) | copy-start | bytes 786436
  20.8 1.0 %copy-start.1 = (f32[2,256,128]{2,1,0:T(8,128)S(1)}, f32[2,256,128]{2,1,0:T(8,128)}, u32[]{:S(2)}) copy-start(f32[2,256,128]{2,1,0:T(8,128)} %param.12) | copy-start | bytes 786436
  20.8 0.9 %copy-start.3 = (f32[128,128]{1,0:T(8,128)S(1)}, f32[128,128]{1,0:T(8,128)}, u32[]{:S(2)}) copy-start(f32[128,128]{1,0:T(8,128)} %param.17) | copy-start | bytes 196612
  21.8 0.8 %copy-start.2 = (f32[128,128]{1,0:T(8,128)S(1)}, f32[128,128]{1,0:T(8,128)}, u32[]{:S(2)}) copy-start(f32[128,128]{1,0:T(8,128)} %param.15) | copy-start | bytes 196612
  24.2 7.2 %collective-permute-start.4 = (f32[2,16,128]{2,1,0:T(8,128)S(1)}, f32[2,16,128]{2,1,0:T(8,128)S(1)}, u32[]{:S(2)}, u32[]{:S(2)}) collective-permute-start(f32[2,16,128]{2,1,0:T(8,128)S(1)} %get-tuple-element.96), channel_id=1, source_target_pairs={{0,1},{1,2},{2,3},{3,4},{4,5},{5,6},{6,7},{7,0},{8,9},{9,10},{10,1... | collective-permute-start | bytes 49160 | tf_op jit(solution)/shard_map/ppermute | solution.py:15
  24.3 7.1 %collective-permute-start.5 = (f32[2,16,128]{2,1,0:T(8,128)S(1)}, f32[2,16,128]{2,1,0:T(8,128)S(1)}, u32[]{:S(2)}, u32[]{:S(2)}) collective-permute-start(f32[2,16,128]{2,1,0:T(8,128)S(1)} %get-tuple-element.97), channel_id=1, source_target_pairs={{1,0},{2,1},{3,2},{4,3},{5,4},{6,5},{7,6},{0,7},{9,8},{10,9},{11,1... | collective-permute-start | bytes 49160 | tf_op jit(solution)/shard_map/ppermute | solution.py:18
  27.8 10.8 %collective-permute-start.3 = (f32[256,128]{1,0:T(8,128)S(1)}, f32[256,128]{1,0:T(8,128)S(1)}, u32[]{:S(2)}, u32[]{:S(2)}) collective-permute-start(f32[256,128]{1,0:T(8,128)S(1)} %get-tuple-element.88), channel_id=1, source_target_pairs={{0,8},{8,16},{16,24},{1,9},{9,17},{17,25},{2,10},{10,18},{18,26},{... | collective-permute-start | bytes 393224 | tf_op jit(solution)/shard_map/ppermute | solution.py:26
  39.0 10.2 %copy-start.5 = (f32[4,256,128]{2,1,0:T(8,128)S(1)}, f32[4,256,128]{2,1,0:T(8,128)}, u32[]{:S(2)}) copy-start(f32[4,256,128]{2,1,0:T(8,128)} %custom-call.41) | copy-start | bytes 1572868
  52.7 6.3 %collective-permute-start.7 = (f32[2,16,128]{2,1,0:T(8,128)S(1)}, f32[2,16,128]{2,1,0:T(8,128)S(1)}, u32[]{:S(2)}, u32[]{:S(2)}) collective-permute-start(f32[2,16,128]{2,1,0:T(8,128)S(1)} %get-tuple-element.94), channel_id=1, source_target_pairs={{0,1},{1,2},{2,3},{3,4},{4,5},{5,6},{6,7},{7,0},{8,9},{9,10},{10,1... | collective-permute-start | bytes 49160 | tf_op jit(solution)/shard_map/ppermute | solution.py:15
  52.8 6.3 %collective-permute-start.8 = (f32[2,16,128]{2,1,0:T(8,128)S(1)}, f32[2,16,128]{2,1,0:T(8,128)S(1)}, u32[]{:S(2)}, u32[]{:S(2)}) collective-permute-start(f32[2,16,128]{2,1,0:T(8,128)S(1)} %get-tuple-element.95), channel_id=1, source_target_pairs={{1,0},{2,1},{3,2},{4,3},{5,4},{6,5},{7,6},{0,7},{9,8},{10,9},{11,1... | collective-permute-start | bytes 49160 | tf_op jit(solution)/shard_map/ppermute | solution.py:18
  56.3 9.9 %collective-permute-start.6 = (f32[256,128]{1,0:T(8,128)S(1)}, f32[256,128]{1,0:T(8,128)S(1)}, u32[]{:S(2)}, u32[]{:S(2)}) collective-permute-start(f32[256,128]{1,0:T(8,128)S(1)} %get-tuple-element.86), channel_id=1, source_target_pairs={{0,8},{8,16},{16,24},{1,9},{9,17},{17,25},{2,10},{10,18},{18,26},{... | collective-permute-start | bytes 393224 | tf_op jit(solution)/shard_map/ppermute | solution.py:26
  68.2 7.0 %collective-permute-start.10 = (f32[2,16,128]{2,1,0:T(8,128)S(1)}, f32[2,16,128]{2,1,0:T(8,128)S(1)}, u32[]{:S(2)}, u32[]{:S(2)}) collective-permute-start(f32[2,16,128]{2,1,0:T(8,128)S(1)} %get-tuple-element.92), channel_id=1, source_target_pairs={{0,1},{1,2},{2,3},{3,4},{4,5},{5,6},{6,7},{7,0},{8,9},{9,10},{10,1... | collective-permute-start | bytes 49160 | tf_op jit(solution)/shard_map/ppermute | solution.py:15
  68.3 6.9 %collective-permute-start.11 = (f32[2,16,128]{2,1,0:T(8,128)S(1)}, f32[2,16,128]{2,1,0:T(8,128)S(1)}, u32[]{:S(2)}, u32[]{:S(2)}) collective-permute-start(f32[2,16,128]{2,1,0:T(8,128)S(1)} %get-tuple-element.93), channel_id=1, source_target_pairs={{1,0},{2,1},{3,2},{4,3},{5,4},{6,5},{7,6},{0,7},{9,8},{10,9},{11,1... | collective-permute-start | bytes 49160 | tf_op jit(solution)/shard_map/ppermute | solution.py:18
  71.8 10.6 %collective-permute-start.9 = (f32[256,128]{1,0:T(8,128)S(1)}, f32[256,128]{1,0:T(8,128)S(1)}, u32[]{:S(2)}, u32[]{:S(2)}) collective-permute-start(f32[256,128]{1,0:T(8,128)S(1)} %get-tuple-element.84), channel_id=1, source_target_pairs={{0,8},{8,16},{16,24},{1,9},{9,17},{17,25},{2,10},{10,18},{18,26},{... | collective-permute-start | bytes 393224 | tf_op jit(solution)/shard_map/ppermute | solution.py:26
where the time goes:
time: 84.2 us; the launch traced here: 83.8 us
  starting transfers between devices  28.9 us (34%)
  local copies, waits for them, and re-layouts  23.3 us (28%)
  matrix products  14 us (17%)
  blocking collectives  10.1 us (12%)
  other arithmetic  6.3 us (7%)
  between operations  1.08 us (1%)
    gather x16, local copies, waits for them, and re-layouts, operate(): picked = jnp.take(extended, neighbours[:, face_index], axis=1)  15.6 us
    ppermute x4, starting transfers between devices, with_halo(): lax.ppermute(lax.slice_in_dim(block, 0, width, axis=dim), axis, backward)  14.7 us
    dot_general x36, matrix products, product(): jnp.dot(left, right, precision=lax.Precision.HIGHEST, preferred_element_t...  14 us
    ppermute x4, starting transfers between devices, passed_along(): return lax.ppermute(x, axis, pairs)  13.5 us
    all_gather x1, blocking collectives, body(): gathered_rhs = lax.all_gather(coarse_rhs, 'tm', axis=0, tiled=True)  10.1 us
    select_n x20, other arithmetic, operate(): picked = jnp.take(extended, neighbours[:, face_index], axis=1)  5.39 us
    unnamed x18, local copies, waits for them, and re-layouts  3.04 us
    gather x8, local copies, waits for them, and re-layouts, operate(): outgoing = field[:, send_order, :]  2.45 us
  transfers between devices with their start and end apart: 12, of which 0 were waited for; matrix products, arithmetic and copies ran while one was open for 34% of the time, Pallas kernels for 0%

commit v1 on v0

v1 whole, which is shorter than its diff:
```python
import jax
import jax.numpy as jnp
from jax import lax
from jax.experimental import pallas as pl
from jax.experimental.pallas import tpu as pltpu
from jax.sharding import PartitionSpec as P

DAMPING = 0.7
F32 = jnp.float32
BF16 = jnp.bfloat16
VMEM = pltpu.VMEM
SMEM = pltpu.SMEM

W_DIAG, W_FACE, W_SOURCE_TIME, W_TIME = 0, 1, 5, 6


def call(kernel, out_shapes, args, spaces=None, scratch=(), flops=4e8):
    spaces = spaces or [VMEM] * len(args)
    return pl.pallas_call(
        kernel,
        out_shape=[jax.ShapeDtypeStruct(s, d) for s, d in out_shapes],
        in_specs=[pl.BlockSpec(memory_space=s) for s in spaces],
        out_specs=[pl.BlockSpec(memory_space=VMEM)] * len(out_shapes),
        scratch_shapes=list(scratch),
        compiler_params=pltpu.CompilerParams(vmem_limit_bytes=24 << 20),
        cost_estimate=pl.CostEstimate(flops=int(flops), bytes_accessed=1 << 20, transcendentals=0),
    )(*args)


def split(x):
    head = x.astype(BF16)
    tail = (x - head.astype(F32)).astype(BF16)
    return jnp.concatenate([head, tail], axis=1)


def halves(x):
    width = x.shape[1] // 2
    return x[:, :width] + x[:, width:]


def dot(left, right):
    return jnp.dot(left, right, preferred_element_type=F32)


def dot32(left, right):
    return jnp.dot(left, right, precision=lax.Precision.HIGHEST, preferred_element_type=F32)


def product(parts, tile):
    return halves(dot(parts, tile))


def weight_tile(w):
    head = w.astype(BF16)
    tail = (w - head.astype(F32)).astype(BF16)
    top = jnp.concatenate([head, tail], axis=1)
    low = jnp.concatenate([head, jnp.zeros_like(head)], axis=1)
    return jnp.concatenate([top, low], axis=0)


def column(row, width):
    return jnp.transpose(jnp.broadcast_to(row, (width, row.shape[1])))


def own_faces(faces, pick_ref, weights_ref, parts):
    count = len(parts)
    width = parts[0].shape[1]
    rows = parts[0].shape[0]
    every = jnp.concatenate(parts, axis=1) if count > 1 else parts[0]
    sums = [None] * count
    for face in range(faces):
        picked = dot(pick_ref[face * rows : (face + 1) * rows, :], every).astype(BF16)
        for i in range(count):
            term = dot(picked[:, i * width : (i + 1) * width], weights_ref[W_FACE + face])
            sums[i] = term if sums[i] is None else sums[i] + term
    return [halves(s) for s in sums]


def arrived(from_e, from_o, count):
    even = lax.axis_index("space") % 2 == 0
    left = jnp.where(even, from_o[...], from_e[...])
    right = jnp.where(even, from_e[...], from_o[...])
    rows = left.shape[0] // count
    return [
        jnp.concatenate([left[i * rows : (i + 1) * rows], right[i * rows : (i + 1) * rows]], axis=0)
        for i in range(count)
    ]


def far_faces(faces, rows_in, weights_ref):
    count = len(rows_in)
    n = rows_in[0].shape[0]
    parts = split(jnp.concatenate(rows_in, axis=0) if count > 1 else rows_in[0])
    per_face = [product(parts, weights_ref[W_FACE + f]) for f in range(faces)]
    lanes = [
        split(jnp.concatenate([u[i * n : (i + 1) * n] for u in per_face], axis=0))
        for i in range(count)
    ]
    return jnp.concatenate(lanes, axis=1) if count > 1 else lanes[0]


def spread(select, table, count):
    total = dot(select, table)
    width = total.shape[1] // count
    return [halves(total[:, i * width : (i + 1) * width]) for i in range(count)]


def put_sent(e_ref, o_ref, slabs):
    rows = slabs[0].shape[0] // 2
    for i, s in enumerate(slabs):
        e_ref[i * rows : (i + 1) * rows, :] = s[:rows]
        o_ref[i * rows : (i + 1) * rows, :] = s[rows:]


def at_sent(sent_ref, values):
    every = jnp.concatenate([split(v) for v in values], axis=1)
    return spread(sent_ref[...], every, len(values))


def body(
    source, elem_scale, diag_block, block_inverse, face_flux, time_trace, neighbours, send_rows
):
    slabs, elements, width = source.shape
    faces = neighbours.shape[1]
    sent = send_rows.shape[1]
    halo = sent // 2
    groups = lax.axis_size("tm")
    ring = lax.axis_size("space")
    flat = source.reshape(slabs * elements, width)
    scale_row = elem_scale.reshape(1, elements)
    faces_row = neighbours.T
    stack = W_TIME + groups - 1
    full = ((elements, width), F32)
    two = ((slabs * elements, width), F32)
    edge = ((slabs * halo, width), F32)
    far = faces * sent

    swap_e = [(i, i ^ 1) for i in range(ring)]
    swap_o = [(i, (i + 1) % ring if i % 2 else (i - 1) % ring) for i in range(ring)]

    def exchange(to_e, to_o):
        return lax.ppermute(to_e, "space", swap_e), lax.ppermute(to_o, "space", swap_o)

    def later(x, by):
        return lax.ppermute(x, "tm", [(i, (i + by) % groups) for i in range(groups)])

    def sent_at(send_ref, i):
        first = jnp.where(lax.axis_index("space") % 2 == 0, halo, 0)
        return send_ref[0, lax.rem(first + i, sent)]

    def first_kernel(s_ref, scale_ref, inv_ref, send_ref, e_ref, o_ref, x_ref, g_ref):
        sigma = DAMPING / column(scale_ref[...], width)
        for t in range(slabs):
            x_ref[t * elements : (t + 1) * elements, :] = (
                s_ref[t * elements : (t + 1) * elements, :] * sigma
            )
        for i in range(sent):
            at = sent_at(send_ref, i)
            base = (i // halo) * slabs * halo + i % halo
            for t in range(slabs):
                g_ref[base + t * halo : base + t * halo + 1, :] = x_ref[
                    pl.ds(t * elements + at, 1), :
                ]
        out = dot32(g_ref[...], inv_ref[...])
        e_ref[...] = out[: slabs * halo]
        o_ref[...] = out[slabs * halo :]

    e0, o0 = call(
        first_kernel,
        [edge, edge],
        [flat, scale_row, block_inverse, send_rows],
        spaces=[VMEM, VMEM, VMEM, SMEM],
        scratch=[VMEM((slabs * elements, width), F32), VMEM((slabs * sent, width), F32)],
        flops=1e7,
    )
    before = later(source[-1], 1)
    re0, ro0 = exchange(e0, o0)

    def setup_kernel(
        s_ref, scale_ref, d_ref, inv_ref, f_ref, t_ref, nbr_ref, send_ref,
        v_ref, part_ref, psent_ref, sigs_ref, w_ref, pick_ref, q_ref, qs_ref, sent_ref,
        sig_ref, frac_ref, rows_ref,
    ):
        inv = inv_ref[...]
        trace = dot32(t_ref[...], inv)
        w_ref[W_DIAG] = weight_tile(dot32(d_ref[...], inv))
        for f in range(faces):
            w_ref[W_FACE + f] = weight_tile(dot32(f_ref[f], inv))
        w_ref[W_SOURCE_TIME] = weight_tile(dot32(inv, trace))
        power = trace
        for a in range(groups - 1):
            w_ref[W_TIME + a] = weight_tile(power)
            if a < groups - 2:
                power = dot32(power, trace)
        scale = column(scale_ref[...], width)
        sigma = DAMPING / scale
        sig_ref[...] = sigma
        frac_ref[...] = 1.0 / (2.0 * scale - 1.0)
        lane = lax.broadcasted_iota(jnp.int32, (elements, elements), 1)
        spot = lax.broadcasted_iota(jnp.int32, (elements, far), 1)
        wanted = jnp.zeros((elements, far), jnp.int32)
        for f in range(faces):
            wide = column(nbr_ref[f : f + 1, :], elements)
            pick_ref[f * elements : (f + 1) * elements, :] = jnp.where(
                wide == lane, 1.0, 0.0
            ).astype(BF16)
            wanted = jnp.where(spot // sent == f, column(nbr_ref[f : f + 1, :], far), wanted)
        q = jnp.where(wanted == elements + spot % sent, 1.0, 0.0).astype(BF16)
        q_ref[...] = q
        strip = lax.broadcasted_iota(jnp.int32, (1, elements), 1)
        for i in range(sent):
            rows_ref[i : i + 1, :] = jnp.where(strip == sent_at(send_ref, i), 1.0, 0.0)
        chosen = rows_ref[...].astype(BF16)
        sent_ref[...] = chosen
        qs_ref[...] = dot(chosen, q).astype(BF16)
        head = weight_tile(inv)
        v = [
            sigma * product(split(s_ref[t * elements : (t + 1) * elements, :]), head)
            for t in range(slabs)
        ]
        cut = [split(x) for x in v]
        near = own_faces(faces, pick_ref, w_ref, cut)
        parts = []
        for t in range(slabs):
            term = near[t]
            if t:
                term = term + product(cut[t - 1], w_ref[W_TIME])
            parts.append(
                2.0 * v[t] - DAMPING * product(cut[t], w_ref[W_DIAG]) + sigma * term
            )
            v_ref[t * elements : (t + 1) * elements, :] = v[t]
            part_ref[t * elements : (t + 1) * elements, :] = parts[t]
        got = at_sent(sent_ref, parts + [sigma])
        for t in range(slabs):
            psent_ref[t * sent : (t + 1) * sent, :] = got[t]
        sigs_ref[...] = got[slabs]

    (
        v0, part1, psent1, sig_sent, weights, pick, q_all, q_sent, choose, sigma_all, frac_all,
    ) = call(
        setup_kernel,
        [
            two, two, ((slabs * sent, width), F32), ((sent, width), F32),
            ((stack, 2 * width, 2 * width), BF16), ((faces * elements, elements), BF16),
            ((elements, far), BF16), ((sent, far), BF16), ((sent, elements), BF16), full, full,
        ],
        [
            flat, scale_row, diag_block, block_inverse, face_flux, time_trace, faces_row,
            send_rows,
        ],
        spaces=[VMEM] * 7 + [SMEM],
        scratch=[VMEM((sent, elements), F32)],
        flops=2e9,
    )

    def time_mask(x, by=1):
        return jnp.where(lax.axis_index("tm") >= by, x, jnp.zeros_like(x))

    def edge_one(
        re_ref, ro_ref, b_ref, psent_ref, sigs_ref, w_ref, qs_ref, sent_ref, e_ref, o_ref
    ):
        table = far_faces(faces, arrived(re_ref, ro_ref, slabs), w_ref)
        add = spread(qs_ref[...], table, slabs)
        picked = dot(sent_ref[...], split(b_ref[...])).astype(BF16)
        old = time_mask(product(picked, w_ref[W_SOURCE_TIME]))
        sig = sigs_ref[...]
        new = [psent_ref[t * sent : (t + 1) * sent, :] + sig * add[t] for t in range(slabs)]
        new[0] = new[0] + sig * sig * old
        put_sent(e_ref, o_ref, new)

    e1, o1 = call(
        edge_one,
        [edge, edge],
        [re0, ro0, before, psent1, sig_sent, weights, q_sent, choose],
        flops=1e7,
    )
    re1, ro1 = exchange(e1, o1)

    def middle(
        re_ref, ro_ref, b_ref, part_ref, v_ref, w_ref, pick_ref, q_ref, sig_ref, frac_ref,
        v1_ref, pa_ref, pb_ref, wp_ref, x_ref,
    ):
        sigma = sig_ref[...]
        frac = frac_ref[...]
        add = spread(q_ref[...], far_faces(faces, arrived(re_ref, ro_ref, slabs), w_ref), slabs)
        old = time_mask(product(split(b_ref[...]), w_ref[W_SOURCE_TIME]))
        va = part_ref[:elements, :] + sigma * add[0] + sigma * sigma * old
        vb = part_ref[elements:, :] + sigma * add[1]
        v0a, v0b = v_ref[:elements, :], v_ref[elements:, :]
        v1_ref[...] = vb
        ca, cb = split(va), split(vb)
        ga, gb = own_faces(faces, pick_ref, w_ref, [ca, cb])
        da, db = product(ca, w_ref[W_DIAG]), product(cb, w_ref[W_DIAG])
        ta, tb = product(ca, w_ref[W_TIME]), product(cb, w_ref[W_TIME])
        pa_ref[...] = va + v0a - DAMPING * da + sigma * ga
        pb_ref[...] = vb + v0b - DAMPING * db + sigma * (ta + gb)
        wp_ref[...] = (
            frac * (((v0a + v0b) - DAMPING * (da + db)) / sigma + ta + ga + gb) + vb
        )
        x_ref[...] = v0b + sigma * (ta - tb)

    v1b, pa0, pb0, wp, x_own = call(
        middle,
        [full] * 5,
        [re0, ro0, before, part1, v0, weights, pick, q_all, sigma_all, frac_all],
        flops=2e9,
    )

    def coarse_kernel(
        re_ref, ro_ref, wp_ref, pa_ref, pb_ref, w_ref, q_ref, sig_ref, frac_ref,
        w_out, pa_out, pb_out,
    ):
        add = spread(q_ref[...], far_faces(faces, arrived(re_ref, ro_ref, slabs), w_ref), slabs)
        w_out[...] = wp_ref[...] + frac_ref[...] * (add[0] + add[1])
        pa_out[...] = pa_ref[...] + sig_ref[...] * add[0]
        pb_out[...] = pb_ref[...] + sig_ref[...] * add[1]

    w_own, pa1, pb1 = call(
        coarse_kernel,
        [full] * 3,
        [re1, ro1, wp, pa0, pb0, weights, q_all, sigma_all, frac_all],
        flops=1e7,
    )
    earlier = [later(w_own, a) for a in range(1, groups)]
    x_before = later(x_own, 1)

    def recur(*refs):
        olds = refs[: groups - 1]
        w_own_ref, v1_ref, w_ref, sent_ref, frac_ref, c_ref, d_ref, e_ref, o_ref = refs[
            groups - 1 :
        ]
        frac = frac_ref[...]
        d = time_mask(olds[0][...])
        c = w_own_ref[...] - v1_ref[...]
        power = frac
        for a in range(1, groups):
            cut = split(time_mask(power * olds[a - 1][...], a))
            c = c + product(cut, w_ref[W_TIME + a - 1])
            if a < groups - 1:
                cut = split(time_mask(power * olds[a][...], a + 1))
                d = d + product(cut, w_ref[W_TIME + a - 1])
                power = power * frac
        c_ref[...] = c
        d_ref[...] = d
        put_sent(e_ref, o_ref, at_sent(sent_ref, [c, d]))

    c_all, d_all, e2, o2 = call(
        recur,
        [full, full, edge, edge],
        [*earlier, w_own, v1b, weights, choose, frac_all],
        flops=1e8,
    )
    re2, ro2 = exchange(e2, o2)

    def second(
        c_in, d_in, xb_ref, pa_ref, pb_ref, w_ref, pick_ref, sig_ref, sent_ref,
        a_ref, b_ref, z_ref, ps_ref,
    ):
        sigma = sig_ref[...]
        c, d = c_in[...], d_in[...]
        cc, cd = split(c), split(d)
        gc, gd = own_faces(faces, pick_ref, w_ref, [cc, cd])
        same = c - DAMPING * product(cc, w_ref[W_DIAG]) + sigma * gc
        td = product(cd, w_ref[W_TIME])
        a = pa_ref[...] + same + sigma * td
        b = pb_ref[...] + same + sigma * product(cc, w_ref[W_TIME])
        a_ref[...] = a
        b_ref[...] = b
        z_ref[...] = (
            time_mask(xb_ref[...]) + d - DAMPING * product(cd, w_ref[W_DIAG]) + sigma * (td + gd)
        )
        got = at_sent(sent_ref, [a, b])
        for t in range(slabs):
            ps_ref[t * sent : (t + 1) * sent, :] = got[t]

    a3, b3, z3, psent3 = call(
        second,
        [full, full, full, ((slabs * sent, width), F32)],
        [c_all, d_all, x_before, pa1, pb1, weights, pick, sigma_all, choose],
        flops=2e9,
    )

    def edge_two(re_ref, ro_ref, psent_ref, sigs_ref, w_ref, qs_ref, e_ref, o_ref):
        table = far_faces(faces, arrived(re_ref, ro_ref, 2)[:1], w_ref)
        add = sigs_ref[...] * spread(qs_ref[...], table, 1)[0]
        put_sent(
            e_ref, o_ref, [psent_ref[t * sent : (t + 1) * sent, :] + add for t in range(slabs)]
        )

    e3, o3 = call(
        edge_two,
        [edge, edge],
        [re2, ro2, psent3, sig_sent, weights, q_sent],
        flops=1e7,
    )
    re3, ro3 = exchange(e3, o3)

    def third(
        re_ref, ro_ref, a_in, b_in, z_in, v_ref, w_ref, pick_ref, q_ref, sig_ref, out_ref
    ):
        sigma = sig_ref[...]
        add = spread(q_ref[...], far_faces(faces, arrived(re_ref, ro_ref, 2), w_ref), 2)
        a = a_in[...] + sigma * add[0]
        b = b_in[...] + sigma * add[0]
        z = z_in[...] + sigma * add[1]
        ca, cb = split(a), split(b)
        ga, gb = own_faces(faces, pick_ref, w_ref, [ca, cb])
        tz, ta = product(split(z), w_ref[W_TIME]), product(ca, w_ref[W_TIME])
        out_ref[:elements, :] = (
            a + v_ref[:elements, :] - DAMPING * product(ca, w_ref[W_DIAG]) + sigma * (tz + ga)
        )
        out_ref[elements:, :] = (
            b + v_ref[elements:, :] - DAMPING * product(cb, w_ref[W_DIAG]) + sigma * (ta + gb)
        )

    (part4,) = call(
        third,
        [two],
        [re2, ro2, a3, b3, z3, v0, weights, pick, q_all, sigma_all],
        flops=2e9,
    )

    def last(re_ref, ro_ref, p_ref, w_ref, q_ref, sig_ref, out_ref):
        add = spread(q_ref[...], far_faces(faces, arrived(re_ref, ro_ref, slabs), w_ref), slabs)
        for t in range(slabs):
            out_ref[t * elements : (t + 1) * elements, :] = (
                p_ref[t * elements : (t + 1) * elements, :] + sig_ref[...] * add[t]
            )

    (out,) = call(
        last, [two], [re3, ro3, part4, weights, q_all, sigma_all], flops=1e7
    )
    return out.reshape(slabs, elements, width)


def solution(mesh):
    in_specs = (
        P("tm", "space", None),
        P("space"),
        P(),
        P(),
        P(),
        P(),
        P("space", None),
        P("space", None),
    )
    out_specs = P("tm", "space", None)
    return jax.shard_map(body, mesh=mesh, in_specs=in_specs, out_specs=out_specs, check_vma=False)
```

time: 84.2 us -> 46.8 us (0.56)
  waiting for transfers between devices: 0.03 us -> 17 us
  local copies, waits for them, and re-layouts: 23.3 us -> 6.44 us
  starting transfers between devices: 28.9 us -> 12.6 us
  matrix products: 14 us -> 0 us
  Pallas kernels: 0 us -> 10.2 us
  blocking collectives: 10.1 us -> 0 us
  other arithmetic: 6.3 us -> 0 us
  between operations: 1.08 us -> 0.15 us
    gather x24 -> x0, local copies, waits for them, and re-layouts: 18.1 us -> none  [the longest x16 15.6 us: operate(): picked = jnp.take(extended, neighbours[:, face_index], axis=1)]
    ppermute x12 -> x13, waiting for transfers between devices: 0.03 us -> 17 us  [the longest x4 10.1 us: exchange(): lax.ppermute(to_o, 'space', swap_o)]
    ppermute x12 -> x13, starting transfers between devices: 28.9 us -> 12.6 us  [the longest x5 6.52 us: later(): lax.ppermute(x, 'tm', [(i, (i + by) % groups) for i in range(groups)])]
    dot_general x36 -> x0, matrix products: 14 us -> none  [product(): jnp.dot(left, right, precision=lax.Precision.HIGHEST, preferred_element_t...]
    pallas_call x0 -> x10, Pallas kernels: none -> 10.2 us  [call(): pl.pallas_call(kernel, out_shape=[jax.ShapeDtypeStruct(s, d) for s, d in...]
    all_gather x1 -> x0, blocking collectives: 10.1 us -> none  [body(): gathered_rhs = lax.all_gather(coarse_rhs, 'tm', axis=0, tiled=True)]
    select_n x21 -> x0, other arithmetic: 5.39 us -> none  [the longest x20 5.39 us: operate(): picked = jnp.take(extended, neighbours[:, face_index], axis=1)]
    unnamed x18 -> x16, local copies, waits for them, and re-layouts: 3.04 us -> 6.44 us
  transfers between devices with their start and end apart: 12 -> 13, of which waited for: 0 -> 5; matrix products, arithmetic and copies ran while one was open for 34% -> 0% of each run, Pallas kernels for 0% -> 15%
where the time goes in v1:
time: 46.8 us; the launch traced here: 46.5 us
  waiting for transfers between devices  17 us (36%)
  starting transfers between devices  12.6 us (27%)
  Pallas kernels  10.2 us (22%)
  local copies, waits for them, and re-layouts  6.44 us (14%)
    pallas_call x10, Pallas kernels, call(): pl.pallas_call(kernel, out_shape=[jax.ShapeDtypeStruct(s, d) for s, d in...  10.2 us
    ppermute x4, waiting for transfers between devices, exchange(): lax.ppermute(to_o, 'space', swap_o)  10.1 us
    ppermute x5, waiting for transfers between devices, later(): lax.ppermute(x, 'tm', [(i, (i + by) % groups) for i in range(groups)])  6.86 us
    ppermute x5, starting transfers between devices, later(): lax.ppermute(x, 'tm', [(i, (i + by) % groups) for i in range(groups)])  6.52 us
    unnamed x16, local copies, waits for them, and re-layouts  6.44 us
    ppermute x4, starting transfers between devices, exchange(): lax.ppermute(to_o, 'space', swap_o)  5.4 us
  transfers between devices with their start and end apart: 13, of which 5 were waited for; matrix products, arithmetic and copies ran while one was open for 0% of the time, Pallas kernels for 15%

profile of v1, /device:TPU:0, one launch (start us, length us, event | category | flops | bytes accessed | tf_op | source)
XLA Modules:
  0.0 46.5 jit_solution(1016950395557318316)
XLA Ops:
  0.0 0.0 copy-start
  0.0 0.9 %copy-done = f32[2,256,128]{2,1,0:T(8,128)S(1)} copy-done((f32[2,256,128]{2,1,0:T(8,128)S(1)}, f32[2,256,128]{2,1,0:T(8,128)}, u32[]{:S(2)}) %copy-start) | copy-done | bytes 262168
  1.0 0.0 copy-start.1
  1.0 0.8 %copy-done.1 = f32[128,128]{1,0:T(8,128)S(1)} copy-done((f32[128,128]{1,0:T(8,128)S(1)}, f32[128,128]{1,0:T(8,128)}, u32[]{:S(2)}) %copy-start.1) | copy-done | bytes 65560
  1.8 0.0 copy-start.2
  1.8 0.7 %copy-done.2 = f32[256]{0:T(256)S(1)} copy-done((f32[256]{0:T(256)S(1)}, f32[256]{0:T(256)}, u32[]{:S(2)}) %copy-start.2) | copy-done | bytes 1048
  2.5 0.0 copy-start.3
  2.5 0.7 %copy-done.3 = s32[1,32]{1,0:T(1,128)S(1)} copy-done((s32[1,32]{1,0:T(1,128)S(1)}, s32[1,32]{1,0:T(1,128)}, u32[]{:S(2)}) %copy-start.3) | copy-done | bytes 152
  3.1 0.8 %shard_map.82 = (f32[32,128]{1,0:T(8,128)S(1)}, f32[32,128]{1,0:T(8,128)S(1)}) custom-call(f32[512,128]{1,0:T(8,128)S(1)} %bitcast.6, f32[1,256]{1,0:T(1,128)S(1)} %bitcast.8, f32[128,128]{1,0:T(8,128)S(1)} %copy-done.1, s32[1,32]{1,0:T(1,128)S(1)} %copy-done.3), custom_call_target="tpu_custom_call" | custom-call | flops 10000000 | bytes 1048576 | tf_op jit(solution)/shard_map/pallas_call | solution.py:19
  4.0 0.6 %collective-permute-start = (f32[32,128]{1,0:T(8,128)S(1)}, f32[32,128]{1,0:T(8,128)S(1)}, u32[]{:S(2)}, u32[]{:S(2)}) collective-permute-start(f32[32,128]{1,0:T(8,128)S(1)} %get-tuple-element.38), channel_id=1, source_target_pairs={{0,1},{1,0},{2,3},{3,2},{4,5},{5,4},{6,7},{7,6},{8,9},{9,8},{10,11... | collective-permute-start | bytes 49160 | tf_op jit(solution)/shard_map/ppermute | solution.py:142
  4.5 4.7 %collective-permute-start.1 = (f32[32,128]{1,0:T(8,128)S(1)}, f32[32,128]{1,0:T(8,128)S(1)}, u32[]{:S(2)}, u32[]{:S(2)}) collective-permute-start(f32[32,128]{1,0:T(8,128)S(1)} %get-tuple-element.39), channel_id=1, source_target_pairs={{0,7},{1,2},{2,1},{3,4},{4,3},{5,6},{6,5},{7,0},{8,15},{9,10},{10,... | collective-permute-start | bytes 49160 | tf_op jit(solution)/shard_map/ppermute | solution.py:142
  9.3 1.5 %collective-permute-start.2 = (f32[256,128]{1,0:T(8,128)S(1)}, f32[256,128]{1,0:T(8,128)S(1)}, u32[]{:S(2)}, u32[]{:S(2)}) collective-permute-start(f32[256,128]{1,0:T(8,128)S(1)} %slice_bitcast_fusion), channel_id=1, source_target_pairs={{0,8},{8,16},{16,24},{24,0},{1,9},{9,17},{17,25},{25,1},{2,10},{10... | collective-permute-start | bytes 393224 | tf_op jit(solution)/shard_map/ppermute | solution.py:145
  10.8 0.0 copy-start.4
  10.8 0.9 %copy-done.4 = f32[4,128,128]{2,1,0:T(8,128)S(1)} copy-done((f32[4,128,128]{2,1,0:T(8,128)S(1)}, f32[4,128,128]{2,1,0:T(8,128)}, u32[]{:S(2)}) %copy-start.4) | copy-done | bytes 262168
  11.7 0.0 copy-start.5
  11.7 0.8 %copy-done.5 = f32[128,128]{1,0:T(8,128)S(1)} copy-done((f32[128,128]{1,0:T(8,128)S(1)}, f32[128,128]{1,0:T(8,128)}, u32[]{:S(2)}) %copy-start.5) | copy-done | bytes 65560
  12.6 0.0 copy-start.6
  12.6 0.8 %copy-done.6 = f32[128,128]{1,0:T(8,128)S(1)} copy-done((f32[128,128]{1,0:T(8,128)S(1)}, f32[128,128]{1,0:T(8,128)}, u32[]{:S(2)}) %copy-start.6) | copy-done | bytes 65560
  13.4 0.0 copy-start.7
  13.4 0.7 %copy-done.7 = s32[256,4]{0,1:T(4,128)S(1)} copy-done((s32[256,4]{0,1:T(4,128)S(1)}, s32[256,4]{0,1:T(4,128)}, u32[]{:S(2)}) %copy-start.7) | copy-done | bytes 4120
  14.1 2.4 %shard_map.83 = (f32[512,128]{1,0:T(8,128)S(1)}, f32[512,128]{1,0:T(8,128)S(1)}, f32[64,128]{1,0:T(8,128)S(1)}, f32[32,128]{1,0:T(8,128)S(1)}, bf16[9,256,256]{2...) custom-call(f32[512,128]{1,0:T(8,128)S(1)} %bitcast.7, ...), custom_call_target="tpu_custom_call" | custom-call | flops 2000000000 | bytes 1048576 | tf_op jit(solution)/shard_map/pallas_call | solution.py:19
  16.5 0.0 collective-permute-done.re_ref
  16.5 0.0 collective-permute-done.1.ro_ref
  16.5 0.0 collective-permute-done.2.b_ref
  16.5 0.5 %shard_map.84 = (f32[32,128]{1,0:T(8,128)S(1)}, f32[32,128]{1,0:T(8,128)S(1)}) custom-call(f32[32,128]{1,0:T(8,128)S(1)} %collective-permute-done.re_ref, f32[32,128]{1,0:T(8,128)S(1)} %collective-permute-done.1.ro_ref, f32[256,128]{1,0:T(8,128)S(1)} %collective-permute-done.2.b_ref, f32[64,128]{1,0:T(8,128)S(1)} %get-tuple-element.40.psent_ref, ...), custom_call_target="tpu_custom_call" | custom-call | flops 10000000 | bytes 1048576 | tf_op jit(solution)/shard_map/pallas_call | solution.py:19
  17.0 0.1 collective-permute-start.3
  17.1 0.6 %collective-permute-start.4 = (f32[32,128]{1,0:T(8,128)S(1)}, f32[32,128]{1,0:T(8,128)S(1)}, u32[]{:S(2)}, u32[]{:S(2)}) collective-permute-start(f32[32,128]{1,0:T(8,128)S(1)} %get-tuple-element.46), channel_id=1, source_target_pairs={{0,7},{1,2},{2,1},{3,4},{4,3},{5,6},{6,5},{7,0},{8,15},{9,10},{10,... | collective-permute-start | bytes 49160 | tf_op jit(solution)/shard_map/ppermute | solution.py:142
  17.6 1.5 %shard_map.85 = (f32[256,128]{1,0:T(8,128)S(1)}, f32[256,128]{1,0:T(8,128)S(1)}, f32[256,128]{1,0:T(8,128)S(1)}, f32[256,128]{1,0:T(8,128)S(1)}, f32[256,128]{1,0:T(8,128)S(1)}) custom-call(f32[32,128]{1,0:T(8,128)S(1)} %collective-permute-done.re_ref, f32[32,128]{1,0:T(8,128)S(1)} %collective-permute-done.1.ro_ref, ...), custom_call_target="tpu_custom_call" | custom-call | flops 2000000000 | bytes 1048576 | tf_op jit(solution)/shard_map/pallas_call | solution.py:19
  19.2 0.0 collective-permute-done.3.re_ref
  19.2 2.9 %collective-permute-done.4.ro_ref = f32[32,128]{1,0:T(8,128)S(1)} collective-permute-done((f32[32,128]{1,0:T(8,128)S(1)}, f32[32,128]{1,0:T(8,128)S(1)}, u32[]{:S(2)}, u32[]{:S(2)}) %collective-permute-start.4) | collective-permute-done | bytes 16416 | tf_op jit(solution)/shard_map/ppermute | solution.py:142
  22.1 0.4 shard_map.86
  22.5 1.5 %collective-permute-start.7 = (f32[256,128]{1,0:T(8,128)S(1)}, f32[256,128]{1,0:T(8,128)S(1)}, u32[]{:S(2)}, u32[]{:S(2)}) collective-permute-start(f32[256,128]{1,0:T(8,128)S(1)} %get-tuple-element.56.refs_3_), channel_id=1, source_target_pairs={{0,24},{8,0},{16,8},{24,16},{1,25},{9,1},{17,9},{25,17},{2,26},{10... | collective-permute-start | bytes 393224 | tf_op jit(solution)/shard_map/ppermute | solution.py:145
  24.0 1.5 %collective-permute-start.6 = (f32[256,128]{1,0:T(8,128)S(1)}, f32[256,128]{1,0:T(8,128)S(1)}, u32[]{:S(2)}, u32[]{:S(2)}) collective-permute-start(f32[256,128]{1,0:T(8,128)S(1)} %get-tuple-element.56.refs_3_), channel_id=1, source_target_pairs={{0,16},{8,24},{16,0},{24,8},{1,17},{9,25},{17,1},{25,9},{2,18},{10... | collective-permute-start | bytes 393224 | tf_op jit(solution)/shard_map/ppermute | solution.py:145
  25.5 0.6 %collective-permute-start.5 = (f32[256,128]{1,0:T(8,128)S(1)}, f32[256,128]{1,0:T(8,128)S(1)}, u32[]{:S(2)}, u32[]{:S(2)}) collective-permute-start(f32[256,128]{1,0:T(8,128)S(1)} %get-tuple-element.56.refs_3_), channel_id=1, source_target_pairs={{0,8},{8,16},{16,24},{24,0},{1,9},{9,17},{17,25},{25,1},{2,10},{10... | collective-permute-start | bytes 393224 | tf_op jit(solution)/shard_map/ppermute | solution.py:145
  26.1 1.4 %collective-permute-start.10 = (f32[256,128]{1,0:T(8,128)S(1)}, f32[256,128]{1,0:T(8,128)S(1)}, u32[]{:S(2)}, u32[]{:S(2)}) collective-permute-start(f32[256,128]{1,0:T(8,128)S(1)} %get-tuple-element.62), channel_id=1, source_target_pairs={{0,8},{8,16},{16,24},{24,0},{1,9},{9,17},{17,25},{25,1},{2,10},{10... | collective-permute-start | bytes 393224 | tf_op jit(solution)/shard_map/ppermute | solution.py:145
  27.5 1.4 %collective-permute-done.7.refs_2_ = f32[256,128]{1,0:T(8,128)S(1)} collective-permute-done((f32[256,128]{1,0:T(8,128)S(1)}, f32[256,128]{1,0:T(8,128)S(1)}, u32[]{:S(2)}, u32[]{:S(2)}) %collective-permute-start.7) | collective-permute-done | bytes 131104 | tf_op jit(solution)/shard_map/ppermute | solution.py:145
  29.0 5.4 %collective-permute-done.6.refs_1_ = f32[256,128]{1,0:T(8,128)S(1)} collective-permute-done((f32[256,128]{1,0:T(8,128)S(1)}, f32[256,128]{1,0:T(8,128)S(1)}, u32[]{:S(2)}, u32[]{:S(2)}) %collective-permute-start.6) | collective-permute-done | bytes 131104 | tf_op jit(solution)/shard_map/ppermute | solution.py:145
  34.4 0.0 collective-permute-done.5.refs_0_
  34.4 0.5 %shard_map.87 = (f32[256,128]{1,0:T(8,128)S(1)}, f32[256,128]{1,0:T(8,128)S(1)}, f32[32,128]{1,0:T(8,128)S(1)}, f32[32,128]{1,0:T(8,128)S(1)}) custom-call(f32[256,128]{1,0:T(8,128)S(1)} %collective-permute-done.5.refs_0_, f32[256,128]{1,0:T(8,128)S(1)} %collective-permute-done.6.refs_1_, f32[256,128]{1,0:T(8,128)S(1)} %collective-permute-done.7.refs_2_, ...), custom_call_target="tpu_custom_call" | custom-call | flops 100000000 | bytes 1048576 | tf_op jit(solution)/shard_map/pallas_call | solution.py:19
  34.9 0.1 collective-permute-start.8
  35.0 0.1 collective-permute-start.9
  35.0 0.0 collective-permute-done.10.xb_ref
  35.1 1.2 %shard_map.88 = (f32[256,128]{1,0:T(8,128)S(1)}, f32[256,128]{1,0:T(8,128)S(1)}, f32[256,128]{1,0:T(8,128)S(1)}, f32[64,128]{1,0:T(8,128)S(1)}) custom-call(f32[256,128]{1,0:T(8,128)S(1)} %get-tuple-element.60.c_in, f32[256,128]{1,0:T(8,128)S(1)} %get-tuple-element.61.d_in, f32[256,128]{1,0:T(8,128)S(1)} %collective-permute-done.10.xb_ref, ...), custom_call_target="tpu_custom_call" | custom-call | flops 2000000000 | bytes 1048576 | tf_op jit(solution)/shard_map/pallas_call | solution.py:19
  36.3 0.0 collective-permute-done.8.re_ref
  36.3 3.7 %collective-permute-done.9.ro_ref = f32[32,128]{1,0:T(8,128)S(1)} collective-permute-done((f32[32,128]{1,0:T(8,128)S(1)}, f32[32,128]{1,0:T(8,128)S(1)}, u32[]{:S(2)}, u32[]{:S(2)}) %collective-permute-start.9) | collective-permute-done | bytes 16416 | tf_op jit(solution)/shard_map/ppermute | solution.py:142
  40.0 0.3 shard_map.89
  40.3 0.0 collective-permute-start.11
  40.3 0.1 collective-permute-start.12
  40.4 1.5 %shard_map.90.p_ref = f32[512,128]{1,0:T(8,128)S(1)} custom-call(f32[32,128]{1,0:T(8,128)S(1)} %collective-permute-done.8.re_ref, f32[32,128]{1,0:T(8,128)S(1)} %collective-permute-done.9.ro_ref, f32[256,128]{1,0:T(8,128)S(1)} %get-tuple-element.68.a_in, f32[256,128]{1,0:T(8,128)S(1)} %get-tuple-element.69.b_in, f32[256,128]{1,0:T(8,128)S(1)} %get-tuple-element.70.z_in, ...), custom_call_target="tpu_custom_call" | custom-call | flops 2000000000 | bytes 1048576 | tf_op jit(solution)/shard_map/pallas_call | solution.py:19
  41.9 0.0 collective-permute-done.11.re_ref
  41.9 3.5 %collective-permute-done.12.ro_ref = f32[32,128]{1,0:T(8,128)S(1)} collective-permute-done((f32[32,128]{1,0:T(8,128)S(1)}, f32[32,128]{1,0:T(8,128)S(1)}, u32[]{:S(2)}, u32[]{:S(2)}) %collective-permute-start.12) | collective-permute-done | bytes 16416 | tf_op jit(solution)/shard_map/ppermute | solution.py:142
  45.3 1.1 %shard_map.91 = f32[512,128]{1,0:T(8,128)} custom-call(f32[32,128]{1,0:T(8,128)S(1)} %collective-permute-done.11.re_ref, f32[32,128]{1,0:T(8,128)S(1)} %collective-permute-done.12.ro_ref, f32[512,128]{1,0:T(8,128)S(1)} %shard_map.90.p_ref, bf16[9,256,256]{2,1,0:T(8,128)(2,1)S(1)} %get-tuple-element.42.w_ref.refs_5_, ...), custom_call_target="tpu_custom_call" | custom-call | flops 10000000 | bytes 1048576 | tf_op jit(solution)/shard_map/pallas_call | solution.py:19
  (1 shorter events, 0.0 us)
Async XLA Ops:
  0.0 0.9 %copy-start = (f32[2,256,128]{2,1,0:T(8,128)S(1)}, f32[2,256,128]{2,1,0:T(8,128)}, u32[]{:S(2)}) copy-start(f32[2,256,128]{2,1,0:T(8,128)} %param.8) | copy-start | bytes 786436
  1.0 0.8 %copy-start.1 = (f32[128,128]{1,0:T(8,128)S(1)}, f32[128,128]{1,0:T(8,128)}, u32[]{:S(2)}) copy-start(f32[128,128]{1,0:T(8,128)} %inv_ref.3) | copy-start | bytes 196612
  1.8 0.7 %copy-start.2 = (f32[256]{0:T(256)S(1)}, f32[256]{0:T(256)}, u32[]{:S(2)}) copy-start(f32[256]{0:T(256)} %param.9) | copy-start | bytes 3076
  2.5 0.7 %copy-start.3 = (s32[1,32]{1,0:T(1,128)S(1)}, s32[1,32]{1,0:T(1,128)}, u32[]{:S(2)}) copy-start(s32[1,32]{1,0:T(1,128)} %send_ref.3) | copy-start | bytes 388
  4.0 12.5 %collective-permute-start = (f32[32,128]{1,0:T(8,128)S(1)}, f32[32,128]{1,0:T(8,128)S(1)}, u32[]{:S(2)}, u32[]{:S(2)}) collective-permute-start(f32[32,128]{1,0:T(8,128)S(1)} %get-tuple-element.38), channel_id=1, source_target_pairs={{0,1},{1,0},{2,3},{3,2},{4,5},{5,4},{6,7},{7,6},{8,9},{9,8},{10,11... | collective-permute-start | bytes 49160 | tf_op jit(solution)/shard_map/ppermute | solution.py:142
  4.5 12.0 %collective-permute-start.1 = (f32[32,128]{1,0:T(8,128)S(1)}, f32[32,128]{1,0:T(8,128)S(1)}, u32[]{:S(2)}, u32[]{:S(2)}) collective-permute-start(f32[32,128]{1,0:T(8,128)S(1)} %get-tuple-element.39), channel_id=1, source_target_pairs={{0,7},{1,2},{2,1},{3,4},{4,3},{5,6},{6,5},{7,0},{8,15},{9,10},{10,... | collective-permute-start | bytes 49160 | tf_op jit(solution)/shard_map/ppermute | solution.py:142
  9.3 7.3 %collective-permute-start.2 = (f32[256,128]{1,0:T(8,128)S(1)}, f32[256,128]{1,0:T(8,128)S(1)}, u32[]{:S(2)}, u32[]{:S(2)}) collective-permute-start(f32[256,128]{1,0:T(8,128)S(1)} %slice_bitcast_fusion), channel_id=1, source_target_pairs={{0,8},{8,16},{16,24},{24,0},{1,9},{9,17},{17,25},{25,1},{2,10},{10... | collective-permute-start | bytes 393224 | tf_op jit(solution)/shard_map/ppermute | solution.py:145
  10.8 0.9 %copy-start.4 = (f32[4,128,128]{2,1,0:T(8,128)S(1)}, f32[4,128,128]{2,1,0:T(8,128)}, u32[]{:S(2)}) copy-start(f32[4,128,128]{2,1,0:T(8,128)} %f_ref.1) | copy-start | bytes 786436
  11.7 0.8 %copy-start.5 = (f32[128,128]{1,0:T(8,128)S(1)}, f32[128,128]{1,0:T(8,128)}, u32[]{:S(2)}) copy-start(f32[128,128]{1,0:T(8,128)} %d_ref.1) | copy-start | bytes 196612
  12.6 0.8 %copy-start.6 = (f32[128,128]{1,0:T(8,128)S(1)}, f32[128,128]{1,0:T(8,128)}, u32[]{:S(2)}) copy-start(f32[128,128]{1,0:T(8,128)} %t_ref.1) | copy-start | bytes 196612
  13.4 0.7 %copy-start.7 = (s32[256,4]{0,1:T(4,128)S(1)}, s32[256,4]{0,1:T(4,128)}, u32[]{:S(2)}) copy-start(s32[256,4]{0,1:T(4,128)} %param.14) | copy-start | bytes 12292
  17.0 2.2 %collective-permute-start.3 = (f32[32,128]{1,0:T(8,128)S(1)}, f32[32,128]{1,0:T(8,128)S(1)}, u32[]{:S(2)}, u32[]{:S(2)}) collective-permute-start(f32[32,128]{1,0:T(8,128)S(1)} %get-tuple-element.45), channel_id=1, source_target_pairs={{0,1},{1,0},{2,3},{3,2},{4,5},{5,4},{6,7},{7,6},{8,9},{9,8},{10,11... | collective-permute-start | bytes 49160 | tf_op jit(solution)/shard_map/ppermute | solution.py:142
  17.1 5.0 %collective-permute-start.4 = (f32[32,128]{1,0:T(8,128)S(1)}, f32[32,128]{1,0:T(8,128)S(1)}, u32[]{:S(2)}, u32[]{:S(2)}) collective-permute-start(f32[32,128]{1,0:T(8,128)S(1)} %get-tuple-element.46), channel_id=1, source_target_pairs={{0,7},{1,2},{2,1},{3,4},{4,3},{5,6},{6,5},{7,0},{8,15},{9,10},{10,... | collective-permute-start | bytes 49160 | tf_op jit(solution)/shard_map/ppermute | solution.py:142
  22.5 6.4 %collective-permute-start.7 = (f32[256,128]{1,0:T(8,128)S(1)}, f32[256,128]{1,0:T(8,128)S(1)}, u32[]{:S(2)}, u32[]{:S(2)}) collective-permute-start(f32[256,128]{1,0:T(8,128)S(1)} %get-tuple-element.56.refs_3_), channel_id=1, source_target_pairs={{0,24},{8,0},{16,8},{24,16},{1,25},{9,1},{17,9},{25,17},{2,26},{10... | collective-permute-start | bytes 393224 | tf_op jit(solution)/shard_map/ppermute | solution.py:145
  24.0 10.3 %collective-permute-start.6 = (f32[256,128]{1,0:T(8,128)S(1)}, f32[256,128]{1,0:T(8,128)S(1)}, u32[]{:S(2)}, u32[]{:S(2)}) collective-permute-start(f32[256,128]{1,0:T(8,128)S(1)} %get-tuple-element.56.refs_3_), channel_id=1, source_target_pairs={{0,16},{8,24},{16,0},{24,8},{1,17},{9,25},{17,1},{25,9},{2,18},{10... | collective-permute-start | bytes 393224 | tf_op jit(solution)/shard_map/ppermute | solution.py:145
  25.5 8.8 %collective-permute-start.5 = (f32[256,128]{1,0:T(8,128)S(1)}, f32[256,128]{1,0:T(8,128)S(1)}, u32[]{:S(2)}, u32[]{:S(2)}) collective-permute-start(f32[256,128]{1,0:T(8,128)S(1)} %get-tuple-element.56.refs_3_), channel_id=1, source_target_pairs={{0,8},{8,16},{16,24},{24,0},{1,9},{9,17},{17,25},{25,1},{2,10},{10... | collective-permute-start | bytes 393224 | tf_op jit(solution)/shard_map/ppermute | solution.py:145
  26.1 8.9 %collective-permute-start.10 = (f32[256,128]{1,0:T(8,128)S(1)}, f32[256,128]{1,0:T(8,128)S(1)}, u32[]{:S(2)}, u32[]{:S(2)}) collective-permute-start(f32[256,128]{1,0:T(8,128)S(1)} %get-tuple-element.62), channel_id=1, source_target_pairs={{0,8},{8,16},{16,24},{24,0},{1,9},{9,17},{17,25},{25,1},{2,10},{10... | collective-permute-start | bytes 393224 | tf_op jit(solution)/shard_map/ppermute | solution.py:145
  34.9 1.4 %collective-permute-start.8 = (f32[32,128]{1,0:T(8,128)S(1)}, f32[32,128]{1,0:T(8,128)S(1)}, u32[]{:S(2)}, u32[]{:S(2)}) collective-permute-start(f32[32,128]{1,0:T(8,128)S(1)} %get-tuple-element.58), channel_id=1, source_target_pairs={{0,1},{1,0},{2,3},{3,2},{4,5},{5,4},{6,7},{7,6},{8,9},{9,8},{10,11... | collective-permute-start | bytes 49160 | tf_op jit(solution)/shard_map/ppermute | solution.py:142
  35.0 5.0 %collective-permute-start.9 = (f32[32,128]{1,0:T(8,128)S(1)}, f32[32,128]{1,0:T(8,128)S(1)}, u32[]{:S(2)}, u32[]{:S(2)}) collective-permute-start(f32[32,128]{1,0:T(8,128)S(1)} %get-tuple-element.59), channel_id=1, source_target_pairs={{0,7},{1,2},{2,1},{3,4},{4,3},{5,6},{6,5},{7,0},{8,15},{9,10},{10,... | collective-permute-start | bytes 49160 | tf_op jit(solution)/shard_map/ppermute | solution.py:142
  40.3 1.6 %collective-permute-start.11 = (f32[32,128]{1,0:T(8,128)S(1)}, f32[32,128]{1,0:T(8,128)S(1)}, u32[]{:S(2)}, u32[]{:S(2)}) collective-permute-start(f32[32,128]{1,0:T(8,128)S(1)} %get-tuple-element.66), channel_id=1, source_target_pairs={{0,1},{1,0},{2,3},{3,2},{4,5},{5,4},{6,7},{7,6},{8,9},{9,8},{10,11... | collective-permute-start | bytes 49160 | tf_op jit(solution)/shard_map/ppermute | solution.py:142
  40.3 5.0 %collective-permute-start.12 = (f32[32,128]{1,0:T(8,128)S(1)}, f32[32,128]{1,0:T(8,128)S(1)}, u32[]{:S(2)}, u32[]{:S(2)}) collective-permute-start(f32[32,128]{1,0:T(8,128)S(1)} %get-tuple-element.67), channel_id=1, source_target_pairs={{0,7},{1,2},{2,1},{3,4},{4,3},{5,6},{6,5},{7,0},{8,15},{9,10},{10,... | collective-permute-start | bytes 49160 | tf_op jit(solution)/shard_map/ppermute | solution.py:142

commit v2 on v1

--- a/solution.py
+++ b/solution.py
@@ -10,12 +10,16 @@
 BF16 = jnp.bfloat16
 VMEM = pltpu.VMEM
 SMEM = pltpu.SMEM
+HBM = pltpu.MemorySpace.HBM
 
 W_DIAG, W_FACE, W_SOURCE_TIME, W_TIME = 0, 1, 5, 6
 
 
 def call(kernel, out_shapes, args, spaces=None, scratch=(), flops=4e8):
     spaces = spaces or [VMEM] * len(args)
+    args = [
+        pltpu.with_memory_space_constraint(x, HBM) if s is HBM else x for x, s in zip(args, spaces)
+    ]
     return pl.pallas_call(
         kernel,
         out_shape=[jax.ShapeDtypeStruct(s, d) for s, d in out_shapes],
@@ -25,6 +29,13 @@
         compiler_params=pltpu.CompilerParams(vmem_limit_bytes=24 << 20),
         cost_estimate=pl.CostEstimate(flops=int(flops), bytes_accessed=1 << 20, transcendentals=0),
     )(*args)
+
+
+def fetch(pairs, sems):
+    copies = [pltpu.make_async_copy(a, b, sems.at[i]) for i, (a, b) in enumerate(pairs)]
+    for c in copies:
+        c.start()
+    return copies
 
 
 def split(x):
@@ -148,39 +159,64 @@
         first = jnp.where(lax.axis_index("space") % 2 == 0, halo, 0)
         return send_ref[0, lax.rem(first + i, sent)]
 
-    def first_kernel(s_ref, scale_ref, inv_ref, send_ref, e_ref, o_ref, x_ref, g_ref):
+    def first_kernel(
+        s_hbm, scale_hbm, inv_hbm, send_hbm, e_ref, o_ref, xa_ref, xb_ref,
+        s_ref, scale_ref, inv_ref, send_ref, g_ref, sems,
+    ):
+        copies = fetch(
+            [(scale_hbm, scale_ref), (send_hbm, send_ref), (s_hbm, s_ref), (inv_hbm, inv_ref)],
+            sems,
+        )
+        copies[0].wait()
         sigma = DAMPING / column(scale_ref[...], width)
+        copies[1].wait()
+        copies[2].wait()
+        refs = [xa_ref, xb_ref]
         for t in range(slabs):
-            x_ref[t * elements : (t + 1) * elements, :] = (
-                s_ref[t * elements : (t + 1) * elements, :] * sigma
-            )
+            refs[t][...] = s_ref[t * elements : (t + 1) * elements, :] * sigma
         for i in range(sent):
             at = sent_at(send_ref, i)
             base = (i // halo) * slabs * halo + i % halo
             for t in range(slabs):
-                g_ref[base + t * halo : base + t * halo + 1, :] = x_ref[
-                    pl.ds(t * elements + at, 1), :
-                ]
+                g_ref[base + t * halo : base + t * halo + 1, :] = refs[t][pl.ds(at, 1), :]
+        copies[3].wait()
         out = dot32(g_ref[...], inv_ref[...])
         e_ref[...] = out[: slabs * halo]
         o_ref[...] = out[slabs * halo :]
 
-    e0, o0 = call(
+    e0, o0, xa, xb = call(
         first_kernel,
-        [edge, edge],
+        [edge, edge, full, full],
         [flat, scale_row, block_inverse, send_rows],
-        spaces=[VMEM, VMEM, VMEM, SMEM],
-        scratch=[VMEM((slabs * elements, width), F32), VMEM((slabs * sent, width), F32)],
+        spaces=[HBM] * 4,
+        scratch=[
+            VMEM((slabs * elements, width), F32),
+            VMEM((1, elements), F32),
+            VMEM((width, width), F32),
+            SMEM((1, sent), jnp.int32),
+            VMEM((slabs * sent, width), F32),
+            pltpu.SemaphoreType.DMA((4,)),
+        ],
         flops=1e7,
     )
-    before = later(source[-1], 1)
+    before = later(xb, 1)
     re0, ro0 = exchange(e0, o0)
 
     def setup_kernel(
-        s_ref, scale_ref, d_ref, inv_ref, f_ref, t_ref, nbr_ref, send_ref,
+        xa_ref, xb_ref, scale_hbm, d_hbm, inv_hbm, f_hbm, t_hbm, nbr_hbm, send_hbm,
         v_ref, part_ref, psent_ref, sigs_ref, w_ref, pick_ref, q_ref, qs_ref, sent_ref,
-        sig_ref, frac_ref, rows_ref,
-    ):
+        sig_ref, frac_ref,
+        scale_ref, d_ref, inv_ref, f_ref, t_ref, nbr_ref, send_ref, rows_ref, sems,
+    ):
+        copies = fetch(
+            [
+                (inv_hbm, inv_ref), (t_hbm, t_ref), (d_hbm, d_ref), (f_hbm, f_ref),
+                (scale_hbm, scale_ref), (nbr_hbm, nbr_ref), (send_hbm, send_ref),
+            ],
+            sems,
+        )
+        for c in copies:
+            c.wait()
         inv = inv_ref[...]
         trace = dot32(t_ref[...], inv)
         w_ref[W_DIAG] = weight_tile(dot32(d_ref[...], inv))
@@ -214,10 +250,7 @@
         sent_ref[...] = chosen
         qs_ref[...] = dot(chosen, q).astype(BF16)
         head = weight_tile(inv)
-        v = [
-            sigma * product(split(s_ref[t * elements : (t + 1) * elements, :]), head)
-            for t in range(slabs)
-        ]
+        v = [product(split(x[...]), head) for x in (xa_ref, xb_ref)]
         cut = [split(x) for x in v]
         near = own_faces(faces, pick_ref, w_ref, cut)
         parts = []
@@ -245,11 +278,21 @@
             ((elements, far), BF16), ((sent, far), BF16), ((sent, elements), BF16), full, full,
         ],
         [
-            flat, scale_row, diag_block, block_inverse, face_flux, time_trace, faces_row,
+            xa, xb, scale_row, diag_block, block_inverse, face_flux, time_trace, faces_row,
             send_rows,
         ],
-        spaces=[VMEM] * 7 + [SMEM],
-        scratch=[VMEM((sent, elements), F32)],
+        spaces=[VMEM] * 2 + [HBM] * 7,
+        scratch=[
+            VMEM((1, elements), F32),
+            VMEM((width, width), F32),
+            VMEM((width, width), F32),
+            VMEM((faces, width, width), F32),
+            VMEM((width, width), F32),
+            VMEM((faces, elements), jnp.int32),
+            SMEM((1, sent), jnp.int32),
+            VMEM((sent, elements), F32),
+            pltpu.SemaphoreType.DMA((7,)),
+        ],
         flops=2e9,
     )
 
@@ -265,7 +308,7 @@
         old = time_mask(product(picked, w_ref[W_SOURCE_TIME]))
         sig = sigs_ref[...]
         new = [psent_ref[t * sent : (t + 1) * sent, :] + sig * add[t] for t in range(slabs)]
-        new[0] = new[0] + sig * sig * old
+        new[0] = new[0] + sig * old
         put_sent(e_ref, o_ref, new)
 
     e1, o1 = call(
@@ -284,7 +327,7 @@
         frac = frac_ref[...]
         add = spread(q_ref[...], far_faces(faces, arrived(re_ref, ro_ref, slabs), w_ref), slabs)
         old = time_mask(product(split(b_ref[...]), w_ref[W_SOURCE_TIME]))
-        va = part_ref[:elements, :] + sigma * add[0] + sigma * sigma * old
+        va = part_ref[:elements, :] + sigma * add[0] + sigma * old
         vb = part_ref[elements:, :] + sigma * add[1]
         v0a, v0b = v_ref[:elements, :], v_ref[elements:, :]
         v1_ref[...] = vb

time: 46.8 us -> 41.6 us (0.89)
  local copies, waits for them, and re-layouts: 6.44 us -> 0 us
  starting transfers between devices: 12.6 us -> 15.2 us
  waiting for transfers between devices: 17 us -> 15 us
  Pallas kernels: 10.2 us -> 11.2 us
    unnamed x16 -> x0, local copies, waits for them, and re-layouts: 6.44 us -> none
    ppermute x4, starting transfers between devices: 5.4 us -> 7.88 us  [exchange(): lax.ppermute(to_o, 'space', swap_o)]
    ppermute x4, waiting for transfers between devices: 10.1 us -> 7.71 us  [exchange(): lax.ppermute(to_o, 'space', swap_o)]
    pallas_call x10, Pallas kernels: 10.2 us -> 11.2 us  [call(): pl.pallas_call(kernel, out_shape=[jax.ShapeDtypeStruct(s, d) for s, d in...]
  transfers between devices with their start and end apart: 13 -> 13, of which waited for: 5 -> 6; matrix products, arithmetic and copies ran while one was open for 0% -> 0% of each run, Pallas kernels for 15% -> 18%
where the time goes in v2:
time: 41.6 us; the launch traced here: 41.5 us
  starting transfers between devices  15.2 us (37%)
  waiting for transfers between devices  15 us (36%)
  Pallas kernels  11.2 us (27%)
    pallas_call x10, Pallas kernels, call(): pl.pallas_call(kernel, out_shape=[jax.ShapeDtypeStruct(s, d) for s, d in...  11.2 us
    ppermute x4, starting transfers between devices, exchange(): lax.ppermute(to_o, 'space', swap_o)  7.88 us
    ppermute x4, waiting for transfers between devices, exchange(): lax.ppermute(to_o, 'space', swap_o)  7.71 us
    ppermute x5, waiting for transfers between devices, later(): lax.ppermute(x, 'tm', [(i, (i + by) % groups) for i in range(groups)])  7.27 us
    ppermute x5, starting transfers between devices, later(): lax.ppermute(x, 'tm', [(i, (i + by) % groups) for i in range(groups)])  6.58 us
  transfers between devices with their start and end apart: 13, of which 6 were waited for; matrix products, arithmetic and copies ran while one was open for 0% of the time, Pallas kernels for 18%

profile of v2, /device:TPU:0, one launch (start us, length us, event | category | flops | bytes accessed | tf_op | source)
XLA Modules:
  0.0 41.5 jit_solution(3849304374264238095)
XLA Ops:
  0.0 1.3 %shard_map.82 = (f32[32,128]{1,0:T(8,128)S(1)}, f32[32,128]{1,0:T(8,128)S(1)}, f32[256,128]{1,0:T(8,128)S(1)}, f32[256,128]{1,0:T(8,128)S(1)}) custom-call(f32[512,128]{1,0:T(8,128)} %bitcast.4, f32[1,256]{1,0:T(1,128)} %bitcast.5, f32[128,128]{1,0:T(8,128)} %inv_hbm.3, s32[1,32]{1,0:T(1,128)} %send_hbm.3), custom_call_target="tpu_custom_call" | custom-call | flops 10000000 | bytes 1048576 | tf_op jit(solution)/shard_map/pallas_call | solution.py:23
  1.3 0.6 %collective-permute-start = (f32[32,128]{1,0:T(8,128)S(1)}, f32[32,128]{1,0:T(8,128)S(1)}, u32[]{:S(2)}, u32[]{:S(2)}) collective-permute-start(f32[32,128]{1,0:T(8,128)S(1)} %get-tuple-element.40), channel_id=1, source_target_pairs={{0,1},{1,0},{2,3},{3,2},{4,5},{5,4},{6,7},{7,6},{8,9},{9,8},{10,11... | collective-permute-start | bytes 49160 | tf_op jit(solution)/shard_map/ppermute | solution.py:153
  1.8 4.7 %collective-permute-start.1 = (f32[32,128]{1,0:T(8,128)S(1)}, f32[32,128]{1,0:T(8,128)S(1)}, u32[]{:S(2)}, u32[]{:S(2)}) collective-permute-start(f32[32,128]{1,0:T(8,128)S(1)} %get-tuple-element.41), channel_id=1, source_target_pairs={{0,7},{1,2},{2,1},{3,4},{4,3},{5,6},{6,5},{7,0},{8,15},{9,10},{10,... | collective-permute-start | bytes 49160 | tf_op jit(solution)/shard_map/ppermute | solution.py:153
  6.5 1.5 %collective-permute-start.2 = (f32[256,128]{1,0:T(8,128)S(1)}, f32[256,128]{1,0:T(8,128)S(1)}, u32[]{:S(2)}, u32[]{:S(2)}) collective-permute-start(f32[256,128]{1,0:T(8,128)S(1)} %get-tuple-element.42.xb_ref), channel_id=1, source_target_pairs={{0,8},{8,16},{16,24},{24,0},{1,9},{9,17},{17,25},{25,1},{2,10},{10... | collective-permute-start | bytes 393224 | tf_op jit(solution)/shard_map/ppermute | solution.py:156
  8.0 3.0 %shard_map.83 = (f32[512,128]{1,0:T(8,128)S(1)}, f32[512,128]{1,0:T(8,128)S(1)}, f32[64,128]{1,0:T(8,128)S(1)}, f32[32,128]{1,0:T(8,128)S(1)}, bf16[9,256,256]{2...) custom-call(f32[256,128]{1,0:T(8,128)S(1)} %get-tuple-element.43.xa_, ...), custom_call_target="tpu_custom_call" | custom-call | flops 2000000000 | bytes 1048576 | tf_op jit(solution)/shard_map/pallas_call | solution.py:23
  11.0 0.0 collective-permute-done.re_ref
  11.0 0.0 collective-permute-done.1.ro_ref
  11.0 1.4 %collective-permute-done.2.b_ref = f32[256,128]{1,0:T(8,128)S(1)} collective-permute-done((f32[256,128]{1,0:T(8,128)S(1)}, f32[256,128]{1,0:T(8,128)S(1)}, u32[]{:S(2)}, u32[]{:S(2)}) %collective-permute-start.2) | collective-permute-done | bytes 131104 | tf_op jit(solution)/shard_map/ppermute | solution.py:156
  12.4 0.5 %shard_map.84 = (f32[32,128]{1,0:T(8,128)S(1)}, f32[32,128]{1,0:T(8,128)S(1)}) custom-call(f32[32,128]{1,0:T(8,128)S(1)} %collective-permute-done.re_ref, f32[32,128]{1,0:T(8,128)S(1)} %collective-permute-done.1.ro_ref, f32[256,128]{1,0:T(8,128)S(1)} %collective-permute-done.2.b_ref, f32[64,128]{1,0:T(8,128)S(1)} %get-tuple-element.44.psent_ref, ...), custom_call_target="tpu_custom_call" | custom-call | flops 10000000 | bytes 1048576 | tf_op jit(solution)/shard_map/pallas_call | solution.py:23
  12.9 0.1 collective-permute-start.3
  13.0 0.9 %collective-permute-start.4 = (f32[32,128]{1,0:T(8,128)S(1)}, f32[32,128]{1,0:T(8,128)S(1)}, u32[]{:S(2)}, u32[]{:S(2)}) collective-permute-start(f32[32,128]{1,0:T(8,128)S(1)} %get-tuple-element.50), channel_id=1, source_target_pairs={{0,7},{1,2},{2,1},{3,4},{4,3},{5,6},{6,5},{7,0},{8,15},{9,10},{10,... | collective-permute-start | bytes 49160 | tf_op jit(solution)/shard_map/ppermute | solution.py:153
  13.9 1.5 %shard_map.85 = (f32[256,128]{1,0:T(8,128)S(1)}, f32[256,128]{1,0:T(8,128)S(1)}, f32[256,128]{1,0:T(8,128)S(1)}, f32[256,128]{1,0:T(8,128)S(1)}, f32[256,128]{1,0:T(8,128)S(1)}) custom-call(f32[32,128]{1,0:T(8,128)S(1)} %collective-permute-done.re_ref, f32[32,128]{1,0:T(8,128)S(1)} %collective-permute-done.1.ro_ref, ...), custom_call_target="tpu_custom_call" | custom-call | flops 2000000000 | bytes 1048576 | tf_op jit(solution)/shard_map/pallas_call | solution.py:23
  15.4 0.0 collective-permute-done.3.re_ref
  15.4 2.6 %collective-permute-done.4.ro_ref = f32[32,128]{1,0:T(8,128)S(1)} collective-permute-done((f32[32,128]{1,0:T(8,128)S(1)}, f32[32,128]{1,0:T(8,128)S(1)}, u32[]{:S(2)}, u32[]{:S(2)}) %collective-permute-start.4) | collective-permute-done | bytes 16416 | tf_op jit(solution)/shard_map/ppermute | solution.py:153
  18.0 0.4 shard_map.86
  18.4 1.6 %collective-permute-start.7 = (f32[256,128]{1,0:T(8,128)S(1)}, f32[256,128]{1,0:T(8,128)S(1)}, u32[]{:S(2)}, u32[]{:S(2)}) collective-permute-start(f32[256,128]{1,0:T(8,128)S(1)} %get-tuple-element.60.refs_3_), channel_id=1, source_target_pairs={{0,24},{8,0},{16,8},{24,16},{1,25},{9,1},{17,9},{25,17},{2,26},{10... | collective-permute-start | bytes 393224 | tf_op jit(solution)/shard_map/ppermute | solution.py:156
  20.0 0.5 %collective-permute-start.6 = (f32[256,128]{1,0:T(8,128)S(1)}, f32[256,128]{1,0:T(8,128)S(1)}, u32[]{:S(2)}, u32[]{:S(2)}) collective-permute-start(f32[256,128]{1,0:T(8,128)S(1)} %get-tuple-element.60.refs_3_), channel_id=1, source_target_pairs={{0,16},{8,24},{16,0},{24,8},{1,17},{9,25},{17,1},{25,9},{2,18},{10... | collective-permute-start | bytes 393224 | tf_op jit(solution)/shard_map/ppermute | solution.py:156
  20.5 1.5 %collective-permute-start.5 = (f32[256,128]{1,0:T(8,128)S(1)}, f32[256,128]{1,0:T(8,128)S(1)}, u32[]{:S(2)}, u32[]{:S(2)}) collective-permute-start(f32[256,128]{1,0:T(8,128)S(1)} %get-tuple-element.60.refs_3_), channel_id=1, source_target_pairs={{0,8},{8,16},{16,24},{24,0},{1,9},{9,17},{17,25},{25,1},{2,10},{10... | collective-permute-start | bytes 393224 | tf_op jit(solution)/shard_map/ppermute | solution.py:156
  22.0 1.5 %collective-permute-start.10 = (f32[256,128]{1,0:T(8,128)S(1)}, f32[256,128]{1,0:T(8,128)S(1)}, u32[]{:S(2)}, u32[]{:S(2)}) collective-permute-start(f32[256,128]{1,0:T(8,128)S(1)} %get-tuple-element.66), channel_id=1, source_target_pairs={{0,8},{8,16},{16,24},{24,0},{1,9},{9,17},{17,25},{25,1},{2,10},{10... | collective-permute-start | bytes 393224 | tf_op jit(solution)/shard_map/ppermute | solution.py:156
  23.5 1.2 %collective-permute-done.7.refs_2_ = f32[256,128]{1,0:T(8,128)S(1)} collective-permute-done((f32[256,128]{1,0:T(8,128)S(1)}, f32[256,128]{1,0:T(8,128)S(1)}, u32[]{:S(2)}, u32[]{:S(2)}) %collective-permute-start.7) | collective-permute-done | bytes 131104 | tf_op jit(solution)/shard_map/ppermute | solution.py:156
  24.7 4.7 %collective-permute-done.6.refs_1_ = f32[256,128]{1,0:T(8,128)S(1)} collective-permute-done((f32[256,128]{1,0:T(8,128)S(1)}, f32[256,128]{1,0:T(8,128)S(1)}, u32[]{:S(2)}, u32[]{:S(2)}) %collective-permute-start.6) | collective-permute-done | bytes 131104 | tf_op jit(solution)/shard_map/ppermute | solution.py:156
  29.4 0.0 collective-permute-done.5.refs_0_
  29.4 0.5 %shard_map.87 = (f32[256,128]{1,0:T(8,128)S(1)}, f32[256,128]{1,0:T(8,128)S(1)}, f32[32,128]{1,0:T(8,128)S(1)}, f32[32,128]{1,0:T(8,128)S(1)}) custom-call(f32[256,128]{1,0:T(8,128)S(1)} %collective-permute-done.5.refs_0_, f32[256,128]{1,0:T(8,128)S(1)} %collective-permute-done.6.refs_1_, f32[256,128]{1,0:T(8,128)S(1)} %collective-permute-done.7.refs_2_, ...), custom_call_target="tpu_custom_call" | custom-call | flops 100000000 | bytes 1048576 | tf_op jit(solution)/shard_map/pallas_call | solution.py:23
  29.9 0.1 collective-permute-start.8
  30.0 1.1 %collective-permute-start.9 = (f32[32,128]{1,0:T(8,128)S(1)}, f32[32,128]{1,0:T(8,128)S(1)}, u32[]{:S(2)}, u32[]{:S(2)}) collective-permute-start(f32[32,128]{1,0:T(8,128)S(1)} %get-tuple-element.63), channel_id=1, source_target_pairs={{0,7},{1,2},{2,1},{3,4},{4,3},{5,6},{6,5},{7,0},{8,15},{9,10},{10,... | collective-permute-start | bytes 49160 | tf_op jit(solution)/shard_map/ppermute | solution.py:153
  31.1 0.0 collective-permute-done.10.xb_ref
  31.1 1.2 %shard_map.88 = (f32[256,128]{1,0:T(8,128)S(1)}, f32[256,128]{1,0:T(8,128)S(1)}, f32[256,128]{1,0:T(8,128)S(1)}, f32[64,128]{1,0:T(8,128)S(1)}) custom-call(f32[256,128]{1,0:T(8,128)S(1)} %get-tuple-element.64.c_in, f32[256,128]{1,0:T(8,128)S(1)} %get-tuple-element.65.d_in, f32[256,128]{1,0:T(8,128)S(1)} %collective-permute-done.10.xb_ref, ...), custom_call_target="tpu_custom_call" | custom-call | flops 2000000000 | bytes 1048576 | tf_op jit(solution)/shard_map/pallas_call | solution.py:23
  32.3 0.0 collective-permute-done.8.re_ref
  32.3 2.7 %collective-permute-done.9.ro_ref = f32[32,128]{1,0:T(8,128)S(1)} collective-permute-done((f32[32,128]{1,0:T(8,128)S(1)}, f32[32,128]{1,0:T(8,128)S(1)}, u32[]{:S(2)}, u32[]{:S(2)}) %collective-permute-start.9) | collective-permute-done | bytes 16416 | tf_op jit(solution)/shard_map/ppermute | solution.py:153
  35.0 0.3 shard_map.89
  35.3 0.0 collective-permute-start.11
  35.4 1.1 %collective-permute-start.12 = (f32[32,128]{1,0:T(8,128)S(1)}, f32[32,128]{1,0:T(8,128)S(1)}, u32[]{:S(2)}, u32[]{:S(2)}) collective-permute-start(f32[32,128]{1,0:T(8,128)S(1)} %get-tuple-element.71), channel_id=1, source_target_pairs={{0,7},{1,2},{2,1},{3,4},{4,3},{5,6},{6,5},{7,0},{8,15},{9,10},{10,... | collective-permute-start | bytes 49160 | tf_op jit(solution)/shard_map/ppermute | solution.py:153
  36.5 1.5 %shard_map.90.p_ref = f32[512,128]{1,0:T(8,128)S(1)} custom-call(f32[32,128]{1,0:T(8,128)S(1)} %collective-permute-done.8.re_ref, f32[32,128]{1,0:T(8,128)S(1)} %collective-permute-done.9.ro_ref, f32[256,128]{1,0:T(8,128)S(1)} %get-tuple-element.72.a_in, f32[256,128]{1,0:T(8,128)S(1)} %get-tuple-element.73.b_in, f32[256,128]{1,0:T(8,128)S(1)} %get-tuple-element.74.z_in, ...), custom_call_target="tpu_custom_call" | custom-call | flops 2000000000 | bytes 1048576 | tf_op jit(solution)/shard_map/pallas_call | solution.py:23
  37.9 0.0 collective-permute-done.11.re_ref
  37.9 2.4 %collective-permute-done.12.ro_ref = f32[32,128]{1,0:T(8,128)S(1)} collective-permute-done((f32[32,128]{1,0:T(8,128)S(1)}, f32[32,128]{1,0:T(8,128)S(1)}, u32[]{:S(2)}, u32[]{:S(2)}) %collective-permute-start.12) | collective-permute-done | bytes 16416 | tf_op jit(solution)/shard_map/ppermute | solution.py:153
  40.4 1.1 %shard_map.91 = f32[512,128]{1,0:T(8,128)} custom-call(f32[32,128]{1,0:T(8,128)S(1)} %collective-permute-done.11.re_ref, f32[32,128]{1,0:T(8,128)S(1)} %collective-permute-done.12.ro_ref, f32[512,128]{1,0:T(8,128)S(1)} %shard_map.90.p_ref, bf16[9,256,256]{2,1,0:T(8,128)(2,1)S(1)} %get-tuple-element.46.w_ref.refs_5_, ...), custom_call_target="tpu_custom_call" | custom-call | flops 10000000 | bytes 1048576 | tf_op jit(solution)/shard_map/pallas_call | solution.py:23
Async XLA Ops:
  1.3 9.7 %collective-permute-start = (f32[32,128]{1,0:T(8,128)S(1)}, f32[32,128]{1,0:T(8,128)S(1)}, u32[]{:S(2)}, u32[]{:S(2)}) collective-permute-start(f32[32,128]{1,0:T(8,128)S(1)} %get-tuple-element.40), channel_id=1, source_target_pairs={{0,1},{1,0},{2,3},{3,2},{4,5},{5,4},{6,7},{7,6},{8,9},{9,8},{10,11... | collective-permute-start | bytes 49160 | tf_op jit(solution)/shard_map/ppermute | solution.py:153
  1.8 9.2 %collective-permute-start.1 = (f32[32,128]{1,0:T(8,128)S(1)}, f32[32,128]{1,0:T(8,128)S(1)}, u32[]{:S(2)}, u32[]{:S(2)}) collective-permute-start(f32[32,128]{1,0:T(8,128)S(1)} %get-tuple-element.41), channel_id=1, source_target_pairs={{0,7},{1,2},{2,1},{3,4},{4,3},{5,6},{6,5},{7,0},{8,15},{9,10},{10,... | collective-permute-start | bytes 49160 | tf_op jit(solution)/shard_map/ppermute | solution.py:153
  6.5 5.9 %collective-permute-start.2 = (f32[256,128]{1,0:T(8,128)S(1)}, f32[256,128]{1,0:T(8,128)S(1)}, u32[]{:S(2)}, u32[]{:S(2)}) collective-permute-start(f32[256,128]{1,0:T(8,128)S(1)} %get-tuple-element.42.xb_ref), channel_id=1, source_target_pairs={{0,8},{8,16},{16,24},{24,0},{1,9},{9,17},{17,25},{25,1},{2,10},{10... | collective-permute-start | bytes 393224 | tf_op jit(solution)/shard_map/ppermute | solution.py:156
  12.9 2.5 %collective-permute-start.3 = (f32[32,128]{1,0:T(8,128)S(1)}, f32[32,128]{1,0:T(8,128)S(1)}, u32[]{:S(2)}, u32[]{:S(2)}) collective-permute-start(f32[32,128]{1,0:T(8,128)S(1)} %get-tuple-element.49), channel_id=1, source_target_pairs={{0,1},{1,0},{2,3},{3,2},{4,5},{5,4},{6,7},{7,6},{8,9},{9,8},{10,11... | collective-permute-start | bytes 49160 | tf_op jit(solution)/shard_map/ppermute | solution.py:153
  13.0 5.0 %collective-permute-start.4 = (f32[32,128]{1,0:T(8,128)S(1)}, f32[32,128]{1,0:T(8,128)S(1)}, u32[]{:S(2)}, u32[]{:S(2)}) collective-permute-start(f32[32,128]{1,0:T(8,128)S(1)} %get-tuple-element.50), channel_id=1, source_target_pairs={{0,7},{1,2},{2,1},{3,4},{4,3},{5,6},{6,5},{7,0},{8,15},{9,10},{10,... | collective-permute-start | bytes 49160 | tf_op jit(solution)/shard_map/ppermute | solution.py:153
  18.4 6.3 %collective-permute-start.7 = (f32[256,128]{1,0:T(8,128)S(1)}, f32[256,128]{1,0:T(8,128)S(1)}, u32[]{:S(2)}, u32[]{:S(2)}) collective-permute-start(f32[256,128]{1,0:T(8,128)S(1)} %get-tuple-element.60.refs_3_), channel_id=1, source_target_pairs={{0,24},{8,0},{16,8},{24,16},{1,25},{9,1},{17,9},{25,17},{2,26},{10... | collective-permute-start | bytes 393224 | tf_op jit(solution)/shard_map/ppermute | solution.py:156
  20.0 9.4 %collective-permute-start.6 = (f32[256,128]{1,0:T(8,128)S(1)}, f32[256,128]{1,0:T(8,128)S(1)}, u32[]{:S(2)}, u32[]{:S(2)}) collective-permute-start(f32[256,128]{1,0:T(8,128)S(1)} %get-tuple-element.60.refs_3_), channel_id=1, source_target_pairs={{0,16},{8,24},{16,0},{24,8},{1,17},{9,25},{17,1},{25,9},{2,18},{10... | collective-permute-start | bytes 393224 | tf_op jit(solution)/shard_map/ppermute | solution.py:156
  20.5 8.9 %collective-permute-start.5 = (f32[256,128]{1,0:T(8,128)S(1)}, f32[256,128]{1,0:T(8,128)S(1)}, u32[]{:S(2)}, u32[]{:S(2)}) collective-permute-start(f32[256,128]{1,0:T(8,128)S(1)} %get-tuple-element.60.refs_3_), channel_id=1, source_target_pairs={{0,8},{8,16},{16,24},{24,0},{1,9},{9,17},{17,25},{25,1},{2,10},{10... | collective-permute-start | bytes 393224 | tf_op jit(solution)/shard_map/ppermute | solution.py:156
  22.0 9.1 %collective-permute-start.10 = (f32[256,128]{1,0:T(8,128)S(1)}, f32[256,128]{1,0:T(8,128)S(1)}, u32[]{:S(2)}, u32[]{:S(2)}) collective-permute-start(f32[256,128]{1,0:T(8,128)S(1)} %get-tuple-element.66), channel_id=1, source_target_pairs={{0,8},{8,16},{16,24},{24,0},{1,9},{9,17},{17,25},{25,1},{2,10},{10... | collective-permute-start | bytes 393224 | tf_op jit(solution)/shard_map/ppermute | solution.py:156
  29.9 2.4 %collective-permute-start.8 = (f32[32,128]{1,0:T(8,128)S(1)}, f32[32,128]{1,0:T(8,128)S(1)}, u32[]{:S(2)}, u32[]{:S(2)}) collective-permute-start(f32[32,128]{1,0:T(8,128)S(1)} %get-tuple-element.62), channel_id=1, source_target_pairs={{0,1},{1,0},{2,3},{3,2},{4,5},{5,4},{6,7},{7,6},{8,9},{9,8},{10,11... | collective-permute-start | bytes 49160 | tf_op jit(solution)/shard_map/ppermute | solution.py:153
  30.0 5.0 %collective-permute-start.9 = (f32[32,128]{1,0:T(8,128)S(1)}, f32[32,128]{1,0:T(8,128)S(1)}, u32[]{:S(2)}, u32[]{:S(2)}) collective-permute-start(f32[32,128]{1,0:T(8,128)S(1)} %get-tuple-element.63), channel_id=1, source_target_pairs={{0,7},{1,2},{2,1},{3,4},{4,3},{5,6},{6,5},{7,0},{8,15},{9,10},{10,... | collective-permute-start | bytes 49160 | tf_op jit(solution)/shard_map/ppermute | solution.py:153
  35.3 2.6 %collective-permute-start.11 = (f32[32,128]{1,0:T(8,128)S(1)}, f32[32,128]{1,0:T(8,128)S(1)}, u32[]{:S(2)}, u32[]{:S(2)}) collective-permute-start(f32[32,128]{1,0:T(8,128)S(1)} %get-tuple-element.70), channel_id=1, source_target_pairs={{0,1},{1,0},{2,3},{3,2},{4,5},{5,4},{6,7},{7,6},{8,9},{9,8},{10,11... | collective-permute-start | bytes 49160 | tf_op jit(solution)/shard_map/ppermute | solution.py:153
  35.4 5.0 %collective-permute-start.12 = (f32[32,128]{1,0:T(8,128)S(1)}, f32[32,128]{1,0:T(8,128)S(1)}, u32[]{:S(2)}, u32[]{:S(2)}) collective-permute-start(f32[32,128]{1,0:T(8,128)S(1)} %get-tuple-element.71), channel_id=1, source_target_pairs={{0,7},{1,2},{2,1},{3,4},{4,3},{5,6},{6,5},{7,0},{8,15},{9,10},{10,... | collective-permute-start | bytes 49160 | tf_op jit(solution)/shard_map/ppermute | solution.py:153

commit v3 on v2

--- a/solution.py
+++ b/solution.py
@@ -149,8 +149,11 @@
     swap_e = [(i, i ^ 1) for i in range(ring)]
     swap_o = [(i, (i + 1) % ring if i % 2 else (i - 1) % ring) for i in range(ring)]
 
-    def exchange(to_e, to_o):
-        return lax.ppermute(to_e, "space", swap_e), lax.ppermute(to_o, "space", swap_o)
+    def over_e(x):
+        return lax.ppermute(x, "space", swap_e)
+
+    def over_o(x):
+        return lax.ppermute(x, "space", swap_o)
 
     def later(x, by):
         return lax.ppermute(x, "tm", [(i, (i + by) % groups) for i in range(groups)])
@@ -200,12 +203,12 @@
         flops=1e7,
     )
     before = later(xb, 1)
-    re0, ro0 = exchange(e0, o0)
+    re0, ro0 = over_e(e0), over_o(o0)
 
     def setup_kernel(
         xa_ref, xb_ref, scale_hbm, d_hbm, inv_hbm, f_hbm, t_hbm, nbr_hbm, send_hbm,
-        v_ref, part_ref, psent_ref, sigs_ref, w_ref, pick_ref, q_ref, qs_ref, sent_ref,
-        sig_ref, frac_ref,
+        v_ref, part_ref, psent_ref, sigs_ref, fracs_ref, w_ref, pick_ref, picko_ref, q_ref, qs_ref,
+        qo_ref, sent_ref, sig_ref, frac_ref,
         scale_ref, d_ref, inv_ref, f_ref, t_ref, nbr_ref, send_ref, rows_ref, sems,
     ):
         copies = fetch(
@@ -231,7 +234,8 @@
         scale = column(scale_ref[...], width)
         sigma = DAMPING / scale
         sig_ref[...] = sigma
-        frac_ref[...] = 1.0 / (2.0 * scale - 1.0)
+        frac = 1.0 / (2.0 * scale - 1.0)
+        frac_ref[...] = frac
         lane = lax.broadcasted_iota(jnp.int32, (elements, elements), 1)
         spot = lax.broadcasted_iota(jnp.int32, (elements, far), 1)
         wanted = jnp.zeros((elements, far), jnp.int32)
@@ -248,7 +252,12 @@
             rows_ref[i : i + 1, :] = jnp.where(strip == sent_at(send_ref, i), 1.0, 0.0)
         chosen = rows_ref[...].astype(BF16)
         sent_ref[...] = chosen
-        qs_ref[...] = dot(chosen, q).astype(BF16)
+        qs = dot(chosen, q)
+        qs_ref[...] = qs.astype(BF16)
+        for f in range(faces):
+            picko_ref[f * halo : (f + 1) * halo, :] = dot(
+                chosen[halo:], pick_ref[f * elements : (f + 1) * elements, :]
+            ).astype(BF16)
         head = weight_tile(inv)
         v = [product(split(x[...]), head) for x in (xa_ref, xb_ref)]
         cut = [split(x) for x in v]
@@ -263,19 +272,26 @@
             )
             v_ref[t * elements : (t + 1) * elements, :] = v[t]
             part_ref[t * elements : (t + 1) * elements, :] = parts[t]
-        got = at_sent(sent_ref, parts + [sigma])
+        got = at_sent(sent_ref, parts + [sigma, frac])
         for t in range(slabs):
             psent_ref[t * sent : (t + 1) * sent, :] = got[t]
         sigs_ref[...] = got[slabs]
+        fracs_ref[...] = got[slabs + 1]
+        near_half = lax.broadcasted_iota(jnp.int32, (halo, far), 1) % sent < halo
+        even = lax.axis_index("space") % 2 == 0
+        kept = jnp.where(near_half, jnp.where(even, 1.0, 0.0), jnp.where(even, 0.0, 1.0))
+        qo_ref[...] = got[slabs + 1][halo:] * qs[halo:] * kept
 
     (
-        v0, part1, psent1, sig_sent, weights, pick, q_all, q_sent, choose, sigma_all, frac_all,
+        v0, part1, psent1, sig_sent, frac_sent, weights, pick, pick_o, q_all, q_sent, q_o, choose,
+        sigma_all, frac_all,
     ) = call(
         setup_kernel,
         [
-            two, two, ((slabs * sent, width), F32), ((sent, width), F32),
+            two, two, ((slabs * sent, width), F32), ((sent, width), F32), ((sent, width), F32),
             ((stack, 2 * width, 2 * width), BF16), ((faces * elements, elements), BF16),
-            ((elements, far), BF16), ((sent, far), BF16), ((sent, elements), BF16), full, full,
+            ((faces * halo, elements), BF16), ((elements, far), BF16), ((sent, far), BF16),
+            ((halo, far), F32), ((sent, elements), BF16), full, full,
         ],
         [
             xa, xb, scale_row, diag_block, block_inverse, face_flux, time_trace, faces_row,
@@ -311,26 +327,74 @@
         new[0] = new[0] + sig * old
         put_sent(e_ref, o_ref, new)
 
-    e1, o1 = call(
+    e1, vo = call(
         edge_one,
         [edge, edge],
         [re0, ro0, before, psent1, sig_sent, weights, q_sent, choose],
         flops=1e7,
     )
-    re1, ro1 = exchange(e1, o1)
-
-    def middle(
-        re_ref, ro_ref, b_ref, part_ref, v_ref, w_ref, pick_ref, q_ref, sig_ref, frac_ref,
-        v1_ref, pa_ref, pb_ref, wp_ref, x_ref,
+    re1 = over_e(e1)
+
+    def ahead(
+        re_ref, ro_ref, b_ref, part_ref, vo_ref, o0_ref, w_ref, picko_ref, q_ref, sig_ref,
+        sigs_ref, fracs_ref, v1_ref, wo_ref,
     ):
         sigma = sig_ref[...]
-        frac = frac_ref[...]
         add = spread(q_ref[...], far_faces(faces, arrived(re_ref, ro_ref, slabs), w_ref), slabs)
         old = time_mask(product(split(b_ref[...]), w_ref[W_SOURCE_TIME]))
         va = part_ref[:elements, :] + sigma * add[0] + sigma * old
         vb = part_ref[elements:, :] + sigma * add[1]
+        v1_ref[:elements, :] = va
+        v1_ref[elements:, :] = vb
+        picked = dot(picko_ref[...], split(va + vb)).astype(BF16)
+        near = None
+        for f in range(faces):
+            term = dot(picked[f * halo : (f + 1) * halo], w_ref[W_FACE + f])
+            near = term if near is None else near + term
+        sa, sb = vo_ref[:halo, :], vo_ref[halo:, :]
+        rest = (
+            o0_ref[:halo, :] + o0_ref[halo:, :] - DAMPING * product(split(sa + sb), w_ref[W_DIAG])
+        ) / sigs_ref[halo:, :]
+        rest = rest + product(split(sa), w_ref[W_TIME]) + halves(near)
+        wo_ref[...] = fracs_ref[halo:, :] * rest + sb
+
+    v1, w_part = call(
+        ahead,
+        [two, ((halo, width), F32)],
+        [
+            re0, ro0, before, part1, vo, o0, weights, pick_o, q_all, sigma_all, sig_sent,
+            frac_sent,
+        ],
+        flops=2e8,
+    )
+
+    def edge_w(re_ref, wo_ref, vo_ref, w_ref, qs_ref, fracs_ref, qo_ref, o_ref):
+        both = re_ref[:halo, :] + re_ref[halo:, :]
+        none = jnp.zeros_like(both)
+        even = lax.axis_index("space") % 2 == 0
+        rows = jnp.concatenate([jnp.where(even, none, both), jnp.where(even, both, none)], axis=0)
+        add = spread(qs_ref[halo:, :], far_faces(faces, [rows], w_ref), 1)[0]
+        frac = fracs_ref[halo:, :]
+        o_ref[: slabs * halo, :] = vo_ref[...]
+        o_ref[slabs * halo : (slabs + 1) * halo, :] = wo_ref[...] + frac * add
+        o_ref[(slabs + 1) * halo : (slabs + 2) * halo, :] = qo_ref[...]
+        o_ref[(slabs + 2) * halo :, :] = frac
+
+    (o1,) = call(
+        edge_w,
+        [(((slabs + 3) * halo, width), F32)],
+        [re1, w_part, vo, weights, q_sent, frac_sent, q_o],
+        flops=1e7,
+    )
+    ro1 = over_o(o1)
+
+    def middle(
+        v1_ref, v_ref, w_ref, pick_ref, sig_ref, frac_ref, pa_ref, pb_ref, wp_ref, x_ref
+    ):
+        sigma = sig_ref[...]
+        frac = frac_ref[...]
+        va, vb = v1_ref[:elements, :], v1_ref[elements:, :]
         v0a, v0b = v_ref[:elements, :], v_ref[elements:, :]
-        v1_ref[...] = vb
         ca, cb = split(va), split(vb)
         ga, gb = own_faces(faces, pick_ref, w_ref, [ca, cb])
         da, db = product(ca, w_ref[W_DIAG]), product(cb, w_ref[W_DIAG])
@@ -342,26 +406,37 @@
         )
         x_ref[...] = v0b + sigma * (ta - tb)
 
-    v1b, pa0, pb0, wp, x_own = call(
+    pa0, pb0, wp, x_own = call(
         middle,
-        [full] * 5,
-        [re0, ro0, before, part1, v0, weights, pick, q_all, sigma_all, frac_all],
-        flops=2e9,
-    )
+        [full] * 4,
+        [v1, v0, weights, pick, sigma_all, frac_all],
+        flops=1e9,
+    )
+
+    more = ((elements + halo, width), F32)
 
     def coarse_kernel(
-        re_ref, ro_ref, wp_ref, pa_ref, pb_ref, w_ref, q_ref, sig_ref, frac_ref,
+        re_ref, ro_ref, vo_ref, wp_ref, pa_ref, pb_ref, w_ref, q_ref, sig_ref, frac_ref,
         w_out, pa_out, pb_out,
     ):
-        add = spread(q_ref[...], far_faces(faces, arrived(re_ref, ro_ref, slabs), w_ref), slabs)
-        w_out[...] = wp_ref[...] + frac_ref[...] * (add[0] + add[1])
+        rows = arrived(re_ref, ro_ref.at[: slabs * halo, :], slabs)
+        both = vo_ref[:halo, :] + vo_ref[halo:, :]
+        rows.append(jnp.concatenate([both, both], axis=0))
+        table = far_faces(faces, rows, w_ref)
+        lanes = 2 * width
+        add = spread(q_ref[...], table[:, : slabs * lanes], slabs)
+        mine = halves(table[:, slabs * lanes :].astype(F32))
+        w_out[:elements, :] = wp_ref[...] + frac_ref[...] * (add[0] + add[1])
+        w_out[elements:, :] = ro_ref[slabs * halo : (slabs + 1) * halo, :] + dot32(
+            ro_ref[(slabs + 1) * halo : (slabs + 2) * halo, :], mine
+        )
         pa_out[...] = pa_ref[...] + sig_ref[...] * add[0]
         pb_out[...] = pb_ref[...] + sig_ref[...] * add[1]
 
     w_own, pa1, pb1 = call(
         coarse_kernel,
-        [full] * 3,
-        [re1, ro1, wp, pa0, pb0, weights, q_all, sigma_all, frac_all],
+        [more, full, full],
+        [re1, ro1, vo, wp, pa0, pb0, weights, q_all, sigma_all, frac_all],
         flops=1e7,
     )
     earlier = [later(w_own, a) for a in range(1, groups)]
@@ -369,12 +444,16 @@
 
     def recur(*refs):
         olds = refs[: groups - 1]
-        w_own_ref, v1_ref, w_ref, sent_ref, frac_ref, c_ref, d_ref, e_ref, o_ref = refs[
+        w_own_ref, v1_ref, ro_ref, w_ref, sent_ref, frac_ref, c_ref, d_ref, e_ref, oh_ref = refs[
             groups - 1 :
         ]
-        frac = frac_ref[...]
+        frac = jnp.concatenate([frac_ref[...], ro_ref[(slabs + 2) * halo :, :]], axis=0)
+        v_last = jnp.concatenate(
+            [v1_ref[(slabs - 1) * elements :, :], ro_ref[(slabs - 1) * halo : slabs * halo, :]],
+            axis=0,
+        )
         d = time_mask(olds[0][...])
-        c = w_own_ref[...] - v1_ref[...]
+        c = w_own_ref[...] - v_last
         power = frac
         for a in range(1, groups):
             cut = split(time_mask(power * olds[a - 1][...], a))
@@ -383,17 +462,22 @@
                 cut = split(time_mask(power * olds[a][...], a + 1))
                 d = d + product(cut, w_ref[W_TIME + a - 1])
                 power = power * frac
-        c_ref[...] = c
-        d_ref[...] = d
-        put_sent(e_ref, o_ref, at_sent(sent_ref, [c, d]))
-
-    c_all, d_all, e2, o2 = call(
+        c_ref[...] = c[:elements]
+        d_ref[...] = d[:elements]
+        oh_ref[:halo, :] = c[elements:]
+        oh_ref[halo:, :] = d[elements:]
+        every = jnp.concatenate([split(c[:elements]), split(d[:elements])], axis=1)
+        got = spread(sent_ref[:halo, :], every, 2)
+        e_ref[:halo, :] = got[0]
+        e_ref[halo:, :] = got[1]
+
+    c_all, d_all, e2, ro2 = call(
         recur,
         [full, full, edge, edge],
-        [*earlier, w_own, v1b, weights, choose, frac_all],
+        [*earlier, w_own, v1, ro1, weights, choose, frac_all],
         flops=1e8,
     )
-    re2, ro2 = exchange(e2, o2)
+    re2 = over_e(e2)
 
     def second(
         c_in, d_in, xb_ref, pa_ref, pb_ref, w_ref, pick_ref, sig_ref, sent_ref,
@@ -436,7 +520,7 @@
         [re2, ro2, psent3, sig_sent, weights, q_sent],
         flops=1e7,
     )
-    re3, ro3 = exchange(e3, o3)
+    re3, ro3 = over_e(e3), over_o(o3)
 
     def third(
         re_ref, ro_ref, a_in, b_in, z_in, v_ref, w_ref, pick_ref, q_ref, sig_ref, out_ref

time: 41.6 us -> 40.1 us (0.964)
  waiting for transfers between devices: 15 us -> 13.2 us
  Pallas kernels: 11.2 us -> 12.3 us
  starting transfers between devices: 15.2 us -> 14.4 us
    ppermute x8 -> x7, waiting for transfers between devices: 7.72 us -> 6.06 us  [the longest x3 5.7 us: over_o(): return lax.ppermute(x, 'space', swap_o)]
    pallas_call x10 -> x12, Pallas kernels: 11.2 us -> 12.3 us  [call(): pl.pallas_call(kernel, out_shape=[jax.ShapeDtypeStruct(s, d) for s, d in...]
    ppermute x8 -> x7, starting transfers between devices: 8.58 us -> 7.78 us  [the longest x3 6.63 us: over_o(): return lax.ppermute(x, 'space', swap_o)]
  transfers between devices with their start and end apart: 13 -> 12, of which waited for: 6 -> 6; matrix products, arithmetic and copies ran while one was open for 0% -> 0% of each run, Pallas kernels for 18% -> 21%
where the time goes in v3:
time: 40.1 us; the launch traced here: 39.9 us
  starting transfers between devices  14.4 us (36%)
  waiting for transfers between devices  13.2 us (33%)
  Pallas kernels  12.3 us (31%)
    pallas_call x12, Pallas kernels, call(): pl.pallas_call(kernel, out_shape=[jax.ShapeDtypeStruct(s, d) for s, d in...  12.3 us
    ppermute x5, waiting for transfers between devices, later(): lax.ppermute(x, 'tm', [(i, (i + by) % groups) for i in range(groups)])  7.16 us
    ppermute x3, starting transfers between devices, over_o(): return lax.ppermute(x, 'space', swap_o)  6.63 us
    ppermute x5, starting transfers between devices, later(): lax.ppermute(x, 'tm', [(i, (i + by) % groups) for i in range(groups)])  6.58 us
    ppermute x3, waiting for transfers between devices, over_o(): return lax.ppermute(x, 'space', swap_o)  5.7 us
    ppermute x4, starting transfers between devices, over_e(): return lax.ppermute(x, 'space', swap_e)  1.15 us
  transfers between devices with their start and end apart: 12, of which 6 were waited for; matrix products, arithmetic and copies ran while one was open for 0% of the time, Pallas kernels for 21%

profile of v3, /device:TPU:0, one launch (start us, length us, event | category | flops | bytes accessed | tf_op | source)
XLA Modules:
  0.0 39.9 jit_solution(13732523027858359597)
XLA Ops:
  0.0 1.3 %shard_map.82 = (f32[32,128]{1,0:T(8,128)S(1)}, f32[32,128]{1,0:T(8,128)S(1)}, f32[256,128]{1,0:T(8,128)S(1)}, f32[256,128]{1,0:T(8,128)S(1)}) custom-call(f32[512,128]{1,0:T(8,128)} %bitcast.4, f32[1,256]{1,0:T(1,128)} %bitcast.5, f32[128,128]{1,0:T(8,128)} %inv_hbm.3, s32[1,32]{1,0:T(1,128)} %send_hbm.3), custom_call_target="tpu_custom_call" | custom-call | flops 10000000 | bytes 1048576 | tf_op jit(solution)/shard_map/pallas_call | solution.py:23
  1.3 0.6 %collective-permute-start = (f32[32,128]{1,0:T(8,128)S(1)}, f32[32,128]{1,0:T(8,128)S(1)}, u32[]{:S(2)}, u32[]{:S(2)}) collective-permute-start(f32[32,128]{1,0:T(8,128)S(1)} %get-tuple-element.44), channel_id=1, source_target_pairs={{0,1},{1,0},{2,3},{3,2},{4,5},{5,4},{6,7},{7,6},{8,9},{9,8},{10,11... | collective-permute-start | bytes 49160 | tf_op jit(solution)/shard_map/ppermute | solution.py:153
  1.8 4.7 %collective-permute-start.1 = (f32[32,128]{1,0:T(8,128)S(1)}, f32[32,128]{1,0:T(8,128)S(1)}, u32[]{:S(2)}, u32[]{:S(2)}) collective-permute-start(f32[32,128]{1,0:T(8,128)S(1)} %get-tuple-element.45.o0_ref), channel_id=1, source_target_pairs={{0,7},{1,2},{2,1},{3,4},{4,3},{5,6},{6,5},{7,0},{8,15},{9,10},{10,... | collective-permute-start | bytes 49160 | tf_op jit(solution)/shard_map/ppermute | solution.py:156
  6.5 1.5 %collective-permute-start.2 = (f32[256,128]{1,0:T(8,128)S(1)}, f32[256,128]{1,0:T(8,128)S(1)}, u32[]{:S(2)}, u32[]{:S(2)}) collective-permute-start(f32[256,128]{1,0:T(8,128)S(1)} %get-tuple-element.46.xb_ref), channel_id=1, source_target_pairs={{0,8},{8,16},{16,24},{24,0},{1,9},{9,17},{17,25},{25,1},{2,10},{10... | collective-permute-start | bytes 393224 | tf_op jit(solution)/shard_map/ppermute | solution.py:159
  8.0 3.2 %shard_map.83 = (f32[512,128]{1,0:T(8,128)S(1)}, f32[512,128]{1,0:T(8,128)S(1)}, f32[64,128]{1,0:T(8,128)S(1)}, f32[32,128]{1,0:T(8,128)S(1)}, f32[32,128]{1,0:T...) custom-call(f32[256,128]{1,0:T(8,128)S(1)} %get-tuple-element.47.xa_, ...), custom_call_target="tpu_custom_call" | custom-call | flops 2000000000 | bytes 1048576 | tf_op jit(solution)/shard_map/pallas_call | solution.py:23
  11.2 0.0 collective-permute-done.re_ref
  11.2 0.0 collective-permute-done.1.ro_ref
  11.2 1.2 %collective-permute-done.2.b_ref = f32[256,128]{1,0:T(8,128)S(1)} collective-permute-done((f32[256,128]{1,0:T(8,128)S(1)}, f32[256,128]{1,0:T(8,128)S(1)}, u32[]{:S(2)}, u32[]{:S(2)}) %collective-permute-start.2) | collective-permute-done | bytes 131104 | tf_op jit(solution)/shard_map/ppermute | solution.py:159
  12.4 0.5 %shard_map.84 = (f32[32,128]{1,0:T(8,128)S(1)}, f32[32,128]{1,0:T(8,128)S(1)}) custom-call(f32[32,128]{1,0:T(8,128)S(1)} %collective-permute-done.re_ref, f32[32,128]{1,0:T(8,128)S(1)} %collective-permute-done.1.ro_ref, f32[256,128]{1,0:T(8,128)S(1)} %collective-permute-done.2.b_ref, f32[64,128]{1,0:T(8,128)S(1)} %get-tuple-element.48.psent_ref, ...), custom_call_target="tpu_custom_call" | custom-call | flops 10000000 | bytes 1048576 | tf_op jit(solution)/shard_map/pallas_call | solution.py:23
  12.9 0.1 collective-permute-start.3
  13.0 0.8 %shard_map.85 = (f32[512,128]{1,0:T(8,128)S(1)}, f32[16,128]{1,0:T(8,128)S(1)}) custom-call(f32[32,128]{1,0:T(8,128)S(1)} %collective-permute-done.re_ref, f32[32,128]{1,0:T(8,128)S(1)} %collective-permute-done.1.ro_ref, f32[256,128]{1,0:T(8,128)S(1)} %collective-permute-done.2.b_ref, f32[512,128]{1,0:T(8,128)S(1)} %get-tuple-element.54.part_ref, ...), custom_call_target="tpu_custom_call" | custom-call | flops 200000000 | bytes 1048576 | tf_op jit(solution)/shard_map/pallas_call | solution.py:23
  13.8 0.4 collective-permute-done.3.re_ref
  14.1 0.3 shard_map.86
  14.4 0.6 %collective-permute-start.4 = (f32[80,128]{1,0:T(8,128)S(1)}, f32[80,128]{1,0:T(8,128)S(1)}, u32[]{:S(2)}, u32[]{:S(2)}) collective-permute-start(f32[80,128]{1,0:T(8,128)S(1)} %shard_map.86), channel_id=1, source_target_pairs={{0,7},{1,2},{2,1},{3,4},{4,3},{5,6},{6,5},{7,0},{8,15},{9,10},{10,... | collective-permute-start | bytes 122888 | tf_op jit(solution)/shard_map/ppermute | solution.py:156
  15.1 1.1 %shard_map.87 = (f32[256,128]{1,0:T(8,128)S(1)}, f32[256,128]{1,0:T(8,128)S(1)}, f32[256,128]{1,0:T(8,128)S(1)}, f32[256,128]{1,0:T(8,128)S(1)}) custom-call(f32[512,128]{1,0:T(8,128)S(1)} %get-tuple-element.62.v1_ref.refs_4_, f32[512,128]{1,0:T(8,128)S(1)} %get-tuple-element.63.v_ref, bf16[9,256,256]{2,1,0:T(8,128)(2,1)S(1)} %get-tuple-element.50.w_ref.refs_6_, ...), custom_call_target="tpu_custom_call" | custom-call | flops 1000000000 | bytes 1048576 | tf_op jit(solution)/shard_map/pallas_call | solution.py:23
  16.1 3.5 %collective-permute-done.4.ro_ref.refs_5_ = f32[80,128]{1,0:T(8,128)S(1)} collective-permute-done((f32[80,128]{1,0:T(8,128)S(1)}, f32[80,128]{1,0:T(8,128)S(1)}, u32[]{:S(2)}, u32[]{:S(2)}) %collective-permute-start.4) | collective-permute-done | bytes 40992 | tf_op jit(solution)/shard_map/ppermute | solution.py:156
  19.7 0.4 %shard_map.88 = (f32[272,128]{1,0:T(8,128)S(1)}, f32[256,128]{1,0:T(8,128)S(1)}, f32[256,128]{1,0:T(8,128)S(1)}) custom-call(f32[32,128]{1,0:T(8,128)S(1)} %collective-permute-done.3.re_ref, f32[80,128]{1,0:T(8,128)S(1)} %collective-permute-done.4.ro_ref.refs_5_, f32[32,128]{1,0:T(8,128)S(1)} %get-tuple-element.55.vo_ref, ...), custom_call_target="tpu_custom_call" | custom-call | flops 10000000 | bytes 1048576 | tf_op jit(solution)/shard_map/pallas_call | solution.py:23
  20.1 1.6 %collective-permute-start.7 = (f32[272,128]{1,0:T(8,128)S(1)}, f32[272,128]{1,0:T(8,128)S(1)}, u32[]{:S(2)}, u32[]{:S(2)}) collective-permute-start(f32[272,128]{1,0:T(8,128)S(1)} %get-tuple-element.69.refs_3_), channel_id=1, source_target_pairs={{0,24},{8,0},{16,8},{24,16},{1,25},{9,1},{17,9},{25,17},{2,26},{10... | collective-permute-start | bytes 417800 | tf_op jit(solution)/shard_map/ppermute | solution.py:159
  21.7 0.5 %collective-permute-start.6 = (f32[272,128]{1,0:T(8,128)S(1)}, f32[272,128]{1,0:T(8,128)S(1)}, u32[]{:S(2)}, u32[]{:S(2)}) collective-permute-start(f32[272,128]{1,0:T(8,128)S(1)} %get-tuple-element.69.refs_3_), channel_id=1, source_target_pairs={{0,16},{8,24},{16,0},{24,8},{1,17},{9,25},{17,1},{25,9},{2,18},{10... | collective-permute-start | bytes 417800 | tf_op jit(solution)/shard_map/ppermute | solution.py:159
  22.2 1.5 %collective-permute-start.5 = (f32[272,128]{1,0:T(8,128)S(1)}, f32[272,128]{1,0:T(8,128)S(1)}, u32[]{:S(2)}, u32[]{:S(2)}) collective-permute-start(f32[272,128]{1,0:T(8,128)S(1)} %get-tuple-element.69.refs_3_), channel_id=1, source_target_pairs={{0,8},{8,16},{16,24},{24,0},{1,9},{9,17},{17,25},{25,1},{2,10},{10... | collective-permute-start | bytes 417800 | tf_op jit(solution)/shard_map/ppermute | solution.py:159
  23.7 1.5 %collective-permute-start.9 = (f32[256,128]{1,0:T(8,128)S(1)}, f32[256,128]{1,0:T(8,128)S(1)}, u32[]{:S(2)}, u32[]{:S(2)}) collective-permute-start(f32[256,128]{1,0:T(8,128)S(1)} %get-tuple-element.74), channel_id=1, source_target_pairs={{0,8},{8,16},{16,24},{24,0},{1,9},{9,17},{17,25},{25,1},{2,10},{10... | collective-permute-start | bytes 393224 | tf_op jit(solution)/shard_map/ppermute | solution.py:159
  25.2 1.5 %collective-permute-done.7.refs_2_ = f32[272,128]{1,0:T(8,128)S(1)} collective-permute-done((f32[272,128]{1,0:T(8,128)S(1)}, f32[272,128]{1,0:T(8,128)S(1)}, u32[]{:S(2)}, u32[]{:S(2)}) %collective-permute-start.7) | collective-permute-done | bytes 139296 | tf_op jit(solution)/shard_map/ppermute | solution.py:159
  26.7 4.5 %collective-permute-done.6.refs_1_ = f32[272,128]{1,0:T(8,128)S(1)} collective-permute-done((f32[272,128]{1,0:T(8,128)S(1)}, f32[272,128]{1,0:T(8,128)S(1)}, u32[]{:S(2)}, u32[]{:S(2)}) %collective-permute-start.6) | collective-permute-done | bytes 139296 | tf_op jit(solution)/shard_map/ppermute | solution.py:159
  31.2 0.0 collective-permute-done.5.refs_0_
  31.2 0.5 %shard_map.89 = (f32[256,128]{1,0:T(8,128)S(1)}, f32[256,128]{1,0:T(8,128)S(1)}, f32[32,128]{1,0:T(8,128)S(1)}, f32[32,128]{1,0:T(8,128)S(1)}) custom-call(f32[272,128]{1,0:T(8,128)S(1)} %collective-permute-done.5.refs_0_, f32[272,128]{1,0:T(8,128)S(1)} %collective-permute-done.6.refs_1_, f32[272,128]{1,0:T(8,128)S(1)} %collective-permute-done.7.refs_2_, ...), custom_call_target="tpu_custom_call" | custom-call | flops 100000000 | bytes 1048576 | tf_op jit(solution)/shard_map/pallas_call | solution.py:23
  31.8 0.0 collective-permute-start.8
  31.8 0.0 collective-permute-done.9.xb_ref
  31.8 1.2 %shard_map.90 = (f32[256,128]{1,0:T(8,128)S(1)}, f32[256,128]{1,0:T(8,128)S(1)}, f32[256,128]{1,0:T(8,128)S(1)}, f32[64,128]{1,0:T(8,128)S(1)}) custom-call(f32[256,128]{1,0:T(8,128)S(1)} %get-tuple-element.72.c_in, f32[256,128]{1,0:T(8,128)S(1)} %get-tuple-element.73.d_in, f32[256,128]{1,0:T(8,128)S(1)} %collective-permute-done.9.xb_ref, ...), custom_call_target="tpu_custom_call" | custom-call | flops 2000000000 | bytes 1048576 | tf_op jit(solution)/shard_map/pallas_call | solution.py:23
  33.0 0.0 collective-permute-done.8.re_ref
  33.0 0.3 shard_map.91
  33.3 0.5 %collective-permute-start.10 = (f32[32,128]{1,0:T(8,128)S(1)}, f32[32,128]{1,0:T(8,128)S(1)}, u32[]{:S(2)}, u32[]{:S(2)}) collective-permute-start(f32[32,128]{1,0:T(8,128)S(1)} %get-tuple-element.78), channel_id=1, source_target_pairs={{0,1},{1,0},{2,3},{3,2},{4,5},{5,4},{6,7},{7,6},{8,9},{9,8},{10,11... | collective-permute-start | bytes 49160 | tf_op jit(solution)/shard_map/ppermute | solution.py:153
  33.8 1.3 %collective-permute-start.11 = (f32[32,128]{1,0:T(8,128)S(1)}, f32[32,128]{1,0:T(8,128)S(1)}, u32[]{:S(2)}, u32[]{:S(2)}) collective-permute-start(f32[32,128]{1,0:T(8,128)S(1)} %get-tuple-element.79), channel_id=1, source_target_pairs={{0,7},{1,2},{2,1},{3,4},{4,3},{5,6},{6,5},{7,0},{8,15},{9,10},{10,... | collective-permute-start | bytes 49160 | tf_op jit(solution)/shard_map/ppermute | solution.py:156
  35.2 1.5 %shard_map.92.p_ref = f32[512,128]{1,0:T(8,128)S(1)} custom-call(f32[32,128]{1,0:T(8,128)S(1)} %collective-permute-done.8.re_ref, f32[32,128]{1,0:T(8,128)S(1)} %get-tuple-element.71.ro_ref, f32[256,128]{1,0:T(8,128)S(1)} %get-tuple-element.80.a_in, f32[256,128]{1,0:T(8,128)S(1)} %get-tuple-element.81.b_in, f32[256,128]{1,0:T(8,128)S(1)} %get-tuple-element.82.z_in, ...), custom_call_target="tpu_custom_call" | custom-call | flops 2000000000 | bytes 1048576 | tf_op jit(solution)/shard_map/pallas_call | solution.py:23
  36.6 0.0 collective-permute-done.10.re_ref
  36.6 2.2 %collective-permute-done.11.ro_ref = f32[32,128]{1,0:T(8,128)S(1)} collective-permute-done((f32[32,128]{1,0:T(8,128)S(1)}, f32[32,128]{1,0:T(8,128)S(1)}, u32[]{:S(2)}, u32[]{:S(2)}) %collective-permute-start.11) | collective-permute-done | bytes 16416 | tf_op jit(solution)/shard_map/ppermute | solution.py:156
  38.8 1.1 %shard_map.93 = f32[512,128]{1,0:T(8,128)} custom-call(f32[32,128]{1,0:T(8,128)S(1)} %collective-permute-done.10.re_ref, f32[32,128]{1,0:T(8,128)S(1)} %collective-permute-done.11.ro_ref, f32[512,128]{1,0:T(8,128)S(1)} %shard_map.92.p_ref, bf16[9,256,256]{2,1,0:T(8,128)(2,1)S(1)} %get-tuple-element.50.w_ref.refs_6_, ...), custom_call_target="tpu_custom_call" | custom-call | flops 10000000 | bytes 1048576 | tf_op jit(solution)/shard_map/pallas_call | solution.py:23
Async XLA Ops:
  1.3 10.0 %collective-permute-start = (f32[32,128]{1,0:T(8,128)S(1)}, f32[32,128]{1,0:T(8,128)S(1)}, u32[]{:S(2)}, u32[]{:S(2)}) collective-permute-start(f32[32,128]{1,0:T(8,128)S(1)} %get-tuple-element.44), channel_id=1, source_target_pairs={{0,1},{1,0},{2,3},{3,2},{4,5},{5,4},{6,7},{7,6},{8,9},{9,8},{10,11... | collective-permute-start | bytes 49160 | tf_op jit(solution)/shard_map/ppermute | solution.py:153
  1.8 9.4 %collective-permute-start.1 = (f32[32,128]{1,0:T(8,128)S(1)}, f32[32,128]{1,0:T(8,128)S(1)}, u32[]{:S(2)}, u32[]{:S(2)}) collective-permute-start(f32[32,128]{1,0:T(8,128)S(1)} %get-tuple-element.45.o0_ref), channel_id=1, source_target_pairs={{0,7},{1,2},{2,1},{3,4},{4,3},{5,6},{6,5},{7,0},{8,15},{9,10},{10,... | collective-permute-start | bytes 49160 | tf_op jit(solution)/shard_map/ppermute | solution.py:156
  6.5 5.9 %collective-permute-start.2 = (f32[256,128]{1,0:T(8,128)S(1)}, f32[256,128]{1,0:T(8,128)S(1)}, u32[]{:S(2)}, u32[]{:S(2)}) collective-permute-start(f32[256,128]{1,0:T(8,128)S(1)} %get-tuple-element.46.xb_ref), channel_id=1, source_target_pairs={{0,8},{8,16},{16,24},{24,0},{1,9},{9,17},{17,25},{25,1},{2,10},{10... | collective-permute-start | bytes 393224 | tf_op jit(solution)/shard_map/ppermute | solution.py:159
  12.9 1.2 %collective-permute-start.3 = (f32[32,128]{1,0:T(8,128)S(1)}, f32[32,128]{1,0:T(8,128)S(1)}, u32[]{:S(2)}, u32[]{:S(2)}) collective-permute-start(f32[32,128]{1,0:T(8,128)S(1)} %get-tuple-element.53), channel_id=1, source_target_pairs={{0,1},{1,0},{2,3},{3,2},{4,5},{5,4},{6,7},{7,6},{8,9},{9,8},{10,11... | collective-permute-start | bytes 49160 | tf_op jit(solution)/shard_map/ppermute | solution.py:153
  14.4 5.2 %collective-permute-start.4 = (f32[80,128]{1,0:T(8,128)S(1)}, f32[80,128]{1,0:T(8,128)S(1)}, u32[]{:S(2)}, u32[]{:S(2)}) collective-permute-start(f32[80,128]{1,0:T(8,128)S(1)} %shard_map.86), channel_id=1, source_target_pairs={{0,7},{1,2},{2,1},{3,4},{4,3},{5,6},{6,5},{7,0},{8,15},{9,10},{10,... | collective-permute-start | bytes 122888 | tf_op jit(solution)/shard_map/ppermute | solution.py:156
  20.1 6.6 %collective-permute-start.7 = (f32[272,128]{1,0:T(8,128)S(1)}, f32[272,128]{1,0:T(8,128)S(1)}, u32[]{:S(2)}, u32[]{:S(2)}) collective-permute-start(f32[272,128]{1,0:T(8,128)S(1)} %get-tuple-element.69.refs_3_), channel_id=1, source_target_pairs={{0,24},{8,0},{16,8},{24,16},{1,25},{9,1},{17,9},{25,17},{2,26},{10... | collective-permute-start | bytes 417800 | tf_op jit(solution)/shard_map/ppermute | solution.py:159
  21.7 9.5 %collective-permute-start.6 = (f32[272,128]{1,0:T(8,128)S(1)}, f32[272,128]{1,0:T(8,128)S(1)}, u32[]{:S(2)}, u32[]{:S(2)}) collective-permute-start(f32[272,128]{1,0:T(8,128)S(1)} %get-tuple-element.69.refs_3_), channel_id=1, source_target_pairs={{0,16},{8,24},{16,0},{24,8},{1,17},{9,25},{17,1},{25,9},{2,18},{10... | collective-permute-start | bytes 417800 | tf_op jit(solution)/shard_map/ppermute | solution.py:159
  22.2 9.0 %collective-permute-start.5 = (f32[272,128]{1,0:T(8,128)S(1)}, f32[272,128]{1,0:T(8,128)S(1)}, u32[]{:S(2)}, u32[]{:S(2)}) collective-permute-start(f32[272,128]{1,0:T(8,128)S(1)} %get-tuple-element.69.refs_3_), channel_id=1, source_target_pairs={{0,8},{8,16},{16,24},{24,0},{1,9},{9,17},{17,25},{25,1},{2,10},{10... | collective-permute-start | bytes 417800 | tf_op jit(solution)/shard_map/ppermute | solution.py:159
  23.7 8.0 %collective-permute-start.9 = (f32[256,128]{1,0:T(8,128)S(1)}, f32[256,128]{1,0:T(8,128)S(1)}, u32[]{:S(2)}, u32[]{:S(2)}) collective-permute-start(f32[256,128]{1,0:T(8,128)S(1)} %get-tuple-element.74), channel_id=1, source_target_pairs={{0,8},{8,16},{16,24},{24,0},{1,9},{9,17},{17,25},{25,1},{2,10},{10... | collective-permute-start | bytes 393224 | tf_op jit(solution)/shard_map/ppermute | solution.py:159
  31.8 1.2 %collective-permute-start.8 = (f32[32,128]{1,0:T(8,128)S(1)}, f32[32,128]{1,0:T(8,128)S(1)}, u32[]{:S(2)}, u32[]{:S(2)}) collective-permute-start(f32[32,128]{1,0:T(8,128)S(1)} %get-tuple-element.70), channel_id=1, source_target_pairs={{0,1},{1,0},{2,3},{3,2},{4,5},{5,4},{6,7},{7,6},{8,9},{9,8},{10,11... | collective-permute-start | bytes 49160 | tf_op jit(solution)/shard_map/ppermute | solution.py:153
  33.3 3.3 %collective-permute-start.10 = (f32[32,128]{1,0:T(8,128)S(1)}, f32[32,128]{1,0:T(8,128)S(1)}, u32[]{:S(2)}, u32[]{:S(2)}) collective-permute-start(f32[32,128]{1,0:T(8,128)S(1)} %get-tuple-element.78), channel_id=1, source_target_pairs={{0,1},{1,0},{2,3},{3,2},{4,5},{5,4},{6,7},{7,6},{8,9},{9,8},{10,11... | collective-permute-start | bytes 49160 | tf_op jit(solution)/shard_map/ppermute | solution.py:153
  33.8 5.0 %collective-permute-start.11 = (f32[32,128]{1,0:T(8,128)S(1)}, f32[32,128]{1,0:T(8,128)S(1)}, u32[]{:S(2)}, u32[]{:S(2)}) collective-permute-start(f32[32,128]{1,0:T(8,128)S(1)} %get-tuple-element.79), channel_id=1, source_target_pairs={{0,7},{1,2},{2,1},{3,4},{4,3},{5,6},{6,5},{7,0},{8,15},{9,10},{10,... | collective-permute-start | bytes 49160 | tf_op jit(solution)/shard_map/ppermute | solution.py:156

commit v4 on v3

--- a/solution.py
+++ b/solution.py
@@ -5,6 +5,7 @@
 from jax.experimental.pallas import tpu as pltpu
 from jax.sharding import PartitionSpec as P
 
+
 DAMPING = 0.7
 F32 = jnp.float32
 BF16 = jnp.bfloat16
@@ -15,7 +16,7 @@
 W_DIAG, W_FACE, W_SOURCE_TIME, W_TIME = 0, 1, 5, 6
 
 
-def call(kernel, out_shapes, args, spaces=None, scratch=(), flops=4e8):
+def call(kernel, out_shapes, args, spaces=None, scratch=(), flops=4e8, out_space=VMEM):
     spaces = spaces or [VMEM] * len(args)
     args = [
         pltpu.with_memory_space_constraint(x, HBM) if s is HBM else x for x, s in zip(args, spaces)
@@ -24,7 +25,7 @@
         kernel,
         out_shape=[jax.ShapeDtypeStruct(s, d) for s, d in out_shapes],
         in_specs=[pl.BlockSpec(memory_space=s) for s in spaces],
-        out_specs=[pl.BlockSpec(memory_space=VMEM)] * len(out_shapes),
+        out_specs=[pl.BlockSpec(memory_space=out_space)] * len(out_shapes),
         scratch_shapes=list(scratch),
         compiler_params=pltpu.CompilerParams(vmem_limit_bytes=24 << 20),
         cost_estimate=pl.CostEstimate(flops=int(flops), bytes_accessed=1 << 20, transcendentals=0),
@@ -158,6 +159,14 @@
     def later(x, by):
         return lax.ppermute(x, "tm", [(i, (i + by) % groups) for i in range(groups)])
 
+    def sent_faces(picks_ref, w_ref, parts, start):
+        near = None
+        for f in range(faces):
+            picked = dot(picks_ref[f * sent + start : (f + 1) * sent, :], parts).astype(BF16)
+            term = dot(picked, w_ref[W_FACE + f])
+            near = term if near is None else near + term
+        return halves(near)
+
     def sent_at(send_ref, i):
         first = jnp.where(lax.axis_index("space") % 2 == 0, halo, 0)
         return send_ref[0, lax.rem(first + i, sent)]
@@ -207,7 +216,7 @@
 
     def setup_kernel(
         xa_ref, xb_ref, scale_hbm, d_hbm, inv_hbm, f_hbm, t_hbm, nbr_hbm, send_hbm,
-        v_ref, part_ref, psent_ref, sigs_ref, fracs_ref, w_ref, pick_ref, picko_ref, q_ref, qs_ref,
+        v_ref, part_ref, psent_ref, sigs_ref, fracs_ref, w_ref, pick_ref, picks_ref, q_ref, qs_ref,
         qo_ref, sent_ref, sig_ref, frac_ref,
         scale_ref, d_ref, inv_ref, f_ref, t_ref, nbr_ref, send_ref, rows_ref, sems,
     ):
@@ -255,8 +264,8 @@
         qs = dot(chosen, q)
         qs_ref[...] = qs.astype(BF16)
         for f in range(faces):
-            picko_ref[f * halo : (f + 1) * halo, :] = dot(
-                chosen[halo:], pick_ref[f * elements : (f + 1) * elements, :]
+            picks_ref[f * sent : (f + 1) * sent, :] = dot(
+                chosen, pick_ref[f * elements : (f + 1) * elements, :]
             ).astype(BF16)
         head = weight_tile(inv)
         v = [product(split(x[...]), head) for x in (xa_ref, xb_ref)]
@@ -283,14 +292,14 @@
         qo_ref[...] = got[slabs + 1][halo:] * qs[halo:] * kept
 
     (
-        v0, part1, psent1, sig_sent, frac_sent, weights, pick, pick_o, q_all, q_sent, q_o, choose,
+        v0, part1, psent1, sig_sent, frac_sent, weights, pick, pick_sent, q_all, q_sent, q_o, choose,
         sigma_all, frac_all,
     ) = call(
         setup_kernel,
         [
             two, two, ((slabs * sent, width), F32), ((sent, width), F32), ((sent, width), F32),
             ((stack, 2 * width, 2 * width), BF16), ((faces * elements, elements), BF16),
-            ((faces * halo, elements), BF16), ((elements, far), BF16), ((sent, far), BF16),
+            ((faces * sent, elements), BF16), ((elements, far), BF16), ((sent, far), BF16),
             ((halo, far), F32), ((sent, elements), BF16), full, full,
         ],
         [
@@ -336,7 +345,7 @@
     re1 = over_e(e1)
 
     def ahead(
-        re_ref, ro_ref, b_ref, part_ref, vo_ref, o0_ref, w_ref, picko_ref, q_ref, sig_ref,
+        re_ref, ro_ref, b_ref, part_ref, vo_ref, o0_ref, w_ref, picks_ref, q_ref, sig_ref,
         sigs_ref, fracs_ref, v1_ref, wo_ref,
     ):
         sigma = sig_ref[...]
@@ -346,23 +355,19 @@
         vb = part_ref[elements:, :] + sigma * add[1]
         v1_ref[:elements, :] = va
         v1_ref[elements:, :] = vb
-        picked = dot(picko_ref[...], split(va + vb)).astype(BF16)
-        near = None
-        for f in range(faces):
-            term = dot(picked[f * halo : (f + 1) * halo], w_ref[W_FACE + f])
-            near = term if near is None else near + term
+        near = sent_faces(picks_ref, w_ref, split(va + vb), halo)
         sa, sb = vo_ref[:halo, :], vo_ref[halo:, :]
         rest = (
             o0_ref[:halo, :] + o0_ref[halo:, :] - DAMPING * product(split(sa + sb), w_ref[W_DIAG])
         ) / sigs_ref[halo:, :]
-        rest = rest + product(split(sa), w_ref[W_TIME]) + halves(near)
+        rest = rest + product(split(sa), w_ref[W_TIME]) + near
         wo_ref[...] = fracs_ref[halo:, :] * rest + sb
 
     v1, w_part = call(
         ahead,
         [two, ((halo, width), F32)],
         [
-            re0, ro0, before, part1, vo, o0, weights, pick_o, q_all, sigma_all, sig_sent,
+            re0, ro0, before, part1, vo, o0, weights, pick_sent, q_all, sigma_all, sig_sent,
             frac_sent,
         ],
         flops=2e8,
@@ -388,8 +393,15 @@
     )
     ro1 = over_o(o1)
 
+    def carry(v1_ref, v_ref, w_ref, sig_ref, x_ref):
+        step = split(v1_ref[:elements, :] - v1_ref[elements:, :])
+        x_ref[...] = v_ref[elements:, :] + sig_ref[...] * product(step, w_ref[W_TIME])
+
+    (x_own,) = call(carry, [full], [v1, v0, weights, sigma_all], flops=1e8)
+    x_before = later(x_own, 1)
+
     def middle(
-        v1_ref, v_ref, w_ref, pick_ref, sig_ref, frac_ref, pa_ref, pb_ref, wp_ref, x_ref
+        v1_ref, v_ref, w_ref, pick_ref, sig_ref, frac_ref, pa_ref, pb_ref, wp_ref
     ):
         sigma = sig_ref[...]
         frac = frac_ref[...]
@@ -398,27 +410,18 @@
         ca, cb = split(va), split(vb)
         ga, gb = own_faces(faces, pick_ref, w_ref, [ca, cb])
         da, db = product(ca, w_ref[W_DIAG]), product(cb, w_ref[W_DIAG])
-        ta, tb = product(ca, w_ref[W_TIME]), product(cb, w_ref[W_TIME])
+        ta = product(ca, w_ref[W_TIME])
         pa_ref[...] = va + v0a - DAMPING * da + sigma * ga
         pb_ref[...] = vb + v0b - DAMPING * db + sigma * (ta + gb)
         wp_ref[...] = (
             frac * (((v0a + v0b) - DAMPING * (da + db)) / sigma + ta + ga + gb) + vb
         )
-        x_ref[...] = v0b + sigma * (ta - tb)
-
-    pa0, pb0, wp, x_own = call(
-        middle,
-        [full] * 4,
-        [v1, v0, weights, pick, sigma_all, frac_all],
-        flops=1e9,
-    )
+
+    pa0, pb0, wp = call(middle, [full] * 3, [v1, v0, weights, pick, sigma_all, frac_all], flops=1e9)
 
     more = ((elements + halo, width), F32)
 
-    def coarse_kernel(
-        re_ref, ro_ref, vo_ref, wp_ref, pa_ref, pb_ref, w_ref, q_ref, sig_ref, frac_ref,
-        w_out, pa_out, pb_out,
-    ):
+    def coarse_kernel(re_ref, ro_ref, vo_ref, wp_ref, w_ref, q_ref, frac_ref, w_out, table_ref):
         rows = arrived(re_ref, ro_ref.at[: slabs * halo, :], slabs)
         both = vo_ref[:halo, :] + vo_ref[halo:, :]
         rows.append(jnp.concatenate([both, both], axis=0))
@@ -430,23 +433,38 @@
         w_out[elements:, :] = ro_ref[slabs * halo : (slabs + 1) * halo, :] + dot32(
             ro_ref[(slabs + 1) * halo : (slabs + 2) * halo, :], mine
         )
-        pa_out[...] = pa_ref[...] + sig_ref[...] * add[0]
-        pb_out[...] = pb_ref[...] + sig_ref[...] * add[1]
-
-    w_own, pa1, pb1 = call(
+        table_ref[...] = table[:, : slabs * lanes]
+
+    w_own, table1 = call(
         coarse_kernel,
-        [more, full, full],
-        [re1, ro1, vo, wp, pa0, pb0, weights, q_all, sigma_all, frac_all],
+        [more, ((far, slabs * 2 * width), BF16)],
+        [re1, ro1, vo, wp, weights, q_all, frac_all],
         flops=1e7,
     )
+
+    def rest_kernel(table_ref, pa_ref, pb_ref, q_ref, sig_ref, sent_ref, pa_out, pb_out, ps_out):
+        add = spread(q_ref[...], table_ref[...], slabs)
+        a = pa_ref[...] + sig_ref[...] * add[0]
+        b = pb_ref[...] + sig_ref[...] * add[1]
+        pa_out[...] = a
+        pb_out[...] = b
+        got = at_sent(sent_ref, [a, b])
+        ps_out[:sent, :] = got[0]
+        ps_out[sent:, :] = got[1]
+
+    pa1, pb1, psent2 = call(
+        rest_kernel,
+        [full, full, ((slabs * sent, width), F32)],
+        [table1, pa0, pb0, q_all, sigma_all, choose],
+        flops=1e8,
+    )
     earlier = [later(w_own, a) for a in range(1, groups)]
-    x_before = later(x_own, 1)
 
     def recur(*refs):
         olds = refs[: groups - 1]
-        w_own_ref, v1_ref, ro_ref, w_ref, sent_ref, frac_ref, c_ref, d_ref, e_ref, oh_ref = refs[
-            groups - 1 :
-        ]
+        w_own_ref, v1_ref, ro_ref, w_ref, sent_ref, frac_ref, c_ref, d_ref, s_ref, e_ref, oh_ref = (
+            refs[groups - 1 :]
+        )
         frac = jnp.concatenate([frac_ref[...], ro_ref[(slabs + 2) * halo :, :]], axis=0)
         v_last = jnp.concatenate(
             [v1_ref[(slabs - 1) * elements :, :], ro_ref[(slabs - 1) * halo : slabs * halo, :]],
@@ -467,69 +485,72 @@
         oh_ref[:halo, :] = c[elements:]
         oh_ref[halo:, :] = d[elements:]
         every = jnp.concatenate([split(c[:elements]), split(d[:elements])], axis=1)
-        got = spread(sent_ref[:halo, :], every, 2)
-        e_ref[:halo, :] = got[0]
-        e_ref[halo:, :] = got[1]
-
-    c_all, d_all, e2, ro2 = call(
+        got = spread(sent_ref[...], every, 2)
+        e_ref[:halo, :] = got[0][:halo]
+        e_ref[halo:, :] = got[1][:halo]
+        s_ref[:sent, :] = got[0]
+        s_ref[sent:, :] = got[1]
+
+    c_all, d_all, cd_sent, e2, ro2 = call(
         recur,
-        [full, full, edge, edge],
+        [full, full, ((2 * sent, width), F32), edge, edge],
         [*earlier, w_own, v1, ro1, weights, choose, frac_all],
         flops=1e8,
     )
     re2 = over_e(e2)
 
-    def second(
-        c_in, d_in, xb_ref, pa_ref, pb_ref, w_ref, pick_ref, sig_ref, sent_ref,
-        a_ref, b_ref, z_ref, ps_ref,
+    def ahead_two(c_ref, cds_ref, ps_ref, w_ref, picks_ref, sigs_ref, out_ref):
+        sigma = sigs_ref[...]
+        near = sent_faces(picks_ref, w_ref, split(c_ref[...]), 0)
+        c = cds_ref[:sent, :]
+        cut = split(c)
+        same = c - DAMPING * product(cut, w_ref[W_DIAG]) + sigma * near
+        out_ref[:sent, :] = ps_ref[:sent, :] + same + sigma * product(
+            split(cds_ref[sent:, :]), w_ref[W_TIME]
+        )
+        out_ref[sent:, :] = ps_ref[sent:, :] + same + sigma * product(cut, w_ref[W_TIME])
+
+    (psent3,) = call(
+        ahead_two,
+        [((slabs * sent, width), F32)],
+        [c_all, cd_sent, psent2, weights, pick_sent, sig_sent],
+        flops=1e8,
+    )
+
+    def edge_two(re_ref, ro_ref, psent_ref, sigs_ref, w_ref, qs_ref, e_ref, o_ref):
+        table = far_faces(faces, arrived(re_ref, ro_ref, 2)[:1], w_ref)
+        add = sigs_ref[...] * spread(qs_ref[...], table, 1)[0]
+        put_sent(
+            e_ref, o_ref, [psent_ref[t * sent : (t + 1) * sent, :] + add for t in range(slabs)]
+        )
+
+    e3, o3 = call(
+        edge_two,
+        [edge, edge],
+        [re2, ro2, psent3, sig_sent, weights, q_sent],
+        flops=1e7,
+    )
+    re3, ro3 = over_e(e3), over_o(o3)
+
+    def sweep(
+        re_ref, ro_ref, c_in, d_in, xb_ref, pa_ref, pb_ref, v_ref, w_ref, pick_ref, q_ref, sig_ref,
+        out_ref,
     ):
         sigma = sig_ref[...]
         c, d = c_in[...], d_in[...]
         cc, cd = split(c), split(d)
         gc, gd = own_faces(faces, pick_ref, w_ref, [cc, cd])
-        same = c - DAMPING * product(cc, w_ref[W_DIAG]) + sigma * gc
+        add = spread(q_ref[...], far_faces(faces, arrived(re_ref, ro_ref, 2), w_ref), 2)
+        same = c - DAMPING * product(cc, w_ref[W_DIAG]) + sigma * (gc + add[0])
         td = product(cd, w_ref[W_TIME])
         a = pa_ref[...] + same + sigma * td
         b = pb_ref[...] + same + sigma * product(cc, w_ref[W_TIME])
-        a_ref[...] = a
-        b_ref[...] = b
-        z_ref[...] = (
-            time_mask(xb_ref[...]) + d - DAMPING * product(cd, w_ref[W_DIAG]) + sigma * (td + gd)
-        )
-        got = at_sent(sent_ref, [a, b])
-        for t in range(slabs):
-            ps_ref[t * sent : (t + 1) * sent, :] = got[t]
-
-    a3, b3, z3, psent3 = call(
-        second,
-        [full, full, full, ((slabs * sent, width), F32)],
-        [c_all, d_all, x_before, pa1, pb1, weights, pick, sigma_all, choose],
-        flops=2e9,
-    )
-
-    def edge_two(re_ref, ro_ref, psent_ref, sigs_ref, w_ref, qs_ref, e_ref, o_ref):
-        table = far_faces(faces, arrived(re_ref, ro_ref, 2)[:1], w_ref)
-        add = sigs_ref[...] * spread(qs_ref[...], table, 1)[0]
-        put_sent(
-            e_ref, o_ref, [psent_ref[t * sent : (t + 1) * sent, :] + add for t in range(slabs)]
-        )
-
-    e3, o3 = call(
-        edge_two,
-        [edge, edge],
-        [re2, ro2, psent3, sig_sent, weights, q_sent],
-        flops=1e7,
-    )
-    re3, ro3 = over_e(e3), over_o(o3)
-
-    def third(
-        re_ref, ro_ref, a_in, b_in, z_in, v_ref, w_ref, pick_ref, q_ref, sig_ref, out_ref
-    ):
-        sigma = sig_ref[...]
-        add = spread(q_ref[...], far_faces(faces, arrived(re_ref, ro_ref, 2), w_ref), 2)
-        a = a_in[...] + sigma * add[0]
-        b = b_in[...] + sigma * add[0]
-        z = z_in[...] + sigma * add[1]
+        z = (
+            time_mask(xb_ref[...])
+            + d
+            - DAMPING * product(cd, w_ref[W_DIAG])
+            + sigma * (td + gd + add[1])
+        )
         ca, cb = split(a), split(b)
         ga, gb = own_faces(faces, pick_ref, w_ref, [ca, cb])
         tz, ta = product(split(z), w_ref[W_TIME]), product(ca, w_ref[W_TIME])
@@ -541,21 +562,36 @@
         )
 
     (part4,) = call(
-        third,
+        sweep,
         [two],
-        [re2, ro2, a3, b3, z3, v0, weights, pick, q_all, sigma_all],
+        [re2, ro2, c_all, d_all, x_before, pa1, pb1, v0, weights, pick, q_all, sigma_all],
         flops=2e9,
     )
 
-    def last(re_ref, ro_ref, p_ref, w_ref, q_ref, sig_ref, out_ref):
-        add = spread(q_ref[...], far_faces(faces, arrived(re_ref, ro_ref, slabs), w_ref), slabs)
+    def last(re_ref, ro_ref, p_ref, w_ref, q_ref, sig_ref, out_hbm, out_ref, sems):
+        table = far_faces(faces, arrived(re_ref, ro_ref, slabs), w_ref)
+        lanes = 2 * width
+        copies = []
         for t in range(slabs):
+            rows = pl.ds(t * elements, elements)
+            add = spread(q_ref[...], table[:, t * lanes : (t + 1) * lanes], 1)[0]
             out_ref[t * elements : (t + 1) * elements, :] = (
-                p_ref[t * elements : (t + 1) * elements, :] + sig_ref[...] * add[t]
+                p_ref[t * elements : (t + 1) * elements, :] + sig_ref[...] * add
             )
+            copies.append(
+                pltpu.make_async_copy(out_ref.at[rows, :], out_hbm.at[rows, :], sems.at[t])
+            )
+            copies[-1].start()
+        for c in copies:
+            c.wait()
 
     (out,) = call(
-        last, [two], [re3, ro3, part4, weights, q_all, sigma_all], flops=1e7
+        last,
+        [two],
+        [re3, ro3, part4, weights, q_all, sigma_all],
+        scratch=[VMEM((slabs * elements, width), F32), pltpu.SemaphoreType.DMA((slabs,))],
+        flops=1e7,
+        out_space=HBM,
     )
     return out.reshape(slabs, elements, width)
 

time: 40.1 us -> 38.1 us (0.950)
  starting transfers between devices: 14.4 us -> 13.1 us
  waiting for transfers between devices: 13.2 us -> 12 us
  Pallas kernels: 12.3 us -> 12.8 us
    ppermute x5, waiting for transfers between devices: 7.16 us -> 5.85 us  [later(): lax.ppermute(x, 'tm', [(i, (i + by) % groups) for i in range(groups)])]
    ppermute x5, starting transfers between devices: 6.58 us -> 6.04 us  [later(): lax.ppermute(x, 'tm', [(i, (i + by) % groups) for i in range(groups)])]
    pallas_call x12 -> x14, Pallas kernels: 12.3 us -> 12.8 us  [call(): pl.pallas_call(kernel, out_shape=[jax.ShapeDtypeStruct(s, d) for s, d in...]
    ppermute x3, starting transfers between devices: 6.63 us -> 6.19 us  [over_o(): return lax.ppermute(x, 'space', swap_o)]
  transfers between devices with their start and end apart: 12 -> 12, of which waited for: 6 -> 8; matrix products, arithmetic and copies ran while one was open for 0% -> 0% of each run, Pallas kernels for 21% -> 24%
where the time goes in v4:
time: 38.1 us; the launch traced here: 38 us
  starting transfers between devices  13.1 us (34%)
  Pallas kernels  12.8 us (34%)
  waiting for transfers between devices  12 us (31%)
    pallas_call x14, Pallas kernels, call(): pl.pallas_call(kernel, out_shape=[jax.ShapeDtypeStruct(s, d) for s, d in...  12.8 us
    ppermute x3, starting transfers between devices, over_o(): return lax.ppermute(x, 'space', swap_o)  6.19 us
    ppermute x5, starting transfers between devices, later(): lax.ppermute(x, 'tm', [(i, (i + by) % groups) for i in range(groups)])  6.04 us
    ppermute x5, waiting for transfers between devices, later(): lax.ppermute(x, 'tm', [(i, (i + by) % groups) for i in range(groups)])  5.85 us
    ppermute x3, waiting for transfers between devices, over_o(): return lax.ppermute(x, 'space', swap_o)  5.37 us
    ppermute x4, starting transfers between devices, over_e(): return lax.ppermute(x, 'space', swap_e)  0.87 us
  transfers between devices with their start and end apart: 12, of which 8 were waited for; matrix products, arithmetic and copies ran while one was open for 0% of the time, Pallas kernels for 24%

profile of v4, /device:TPU:0, one launch (start us, length us, event | category | flops | bytes accessed | tf_op | source)
XLA Modules:
  0.0 38.0 jit_solution(9383384619136906454)
XLA Ops:
  0.0 1.3 %shard_map.82 = (f32[32,128]{1,0:T(8,128)S(1)}, f32[32,128]{1,0:T(8,128)S(1)}, f32[256,128]{1,0:T(8,128)S(1)}, f32[256,128]{1,0:T(8,128)S(1)}) custom-call(f32[512,128]{1,0:T(8,128)} %bitcast.4, f32[1,256]{1,0:T(1,128)} %bitcast.5, f32[128,128]{1,0:T(8,128)} %inv_hbm.3, s32[1,32]{1,0:T(1,128)} %send_hbm.3), custom_call_target="tpu_custom_call" | custom-call | flops 10000000 | bytes 1048576 | tf_op jit(solution)/shard_map/pallas_call | solution.py:24
  1.3 0.6 %collective-permute-start = (f32[32,128]{1,0:T(8,128)S(1)}, f32[32,128]{1,0:T(8,128)S(1)}, u32[]{:S(2)}, u32[]{:S(2)}) collective-permute-start(f32[32,128]{1,0:T(8,128)S(1)} %get-tuple-element.42), channel_id=1, source_target_pairs={{0,1},{1,0},{2,3},{3,2},{4,5},{5,4},{6,7},{7,6},{8,9},{9,8},{10,11... | collective-permute-start | bytes 49160 | tf_op jit(solution)/shard_map/ppermute | solution.py:154
  1.8 4.7 %collective-permute-start.1 = (f32[32,128]{1,0:T(8,128)S(1)}, f32[32,128]{1,0:T(8,128)S(1)}, u32[]{:S(2)}, u32[]{:S(2)}) collective-permute-start(f32[32,128]{1,0:T(8,128)S(1)} %get-tuple-element.43.o0_ref), channel_id=1, source_target_pairs={{0,7},{1,2},{2,1},{3,4},{4,3},{5,6},{6,5},{7,0},{8,15},{9,10},{10,... | collective-permute-start | bytes 49160 | tf_op jit(solution)/shard_map/ppermute | solution.py:157
  6.5 1.5 %collective-permute-start.2 = (f32[256,128]{1,0:T(8,128)S(1)}, f32[256,128]{1,0:T(8,128)S(1)}, u32[]{:S(2)}, u32[]{:S(2)}) collective-permute-start(f32[256,128]{1,0:T(8,128)S(1)} %get-tuple-element.44.xb_ref), channel_id=1, source_target_pairs={{0,8},{8,16},{16,24},{24,0},{1,9},{9,17},{17,25},{25,1},{2,10},{10... | collective-permute-start | bytes 393224 | tf_op jit(solution)/shard_map/ppermute | solution.py:160
  8.0 3.2 %shard_map.83 = (f32[512,128]{1,0:T(8,128)S(1)}, f32[512,128]{1,0:T(8,128)S(1)}, f32[64,128]{1,0:T(8,128)S(1)}, f32[32,128]{1,0:T(8,128)S(1)}, f32[32,128]{1,0:T...) custom-call(f32[256,128]{1,0:T(8,128)S(1)} %get-tuple-element.45.xa_, ...), custom_call_target="tpu_custom_call" | custom-call | flops 2000000000 | bytes 1048576 | tf_op jit(solution)/shard_map/pallas_call | solution.py:24
  11.2 0.0 collective-permute-done.re_ref
  11.2 0.0 collective-permute-done.1.ro_ref
  11.2 1.2 %collective-permute-done.2.b_ref = f32[256,128]{1,0:T(8,128)S(1)} collective-permute-done((f32[256,128]{1,0:T(8,128)S(1)}, f32[256,128]{1,0:T(8,128)S(1)}, u32[]{:S(2)}, u32[]{:S(2)}) %collective-permute-start.2) | collective-permute-done | bytes 131104 | tf_op jit(solution)/shard_map/ppermute | solution.py:160
  12.4 0.5 %shard_map.84 = (f32[32,128]{1,0:T(8,128)S(1)}, f32[32,128]{1,0:T(8,128)S(1)}) custom-call(f32[32,128]{1,0:T(8,128)S(1)} %collective-permute-done.re_ref, f32[32,128]{1,0:T(8,128)S(1)} %collective-permute-done.1.ro_ref, f32[256,128]{1,0:T(8,128)S(1)} %collective-permute-done.2.b_ref, f32[64,128]{1,0:T(8,128)S(1)} %get-tuple-element.46.psent_ref, ...), custom_call_target="tpu_custom_call" | custom-call | flops 10000000 | bytes 1048576 | tf_op jit(solution)/shard_map/pallas_call | solution.py:24
  12.9 0.1 collective-permute-start.3
  13.0 0.8 %shard_map.85 = (f32[512,128]{1,0:T(8,128)S(1)}, f32[16,128]{1,0:T(8,128)S(1)}) custom-call(f32[32,128]{1,0:T(8,128)S(1)} %collective-permute-done.re_ref, f32[32,128]{1,0:T(8,128)S(1)} %collective-permute-done.1.ro_ref, f32[256,128]{1,0:T(8,128)S(1)} %collective-permute-done.2.b_ref, f32[512,128]{1,0:T(8,128)S(1)} %get-tuple-element.52.part_ref, ...), custom_call_target="tpu_custom_call" | custom-call | flops 200000000 | bytes 1048576 | tf_op jit(solution)/shard_map/pallas_call | solution.py:24
  13.8 0.3 collective-permute-done.3.re_ref
  14.1 0.3 shard_map.86
  14.4 0.6 %collective-permute-start.4 = (f32[80,128]{1,0:T(8,128)S(1)}, f32[80,128]{1,0:T(8,128)S(1)}, u32[]{:S(2)}, u32[]{:S(2)}) collective-permute-start(f32[80,128]{1,0:T(8,128)S(1)} %shard_map.86), channel_id=1, source_target_pairs={{0,7},{1,2},{2,1},{3,4},{4,3},{5,6},{6,5},{7,0},{8,15},{9,10},{10,... | collective-permute-start | bytes 122888 | tf_op jit(solution)/shard_map/ppermute | solution.py:157
  15.1 1.0 %shard_map.87 = (f32[256,128]{1,0:T(8,128)S(1)}, f32[256,128]{1,0:T(8,128)S(1)}, f32[256,128]{1,0:T(8,128)S(1)}) custom-call(f32[512,128]{1,0:T(8,128)S(1)} %get-tuple-element.60.v1_ref.refs_4_, f32[512,128]{1,0:T(8,128)S(1)} %get-tuple-element.61.v_ref, bf16[9,256,256]{2,1,0:T(8,128)(2,1)S(1)} %get-tuple-element.48.w_ref.refs_6_, ...), custom_call_target="tpu_custom_call" | custom-call | flops 1000000000 | bytes 1048576 | tf_op jit(solution)/shard_map/pallas_call | solution.py:24
  16.1 3.6 %collective-permute-done.4.ro_ref.refs_5_ = f32[80,128]{1,0:T(8,128)S(1)} collective-permute-done((f32[80,128]{1,0:T(8,128)S(1)}, f32[80,128]{1,0:T(8,128)S(1)}, u32[]{:S(2)}, u32[]{:S(2)}) %collective-permute-start.4) | collective-permute-done | bytes 40992 | tf_op jit(solution)/shard_map/ppermute | solution.py:157
  19.7 0.4 %shard_map.88 = (f32[272,128]{1,0:T(8,128)S(1)}, bf16[128,512]{1,0:T(8,128)(2,1)S(1)}) custom-call(f32[32,128]{1,0:T(8,128)S(1)} %collective-permute-done.3.re_ref, f32[80,128]{1,0:T(8,128)S(1)} %collective-permute-done.4.ro_ref.refs_5_, f32[32,128]{1,0:T(8,128)S(1)} %get-tuple-element.53.vo_ref, f32[256,128]{1,0:T(8,128)S(1)} %get-tuple-element.64.wp_ref, ...), custom_call_target="tpu_custom_call" | custom-call | flops 10000000 | bytes 1048576 | tf_op jit(solution)/shard_map/pallas_call | solution.py:24
  20.1 0.6 %collective-permute-start.5 = (f32[272,128]{1,0:T(8,128)S(1)}, f32[272,128]{1,0:T(8,128)S(1)}, u32[]{:S(2)}, u32[]{:S(2)}) collective-permute-start(f32[272,128]{1,0:T(8,128)S(1)} %get-tuple-element.65.refs_3_), channel_id=1, source_target_pairs={{0,8},{8,16},{16,24},{24,0},{1,9},{9,17},{17,25},{25,1},{2,10},{10... | collective-permute-start | bytes 417800 | tf_op jit(solution)/shard_map/ppermute | solution.py:160
  20.8 1.5 %collective-permute-start.6 = (f32[272,128]{1,0:T(8,128)S(1)}, f32[272,128]{1,0:T(8,128)S(1)}, u32[]{:S(2)}, u32[]{:S(2)}) collective-permute-start(f32[272,128]{1,0:T(8,128)S(1)} %get-tuple-element.65.refs_3_), channel_id=1, source_target_pairs={{0,16},{8,24},{16,0},{24,8},{1,17},{9,25},{17,1},{25,9},{2,18},{10... | collective-permute-start | bytes 417800 | tf_op jit(solution)/shard_map/ppermute | solution.py:160
  22.3 2.3 %collective-permute-start.7 = (f32[272,128]{1,0:T(8,128)S(1)}, f32[272,128]{1,0:T(8,128)S(1)}, u32[]{:S(2)}, u32[]{:S(2)}) collective-permute-start(f32[272,128]{1,0:T(8,128)S(1)} %get-tuple-element.65.refs_3_), channel_id=1, source_target_pairs={{0,24},{8,0},{16,8},{24,16},{1,25},{9,1},{17,9},{25,17},{2,26},{10... | collective-permute-start | bytes 417800 | tf_op jit(solution)/shard_map/ppermute | solution.py:160
  24.6 0.2 shard_map.93
  24.8 0.1 collective-permute-start.11
  24.9 2.5 %collective-permute-done.5.refs_0_ = f32[272,128]{1,0:T(8,128)S(1)} collective-permute-done((f32[272,128]{1,0:T(8,128)S(1)}, f32[272,128]{1,0:T(8,128)S(1)}, u32[]{:S(2)}, u32[]{:S(2)}) %collective-permute-start.5) | collective-permute-done | bytes 139296 | tf_op jit(solution)/shard_map/ppermute | solution.py:160
  27.4 1.5 %collective-permute-done.6.refs_1_ = f32[272,128]{1,0:T(8,128)S(1)} collective-permute-done((f32[272,128]{1,0:T(8,128)S(1)}, f32[272,128]{1,0:T(8,128)S(1)}, u32[]{:S(2)}, u32[]{:S(2)}) %collective-permute-start.6) | collective-permute-done | bytes 139296 | tf_op jit(solution)/shard_map/ppermute | solution.py:160
  28.9 0.7 %collective-permute-done.7.refs_2_ = f32[272,128]{1,0:T(8,128)S(1)} collective-permute-done((f32[272,128]{1,0:T(8,128)S(1)}, f32[272,128]{1,0:T(8,128)S(1)}, u32[]{:S(2)}, u32[]{:S(2)}) %collective-permute-start.7) | collective-permute-done | bytes 139296 | tf_op jit(solution)/shard_map/ppermute | solution.py:160
  29.6 0.5 %shard_map.89 = (f32[256,128]{1,0:T(8,128)S(1)}, f32[256,128]{1,0:T(8,128)S(1)}, f32[64,128]{1,0:T(8,128)S(1)}, f32[32,128]{1,0:T(8,128)S(1)}, f32[32,128]{1,0:T(8,128)S(1)}) custom-call(f32[272,128]{1,0:T(8,128)S(1)} %collective-permute-done.5.refs_0_, f32[272,128]{1,0:T(8,128)S(1)} %collective-permute-done.6.refs_1_, ...), custom_call_target="tpu_custom_call" | custom-call | flops 100000000 | bytes 1048576 | tf_op jit(solution)/shard_map/pallas_call | solution.py:24
  30.1 0.1 collective-permute-start.8
  30.2 0.3 shard_map.90
  30.5 0.4 %shard_map.91.psent_ref = f32[64,128]{1,0:T(8,128)S(1)} custom-call(f32[256,128]{1,0:T(8,128)S(1)} %get-tuple-element.68.c_ref.c_in, f32[64,128]{1,0:T(8,128)S(1)} %get-tuple-element.69.cds_ref, f32[64,128]{1,0:T(8,128)S(1)} %get-tuple-element.73.ps_ref, bf16[9,256,256]{2,1,0:T(8,128)(2,1)S(1)} %get-tuple-element.48.w_ref.refs_6_, ...), custom_call_target="tpu_custom_call" | custom-call | flops 100000000 | bytes 1048576 | tf_op jit(solution)/shard_map/pallas_call | solution.py:24
  30.9 0.4 %collective-permute-done.8.re_ref = f32[32,128]{1,0:T(8,128)S(1)} collective-permute-done((f32[32,128]{1,0:T(8,128)S(1)}, f32[32,128]{1,0:T(8,128)S(1)}, u32[]{:S(2)}, u32[]{:S(2)}) %collective-permute-start.8) | collective-permute-done | bytes 16416 | tf_op jit(solution)/shard_map/ppermute | solution.py:154
  31.4 0.3 shard_map.92
  31.7 0.2 collective-permute-start.9
  31.9 0.9 %collective-permute-start.10 = (f32[32,128]{1,0:T(8,128)S(1)}, f32[32,128]{1,0:T(8,128)S(1)}, u32[]{:S(2)}, u32[]{:S(2)}) collective-permute-start(f32[32,128]{1,0:T(8,128)S(1)} %get-tuple-element.75), channel_id=1, source_target_pairs={{0,7},{1,2},{2,1},{3,4},{4,3},{5,6},{6,5},{7,0},{8,15},{9,10},{10,... | collective-permute-start | bytes 49160 | tf_op jit(solution)/shard_map/ppermute | solution.py:157
  32.7 0.0 collective-permute-done.11.xb_ref
  32.7 2.3 %shard_map.94.p_ref = f32[512,128]{1,0:T(8,128)S(1)} custom-call(f32[32,128]{1,0:T(8,128)S(1)} %collective-permute-done.8.re_ref, f32[32,128]{1,0:T(8,128)S(1)} %get-tuple-element.67.ro_ref, f32[256,128]{1,0:T(8,128)S(1)} %get-tuple-element.68.c_ref.c_in, f32[256,128]{1,0:T(8,128)S(1)} %get-tuple-element.76.d_in, ...), custom_call_target="tpu_custom_call" | custom-call | flops 2000000000 | bytes 1048576 | tf_op jit(solution)/shard_map/pallas_call | solution.py:24
  35.0 0.0 collective-permute-done.9.re_ref
  35.1 1.8 %collective-permute-done.10.ro_ref = f32[32,128]{1,0:T(8,128)S(1)} collective-permute-done((f32[32,128]{1,0:T(8,128)S(1)}, f32[32,128]{1,0:T(8,128)S(1)}, u32[]{:S(2)}, u32[]{:S(2)}) %collective-permute-start.10) | collective-permute-done | bytes 16416 | tf_op jit(solution)/shard_map/ppermute | solution.py:157
  36.8 1.1 %shard_map.95 = f32[512,128]{1,0:T(8,128)} custom-call(f32[32,128]{1,0:T(8,128)S(1)} %collective-permute-done.9.re_ref, f32[32,128]{1,0:T(8,128)S(1)} %collective-permute-done.10.ro_ref, f32[512,128]{1,0:T(8,128)S(1)} %shard_map.94.p_ref, bf16[9,256,256]{2,1,0:T(8,128)(2,1)S(1)} %get-tuple-element.48.w_ref.refs_6_, ...), custom_call_target="tpu_custom_call" | custom-call | flops 10000000 | bytes 1048576 | tf_op jit(solution)/shard_map/pallas_call | solution.py:24
Async XLA Ops:
  1.3 10.0 %collective-permute-start = (f32[32,128]{1,0:T(8,128)S(1)}, f32[32,128]{1,0:T(8,128)S(1)}, u32[]{:S(2)}, u32[]{:S(2)}) collective-permute-start(f32[32,128]{1,0:T(8,128)S(1)} %get-tuple-element.42), channel_id=1, source_target_pairs={{0,1},{1,0},{2,3},{3,2},{4,5},{5,4},{6,7},{7,6},{8,9},{9,8},{10,11... | collective-permute-start | bytes 49160 | tf_op jit(solution)/shard_map/ppermute | solution.py:154
  1.8 9.4 %collective-permute-start.1 = (f32[32,128]{1,0:T(8,128)S(1)}, f32[32,128]{1,0:T(8,128)S(1)}, u32[]{:S(2)}, u32[]{:S(2)}) collective-permute-start(f32[32,128]{1,0:T(8,128)S(1)} %get-tuple-element.43.o0_ref), channel_id=1, source_target_pairs={{0,7},{1,2},{2,1},{3,4},{4,3},{5,6},{6,5},{7,0},{8,15},{9,10},{10,... | collective-permute-start | bytes 49160 | tf_op jit(solution)/shard_map/ppermute | solution.py:157
  6.5 5.9 %collective-permute-start.2 = (f32[256,128]{1,0:T(8,128)S(1)}, f32[256,128]{1,0:T(8,128)S(1)}, u32[]{:S(2)}, u32[]{:S(2)}) collective-permute-start(f32[256,128]{1,0:T(8,128)S(1)} %get-tuple-element.44.xb_ref), channel_id=1, source_target_pairs={{0,8},{8,16},{16,24},{24,0},{1,9},{9,17},{17,25},{25,1},{2,10},{10... | collective-permute-start | bytes 393224 | tf_op jit(solution)/shard_map/ppermute | solution.py:160
  12.9 1.2 %collective-permute-start.3 = (f32[32,128]{1,0:T(8,128)S(1)}, f32[32,128]{1,0:T(8,128)S(1)}, u32[]{:S(2)}, u32[]{:S(2)}) collective-permute-start(f32[32,128]{1,0:T(8,128)S(1)} %get-tuple-element.51), channel_id=1, source_target_pairs={{0,1},{1,0},{2,3},{3,2},{4,5},{5,4},{6,7},{7,6},{8,9},{9,8},{10,11... | collective-permute-start | bytes 49160 | tf_op jit(solution)/shard_map/ppermute | solution.py:154
  14.4 5.2 %collective-permute-start.4 = (f32[80,128]{1,0:T(8,128)S(1)}, f32[80,128]{1,0:T(8,128)S(1)}, u32[]{:S(2)}, u32[]{:S(2)}) collective-permute-start(f32[80,128]{1,0:T(8,128)S(1)} %shard_map.86), channel_id=1, source_target_pairs={{0,7},{1,2},{2,1},{3,4},{4,3},{5,6},{6,5},{7,0},{8,15},{9,10},{10,... | collective-permute-start | bytes 122888 | tf_op jit(solution)/shard_map/ppermute | solution.py:157
  20.1 7.2 %collective-permute-start.5 = (f32[272,128]{1,0:T(8,128)S(1)}, f32[272,128]{1,0:T(8,128)S(1)}, u32[]{:S(2)}, u32[]{:S(2)}) collective-permute-start(f32[272,128]{1,0:T(8,128)S(1)} %get-tuple-element.65.refs_3_), channel_id=1, source_target_pairs={{0,8},{8,16},{16,24},{24,0},{1,9},{9,17},{17,25},{25,1},{2,10},{10... | collective-permute-start | bytes 417800 | tf_op jit(solution)/shard_map/ppermute | solution.py:160
  20.8 8.1 %collective-permute-start.6 = (f32[272,128]{1,0:T(8,128)S(1)}, f32[272,128]{1,0:T(8,128)S(1)}, u32[]{:S(2)}, u32[]{:S(2)}) collective-permute-start(f32[272,128]{1,0:T(8,128)S(1)} %get-tuple-element.65.refs_3_), channel_id=1, source_target_pairs={{0,16},{8,24},{16,0},{24,8},{1,17},{9,25},{17,1},{25,9},{2,18},{10... | collective-permute-start | bytes 417800 | tf_op jit(solution)/shard_map/ppermute | solution.py:160
  22.3 7.3 %collective-permute-start.7 = (f32[272,128]{1,0:T(8,128)S(1)}, f32[272,128]{1,0:T(8,128)S(1)}, u32[]{:S(2)}, u32[]{:S(2)}) collective-permute-start(f32[272,128]{1,0:T(8,128)S(1)} %get-tuple-element.65.refs_3_), channel_id=1, source_target_pairs={{0,24},{8,0},{16,8},{24,16},{1,25},{9,1},{17,9},{25,17},{2,26},{10... | collective-permute-start | bytes 417800 | tf_op jit(solution)/shard_map/ppermute | solution.py:160
  24.8 7.9 %collective-permute-start.11 = (f32[256,128]{1,0:T(8,128)S(1)}, f32[256,128]{1,0:T(8,128)S(1)}, u32[]{:S(2)}, u32[]{:S(2)}) collective-permute-start(f32[256,128]{1,0:T(8,128)S(1)} %shard_map.93), channel_id=1, source_target_pairs={{0,8},{8,16},{16,24},{24,0},{1,9},{9,17},{17,25},{25,1},{2,10},{10... | collective-permute-start | bytes 393224 | tf_op jit(solution)/shard_map/ppermute | solution.py:160
  30.1 1.2 %collective-permute-start.8 = (f32[32,128]{1,0:T(8,128)S(1)}, f32[32,128]{1,0:T(8,128)S(1)}, u32[]{:S(2)}, u32[]{:S(2)}) collective-permute-start(f32[32,128]{1,0:T(8,128)S(1)} %get-tuple-element.66), channel_id=1, source_target_pairs={{0,1},{1,0},{2,3},{3,2},{4,5},{5,4},{6,7},{7,6},{8,9},{9,8},{10,11... | collective-permute-start | bytes 49160 | tf_op jit(solution)/shard_map/ppermute | solution.py:154
  31.7 3.4 %collective-permute-start.9 = (f32[32,128]{1,0:T(8,128)S(1)}, f32[32,128]{1,0:T(8,128)S(1)}, u32[]{:S(2)}, u32[]{:S(2)}) collective-permute-start(f32[32,128]{1,0:T(8,128)S(1)} %get-tuple-element.74), channel_id=1, source_target_pairs={{0,1},{1,0},{2,3},{3,2},{4,5},{5,4},{6,7},{7,6},{8,9},{9,8},{10,11... | collective-permute-start | bytes 49160 | tf_op jit(solution)/shard_map/ppermute | solution.py:154
  31.9 5.0 %collective-permute-start.10 = (f32[32,128]{1,0:T(8,128)S(1)}, f32[32,128]{1,0:T(8,128)S(1)}, u32[]{:S(2)}, u32[]{:S(2)}) collective-permute-start(f32[32,128]{1,0:T(8,128)S(1)} %get-tuple-element.75), channel_id=1, source_target_pairs={{0,7},{1,2},{2,1},{3,4},{4,3},{5,6},{6,5},{7,0},{8,15},{9,10},{10,... | collective-permute-start | bytes 49160 | tf_op jit(solution)/shard_map/ppermute | solution.py:157

commit v5 on v4

--- a/solution.py
+++ b/solution.py
@@ -62,6 +62,13 @@
     return halves(dot(parts, tile))
 
 
+def few(x, tile):
+    head = x.astype(BF16)
+    tail = (x - head.astype(F32)).astype(BF16)
+    out = halves(dot(jnp.concatenate([head, tail], axis=0), tile[: x.shape[1], :]))
+    return out[: x.shape[0]] + out[x.shape[0] :]
+
+
 def weight_tile(w):
     head = w.astype(BF16)
     tail = (w - head.astype(F32)).astype(BF16)
@@ -102,8 +109,8 @@
 def far_faces(faces, rows_in, weights_ref):
     count = len(rows_in)
     n = rows_in[0].shape[0]
-    parts = split(jnp.concatenate(rows_in, axis=0) if count > 1 else rows_in[0])
-    per_face = [product(parts, weights_ref[W_FACE + f]) for f in range(faces)]
+    rows = jnp.concatenate(rows_in, axis=0) if count > 1 else rows_in[0]
+    per_face = [few(rows, weights_ref.at[W_FACE + f]) for f in range(faces)]
     lanes = [
         split(jnp.concatenate([u[i * n : (i + 1) * n] for u in per_face], axis=0))
         for i in range(count)
@@ -171,18 +178,31 @@
         first = jnp.where(lax.axis_index("space") % 2 == 0, halo, 0)
         return send_ref[0, lax.rem(first + i, sent)]
 
+    pieces = 2
+    piece = elements // pieces
+
     def first_kernel(
-        s_hbm, scale_hbm, inv_hbm, send_hbm, e_ref, o_ref, xa_ref, xb_ref,
-        s_ref, scale_ref, inv_ref, send_ref, g_ref, sems,
+        s_hbm, scale_hbm, inv_hbm, send_hbm, d_hbm, f_hbm, t_hbm, nbr_hbm,
+        e_ref, o_ref, xa_ref, xb_ref, col_ref, inv_ref, fold_ref, nbr_ref,
+        s_ref, scale_ref, send_ref, g_ref, sems,
     ):
-        copies = fetch(
-            [(scale_hbm, scale_ref), (send_hbm, send_ref), (s_hbm, s_ref), (inv_hbm, inv_ref)],
-            sems,
-        )
+        parts = [pl.ds(i * piece, piece) for i in range(slabs * pieces)]
+        pairs = [(scale_hbm, scale_ref), (send_hbm, send_ref)]
+        pairs += [(s_hbm.at[p, :], s_ref.at[p, :]) for p in parts]
+        pairs += [
+            (inv_hbm, inv_ref),
+            (d_hbm, fold_ref.at[:width, :]),
+            (f_hbm, fold_ref.at[width : (faces + 1) * width, :]),
+            (t_hbm, fold_ref.at[(faces + 1) * width :, :]),
+            (nbr_hbm, nbr_ref),
+        ]
+        copies = fetch(pairs, sems)
         copies[0].wait()
-        sigma = DAMPING / column(scale_ref[...], width)
-        copies[1].wait()
-        copies[2].wait()
+        scale = column(scale_ref[...], width)
+        col_ref[...] = scale
+        sigma = DAMPING / scale
+        for c in copies[1 : 2 + slabs * pieces]:
+            c.wait()
         refs = [xa_ref, xb_ref]
         for t in range(slabs):
             refs[t][...] = s_ref[t * elements : (t + 1) * elements, :] * sigma
@@ -191,23 +211,30 @@
             base = (i // halo) * slabs * halo + i % halo
             for t in range(slabs):
                 g_ref[base + t * halo : base + t * halo + 1, :] = refs[t][pl.ds(at, 1), :]
-        copies[3].wait()
+        copies[2 + slabs * pieces].wait()
         out = dot32(g_ref[...], inv_ref[...])
         e_ref[...] = out[: slabs * halo]
         o_ref[...] = out[slabs * halo :]
-
-    e0, o0, xa, xb = call(
+        for c in copies[3 + slabs * pieces :]:
+            c.wait()
+
+    e0, o0, xa, xb, scale_col, inv_here, fold, faces_here = call(
         first_kernel,
-        [edge, edge, full, full],
-        [flat, scale_row, block_inverse, send_rows],
-        spaces=[HBM] * 4,
+        [
+            edge, edge, full, full, full, ((width, width), F32),
+            (((faces + 2) * width, width), F32), ((faces, elements), jnp.int32),
+        ],
+        [
+            flat, scale_row, block_inverse, send_rows, diag_block,
+            face_flux.reshape(faces * width, width), time_trace, faces_row,
+        ],
+        spaces=[HBM] * 8,
         scratch=[
             VMEM((slabs * elements, width), F32),
             VMEM((1, elements), F32),
-            VMEM((width, width), F32),
             SMEM((1, sent), jnp.int32),
             VMEM((slabs * sent, width), F32),
-            pltpu.SemaphoreType.DMA((4,)),
+            pltpu.SemaphoreType.DMA((slabs * pieces + 7,)),
         ],
         flops=1e7,
     )
@@ -215,48 +242,52 @@
     re0, ro0 = over_e(e0), over_o(o0)
 
     def setup_kernel(
-        xa_ref, xb_ref, scale_hbm, d_hbm, inv_hbm, f_hbm, t_hbm, nbr_hbm, send_hbm,
+        xa_ref, xb_ref, col_ref, inv_ref, fold_ref, nbr_ref, send_hbm,
         v_ref, part_ref, psent_ref, sigs_ref, fracs_ref, w_ref, pick_ref, picks_ref, q_ref, qs_ref,
-        qo_ref, sent_ref, sig_ref, frac_ref,
-        scale_ref, d_ref, inv_ref, f_ref, t_ref, nbr_ref, send_ref, rows_ref, sems,
+        qo_ref, sent_ref, back_ref, sig_ref, frac_ref,
+        send_ref, line_ref, rows_ref, sems,
     ):
-        copies = fetch(
-            [
-                (inv_hbm, inv_ref), (t_hbm, t_ref), (d_hbm, d_ref), (f_hbm, f_ref),
-                (scale_hbm, scale_ref), (nbr_hbm, nbr_ref), (send_hbm, send_ref),
-            ],
-            sems,
-        )
-        for c in copies:
-            c.wait()
-        inv = inv_ref[...]
-        trace = dot32(t_ref[...], inv)
-        w_ref[W_DIAG] = weight_tile(dot32(d_ref[...], inv))
-        for f in range(faces):
-            w_ref[W_FACE + f] = weight_tile(dot32(f_ref[f], inv))
-        w_ref[W_SOURCE_TIME] = weight_tile(dot32(inv, trace))
+        copies = fetch([(send_hbm, send_ref), (send_hbm, line_ref)], sems)
+        head = weight_tile(inv_ref[...])
+        folded = product(split(fold_ref[...]), head)
+        for i in range(faces + 1):
+            w_ref[W_DIAG + i] = weight_tile(folded[i * width : (i + 1) * width])
+        trace = folded[(faces + 1) * width :]
+        step = weight_tile(trace)
+        w_ref[W_TIME] = step
         power = trace
-        for a in range(groups - 1):
+        for a in range(1, groups - 1):
+            if a == 1:
+                both = product(split(jnp.concatenate([inv_ref[...], trace], axis=0)), step)
+                w_ref[W_SOURCE_TIME] = weight_tile(both[:width])
+                power = both[width:]
+            else:
+                power = product(split(power), step)
             w_ref[W_TIME + a] = weight_tile(power)
-            if a < groups - 2:
-                power = dot32(power, trace)
-        scale = column(scale_ref[...], width)
+        if groups < 3:
+            w_ref[W_SOURCE_TIME] = weight_tile(product(split(inv_ref[...]), step))
+        scale = col_ref[...]
         sigma = DAMPING / scale
         sig_ref[...] = sigma
         frac = 1.0 / (2.0 * scale - 1.0)
         frac_ref[...] = frac
-        lane = lax.broadcasted_iota(jnp.int32, (elements, elements), 1)
+        lane = lax.broadcasted_iota(jnp.int32, (elements, far), 1)
         spot = lax.broadcasted_iota(jnp.int32, (elements, far), 1)
         wanted = jnp.zeros((elements, far), jnp.int32)
         for f in range(faces):
-            wide = column(nbr_ref[f : f + 1, :], elements)
-            pick_ref[f * elements : (f + 1) * elements, :] = jnp.where(
-                wide == lane, 1.0, 0.0
-            ).astype(BF16)
-            wanted = jnp.where(spot // sent == f, column(nbr_ref[f : f + 1, :], far), wanted)
+            wide = column(nbr_ref[f : f + 1, :], far)
+            for base in range(0, elements, far):
+                pick_ref[f * elements : (f + 1) * elements, base : base + far] = jnp.where(
+                    wide == lane + base, 1.0, 0.0
+                ).astype(BF16)
+            wanted = jnp.where(spot // sent == f, wide, wanted)
         q = jnp.where(wanted == elements + spot % sent, 1.0, 0.0).astype(BF16)
         q_ref[...] = q
         strip = lax.broadcasted_iota(jnp.int32, (1, elements), 1)
+        for c in copies:
+            c.wait()
+        row = lax.broadcasted_iota(jnp.int32, (elements, sent), 0)
+        back_ref[...] = jnp.where(row == line_ref[...], 1.0, 0.0).astype(BF16)
         for i in range(sent):
             rows_ref[i : i + 1, :] = jnp.where(strip == sent_at(send_ref, i), 1.0, 0.0)
         chosen = rows_ref[...].astype(BF16)
@@ -267,7 +298,6 @@
             picks_ref[f * sent : (f + 1) * sent, :] = dot(
                 chosen, pick_ref[f * elements : (f + 1) * elements, :]
             ).astype(BF16)
-        head = weight_tile(inv)
         v = [product(split(x[...]), head) for x in (xa_ref, xb_ref)]
         cut = [split(x) for x in v]
         near = own_faces(faces, pick_ref, w_ref, cut)
@@ -289,34 +319,28 @@
         near_half = lax.broadcasted_iota(jnp.int32, (halo, far), 1) % sent < halo
         even = lax.axis_index("space") % 2 == 0
         kept = jnp.where(near_half, jnp.where(even, 1.0, 0.0), jnp.where(even, 0.0, 1.0))
-        qo_ref[...] = got[slabs + 1][halo:] * qs[halo:] * kept
+        qo_ref[...] = qs[halo:] * kept
 
     (
         v0, part1, psent1, sig_sent, frac_sent, weights, pick, pick_sent, q_all, q_sent, q_o, choose,
-        sigma_all, frac_all,
+        put_back, sigma_all, frac_all,
     ) = call(
         setup_kernel,
         [
             two, two, ((slabs * sent, width), F32), ((sent, width), F32), ((sent, width), F32),
             ((stack, 2 * width, 2 * width), BF16), ((faces * elements, elements), BF16),
             ((faces * sent, elements), BF16), ((elements, far), BF16), ((sent, far), BF16),
-            ((halo, far), F32), ((sent, elements), BF16), full, full,
+            ((halo, far), F32), ((sent, elements), BF16), ((elements, sent), BF16), full, full,
         ],
         [
-            xa, xb, scale_row, diag_block, block_inverse, face_flux, time_trace, faces_row,
-            send_rows,
+            xa, xb, scale_col, inv_here, fold, faces_here, send_rows,
         ],
-        spaces=[VMEM] * 2 + [HBM] * 7,
+        spaces=[VMEM] * 6 + [HBM],
         scratch=[
-            VMEM((1, elements), F32),
-            VMEM((width, width), F32),
-            VMEM((width, width), F32),
-            VMEM((faces, width, width), F32),
-            VMEM((width, width), F32),
-            VMEM((faces, elements), jnp.int32),
             SMEM((1, sent), jnp.int32),
+            VMEM((1, sent), jnp.int32),
             VMEM((sent, elements), F32),
-            pltpu.SemaphoreType.DMA((7,)),
+            pltpu.SemaphoreType.DMA((2,)),
         ],
         flops=2e9,
     )
@@ -358,9 +382,9 @@
         near = sent_faces(picks_ref, w_ref, split(va + vb), halo)
         sa, sb = vo_ref[:halo, :], vo_ref[halo:, :]
         rest = (
-            o0_ref[:halo, :] + o0_ref[halo:, :] - DAMPING * product(split(sa + sb), w_ref[W_DIAG])
+            o0_ref[:halo, :] + o0_ref[halo:, :] - DAMPING * few(sa + sb, w_ref.at[W_DIAG])
         ) / sigs_ref[halo:, :]
-        rest = rest + product(split(sa), w_ref[W_TIME]) + near
+        rest = rest + few(sa, w_ref.at[W_TIME]) + near
         wo_ref[...] = fracs_ref[halo:, :] * rest + sb
 
     v1, w_part = call(
@@ -392,13 +416,6 @@
         flops=1e7,
     )
     ro1 = over_o(o1)
-
-    def carry(v1_ref, v_ref, w_ref, sig_ref, x_ref):
-        step = split(v1_ref[:elements, :] - v1_ref[elements:, :])
-        x_ref[...] = v_ref[elements:, :] + sig_ref[...] * product(step, w_ref[W_TIME])
-
-    (x_own,) = call(carry, [full], [v1, v0, weights, sigma_all], flops=1e8)
-    x_before = later(x_own, 1)
 
     def middle(
         v1_ref, v_ref, w_ref, pick_ref, sig_ref, frac_ref, pa_ref, pb_ref, wp_ref
@@ -419,65 +436,91 @@
 
     pa0, pb0, wp = call(middle, [full] * 3, [v1, v0, weights, pick, sigma_all, frac_all], flops=1e9)
 
-    more = ((elements + halo, width), F32)
-
-    def coarse_kernel(re_ref, ro_ref, vo_ref, wp_ref, w_ref, q_ref, frac_ref, w_out, table_ref):
+    early_w = [later(wp, a) for a in range(1, groups)]
+
+    def carry(v1_ref, v_ref, w_ref, sig_ref, x_ref):
+        step = split(v1_ref[:elements, :] - v1_ref[elements:, :])
+        x_ref[...] = v_ref[elements:, :] + sig_ref[...] * product(step, w_ref[W_TIME])
+
+    (x_own,) = call(carry, [full], [v1, v0, weights, sigma_all], flops=1e8)
+
+    few_rows = ((sent + halo, width), F32)
+
+    def coarse_kernel(re_ref, ro_ref, vo_ref, w_ref, qs_ref, fracs_ref, w_out, table_ref):
         rows = arrived(re_ref, ro_ref.at[: slabs * halo, :], slabs)
         both = vo_ref[:halo, :] + vo_ref[halo:, :]
         rows.append(jnp.concatenate([both, both], axis=0))
         table = far_faces(faces, rows, w_ref)
         lanes = 2 * width
-        add = spread(q_ref[...], table[:, : slabs * lanes], slabs)
-        mine = halves(table[:, slabs * lanes :].astype(F32))
-        w_out[:elements, :] = wp_ref[...] + frac_ref[...] * (add[0] + add[1])
-        w_out[elements:, :] = ro_ref[slabs * halo : (slabs + 1) * halo, :] + dot32(
-            ro_ref[(slabs + 1) * halo : (slabs + 2) * halo, :], mine
+        add = spread(qs_ref[...], table[:, : slabs * lanes], slabs)
+        late = fracs_ref[...] * (add[0] + add[1])
+        even = lax.axis_index("space") % 2 == 0
+        w_out[:halo, :] = jnp.where(even, late[halo:], late[:halo])
+        w_out[halo:sent, :] = jnp.where(even, late[:halo], late[halo:])
+        mine = spread(
+            ro_ref[(slabs + 1) * halo : (slabs + 2) * halo, :].astype(BF16),
+            table[:, slabs * lanes :],
+            1,
+        )[0]
+        w_out[sent:, :] = (
+            ro_ref[slabs * halo : (slabs + 1) * halo, :] + ro_ref[(slabs + 2) * halo :, :] * mine
         )
         table_ref[...] = table[:, : slabs * lanes]
 
-    w_own, table1 = call(
+    w_late, table1 = call(
         coarse_kernel,
-        [more, ((far, slabs * 2 * width), BF16)],
-        [re1, ro1, vo, wp, weights, q_all, frac_all],
+        [few_rows, ((far, slabs * 2 * width), BF16)],
+        [re1, ro1, vo, weights, q_sent, frac_sent],
         flops=1e7,
     )
-
-    def rest_kernel(table_ref, pa_ref, pb_ref, q_ref, sig_ref, sent_ref, pa_out, pb_out, ps_out):
+    late_w = [later(w_late, a) for a in range(1, groups)]
+    x_before = later(x_own, 1)
+
+    def rest_kernel(
+        table_ref, pa_ref, pb_ref, wp_ref, v1_ref, q_ref, sig_ref, frac_ref, sent_ref,
+        pa_out, pb_out, ps_out, c_out,
+    ):
         add = spread(q_ref[...], table_ref[...], slabs)
         a = pa_ref[...] + sig_ref[...] * add[0]
         b = pb_ref[...] + sig_ref[...] * add[1]
         pa_out[...] = a
         pb_out[...] = b
+        c_out[...] = (
+            wp_ref[...] - v1_ref[(slabs - 1) * elements :, :] + frac_ref[...] * (add[0] + add[1])
+        )
         got = at_sent(sent_ref, [a, b])
         ps_out[:sent, :] = got[0]
         ps_out[sent:, :] = got[1]
 
-    pa1, pb1, psent2 = call(
+    pa1, pb1, psent2, c_start = call(
         rest_kernel,
-        [full, full, ((slabs * sent, width), F32)],
-        [table1, pa0, pb0, q_all, sigma_all, choose],
+        [full, full, ((slabs * sent, width), F32), full],
+        [table1, pa0, pb0, wp, v1, q_all, sigma_all, frac_all, choose],
         flops=1e8,
     )
-    earlier = [later(w_own, a) for a in range(1, groups)]
 
     def recur(*refs):
-        olds = refs[: groups - 1]
-        w_own_ref, v1_ref, ro_ref, w_ref, sent_ref, frac_ref, c_ref, d_ref, s_ref, e_ref, oh_ref = (
-            refs[groups - 1 :]
-        )
+        n = groups - 1
+        earlies, lates = refs[:n], refs[n : 2 * n]
+        c0_ref, late_ref, ro_ref, w_ref, sent_ref, back_ref, frac_ref = refs[2 * n : 2 * n + 7]
+        c_ref, d_ref, s_ref, e_ref, oh_ref = refs[2 * n + 7 :]
+        every = jnp.concatenate([split(x[:sent, :]) for x in lates], axis=1)
+        fixes = spread(back_ref[...], every, n)
+        olds = [
+            jnp.concatenate([x[...] + fix, y[sent:, :]], axis=0)
+            for x, y, fix in zip(earlies, lates, fixes)
+        ]
         frac = jnp.concatenate([frac_ref[...], ro_ref[(slabs + 2) * halo :, :]], axis=0)
-        v_last = jnp.concatenate(
-            [v1_ref[(slabs - 1) * elements :, :], ro_ref[(slabs - 1) * halo : slabs * halo, :]],
-            axis=0,
-        )
-        d = time_mask(olds[0][...])
-        c = w_own_ref[...] - v_last
+        c = jnp.concatenate(
+            [c0_ref[...], late_ref[sent:, :] - ro_ref[(slabs - 1) * halo : slabs * halo, :]], axis=0
+        )
+        d = time_mask(olds[0])
         power = frac
         for a in range(1, groups):
-            cut = split(time_mask(power * olds[a - 1][...], a))
+            cut = split(time_mask(power * olds[a - 1], a))
             c = c + product(cut, w_ref[W_TIME + a - 1])
             if a < groups - 1:
-                cut = split(time_mask(power * olds[a][...], a + 1))
+                cut = split(time_mask(power * olds[a], a + 1))
                 d = d + product(cut, w_ref[W_TIME + a - 1])
                 power = power * frac
         c_ref[...] = c[:elements]
@@ -494,7 +537,7 @@
     c_all, d_all, cd_sent, e2, ro2 = call(
         recur,
         [full, full, ((2 * sent, width), F32), edge, edge],
-        [*earlier, w_own, v1, ro1, weights, choose, frac_all],
+        [*early_w, *late_w, c_start, w_late, ro1, weights, choose, put_back, frac_all],
         flops=1e8,
     )
     re2 = over_e(e2)
@@ -503,12 +546,10 @@
         sigma = sigs_ref[...]
         near = sent_faces(picks_ref, w_ref, split(c_ref[...]), 0)
         c = cds_ref[:sent, :]
-        cut = split(c)
-        same = c - DAMPING * product(cut, w_ref[W_DIAG]) + sigma * near
-        out_ref[:sent, :] = ps_ref[:sent, :] + same + sigma * product(
-            split(cds_ref[sent:, :]), w_ref[W_TIME]
-        )
-        out_ref[sent:, :] = ps_ref[sent:, :] + same + sigma * product(cut, w_ref[W_TIME])
+        same = c - DAMPING * few(c, w_ref.at[W_DIAG]) + sigma * near
+        times = few(cds_ref[...], w_ref.at[W_TIME])
+        out_ref[:sent, :] = ps_ref[:sent, :] + same + sigma * times[sent:]
+        out_ref[sent:, :] = ps_ref[sent:, :] + same + sigma * times[:sent]
 
     (psent3,) = call(
         ahead_two,
@@ -517,6 +558,11 @@
         flops=1e8,
     )
 
+    def near_c(c_ref, w_ref, pick_ref, g_ref):
+        g_ref[...] = own_faces(faces, pick_ref, w_ref, [split(c_ref[...])])[0]
+
+    (g_c,) = call(near_c, [full], [c_all, weights, pick], flops=3e8)
+
     def edge_two(re_ref, ro_ref, psent_ref, sigs_ref, w_ref, qs_ref, e_ref, o_ref):
         table = far_faces(faces, arrived(re_ref, ro_ref, 2)[:1], w_ref)
         add = sigs_ref[...] * spread(qs_ref[...], table, 1)[0]
@@ -533,13 +579,13 @@
     re3, ro3 = over_e(e3), over_o(o3)
 
     def sweep(
-        re_ref, ro_ref, c_in, d_in, xb_ref, pa_ref, pb_ref, v_ref, w_ref, pick_ref, q_ref, sig_ref,
+        re_ref, ro_ref, c_in, d_in, g_ref, xb_ref, pa_ref, pb_ref, v_ref, w_ref, pick_ref, q_ref, sig_ref,
         out_ref,
     ):
         sigma = sig_ref[...]
         c, d = c_in[...], d_in[...]
         cc, cd = split(c), split(d)
-        gc, gd = own_faces(faces, pick_ref, w_ref, [cc, cd])
+        gc, gd = g_ref[...], own_faces(faces, pick_ref, w_ref, [cd])[0]
         add = spread(q_ref[...], far_faces(faces, arrived(re_ref, ro_ref, 2), w_ref), 2)
         same = c - DAMPING * product(cc, w_ref[W_DIAG]) + sigma * (gc + add[0])
         td = product(cd, w_ref[W_TIME])
@@ -564,7 +610,7 @@
     (part4,) = call(
         sweep,
         [two],
-        [re2, ro2, c_all, d_all, x_before, pa1, pb1, v0, weights, pick, q_all, sigma_all],
+        [re2, ro2, c_all, d_all, g_c, x_before, pa1, pb1, v0, weights, pick, q_all, sigma_all],
         flops=2e9,
     )
 

time: 38.1 us -> 43.9 us (1.15)
  waiting for transfers between devices: 12 us -> 15.5 us
  starting transfers between devices: 13.1 us -> 16.1 us
  Pallas kernels: 12.8 us -> 12 us
    ppermute x5 -> x8, waiting for transfers between devices: 5.85 us -> 10.5 us  [later(): lax.ppermute(x, 'tm', [(i, (i + by) % groups) for i in range(groups)])]
    ppermute x5 -> x8, starting transfers between devices: 6.04 us -> 9.2 us  [later(): lax.ppermute(x, 'tm', [(i, (i + by) % groups) for i in range(groups)])]
    pallas_call x14 -> x15, Pallas kernels: 12.8 us -> 12 us  [call(): pl.pallas_call(kernel, out_shape=[jax.ShapeDtypeStruct(s, d) for s, d in...]
    ppermute x4, waiting for transfers between devices: 0.75 us -> 0.16 us  [over_e(): return lax.ppermute(x, 'space', swap_e)]
    ppermute x3, waiting for transfers between devices: 5.37 us -> 4.86 us  [over_o(): return lax.ppermute(x, 'space', swap_o)]
  transfers between devices with their start and end apart: 12 -> 15, of which waited for: 8 -> 6; matrix products, arithmetic and copies ran while one was open for 0% -> 0% of each run, Pallas kernels for 24% -> 21%
where the time goes in v5:
time: 43.9 us; the launch traced here: 43.8 us
  starting transfers between devices  16.1 us (37%)
  waiting for transfers between devices  15.5 us (35%)
  Pallas kernels  12 us (27%)
    pallas_call x15, Pallas kernels, call(): pl.pallas_call(kernel, out_shape=[jax.ShapeDtypeStruct(s, d) for s, d in...  12 us
    ppermute x8, waiting for transfers between devices, later(): lax.ppermute(x, 'tm', [(i, (i + by) % groups) for i in range(groups)])  10.5 us
    ppermute x8, starting transfers between devices, later(): lax.ppermute(x, 'tm', [(i, (i + by) % groups) for i in range(groups)])  9.2 us
    ppermute x3, starting transfers between devices, over_o(): return lax.ppermute(x, 'space', swap_o)  5.96 us
    ppermute x3, waiting for transfers between devices, over_o(): return lax.ppermute(x, 'space', swap_o)  4.86 us
    ppermute x4, starting transfers between devices, over_e(): return lax.ppermute(x, 'space', swap_e)  0.97 us
  transfers between devices with their start and end apart: 15, of which 6 were waited for; matrix products, arithmetic and copies ran while one was open for 0% of the time, Pallas kernels for 21%

profile of v5, /device:TPU:0, one launch (start us, length us, event | category | flops | bytes accessed | tf_op | source)
XLA Modules:
  0.0 43.8 jit_solution(2479012810057270074)
XLA Ops:
  0.0 1.3 %shard_map.82 = (f32[32,128]{1,0:T(8,128)S(1)}, f32[32,128]{1,0:T(8,128)S(1)}, f32[256,128]{1,0:T(8,128)S(1)}, f32[256,128]{1,0:T(8,128)S(1)}, f32[256,128]{1,0:...) custom-call(f32[512,128]{1,0:T(8,128)} %bitcast.5, f32[1,256]{1,0:T(1,128)} %bitcast.8, ...), custom_call_target="tpu_custom_call" | custom-call | flops 10000000 | bytes 1048576 | tf_op jit(solution)/shard_map/pallas_call | solution.py:24
  1.3 3.0 %collective-permute-start.2 = (f32[256,128]{1,0:T(8,128)S(1)}, f32[256,128]{1,0:T(8,128)S(1)}, u32[]{:S(2)}, u32[]{:S(2)}) collective-permute-start(f32[256,128]{1,0:T(8,128)S(1)} %get-tuple-element.50.xb_ref), channel_id=1, source_target_pairs={{0,8},{8,16},{16,24},{24,0},{1,9},{9,17},{17,25},{25,1},{2,10},{10... | collective-permute-start | bytes 393224 | tf_op jit(solution)/shard_map/ppermute | solution.py:167
  4.3 2.8 %collective-permute-start.1 = (f32[32,128]{1,0:T(8,128)S(1)}, f32[32,128]{1,0:T(8,128)S(1)}, u32[]{:S(2)}, u32[]{:S(2)}) collective-permute-start(f32[32,128]{1,0:T(8,128)S(1)} %get-tuple-element.49.o0_ref), channel_id=1, source_target_pairs={{0,7},{1,2},{2,1},{3,4},{4,3},{5,6},{6,5},{7,0},{8,15},{9,10},{10,... | collective-permute-start | bytes 49160 | tf_op jit(solution)/shard_map/ppermute | solution.py:164
  7.1 0.0 collective-permute-start
  7.1 2.2 %shard_map.83 = (f32[512,128]{1,0:T(8,128)S(1)}, f32[512,128]{1,0:T(8,128)S(1)}, f32[64,128]{1,0:T(8,128)S(1)}, f32[32,128]{1,0:T(8,128)S(1)}, f32[32,128]{1,0:T...) custom-call(f32[256,128]{1,0:T(8,128)S(1)} %get-tuple-element.51.xa_, ...), custom_call_target="tpu_custom_call" | custom-call | flops 2000000000 | bytes 1048576 | tf_op jit(solution)/shard_map/pallas_call | solution.py:24
  9.3 0.0 collective-permute-done.1.ro_ref
  9.3 0.0 collective-permute-done.re_ref
  9.3 0.0 collective-permute-done.2.b_ref
  9.3 0.5 %shard_map.84 = (f32[32,128]{1,0:T(8,128)S(1)}, f32[32,128]{1,0:T(8,128)S(1)}) custom-call(f32[32,128]{1,0:T(8,128)S(1)} %collective-permute-done.re_ref, f32[32,128]{1,0:T(8,128)S(1)} %collective-permute-done.1.ro_ref, f32[256,128]{1,0:T(8,128)S(1)} %collective-permute-done.2.b_ref, f32[64,128]{1,0:T(8,128)S(1)} %get-tuple-element.57.psent_ref, ...), custom_call_target="tpu_custom_call" | custom-call | flops 10000000 | bytes 1048576 | tf_op jit(solution)/shard_map/pallas_call | solution.py:24
  9.8 0.6 %collective-permute-start.6 = (f32[32,128]{1,0:T(8,128)S(1)}, f32[32,128]{1,0:T(8,128)S(1)}, u32[]{:S(2)}, u32[]{:S(2)}) collective-permute-start(f32[32,128]{1,0:T(8,128)S(1)} %get-tuple-element.72), channel_id=1, source_target_pairs={{0,1},{1,0},{2,3},{3,2},{4,5},{5,4},{6,7},{7,6},{8,9},{9,8},{10,11... | collective-permute-start | bytes 49160 | tf_op jit(solution)/shard_map/ppermute | solution.py:161
  10.4 0.9 %shard_map.85 = (f32[512,128]{1,0:T(8,128)S(1)}, f32[16,128]{1,0:T(8,128)S(1)}) custom-call(f32[32,128]{1,0:T(8,128)S(1)} %collective-permute-done.re_ref, f32[32,128]{1,0:T(8,128)S(1)} %collective-permute-done.1.ro_ref, f32[256,128]{1,0:T(8,128)S(1)} %collective-permute-done.2.b_ref, f32[512,128]{1,0:T(8,128)S(1)} %get-tuple-element.56.part_ref, ...), custom_call_target="tpu_custom_call" | custom-call | flops 200000000 | bytes 1048576 | tf_op jit(solution)/shard_map/pallas_call | solution.py:24
  11.3 1.0 %shard_map.86 = (f32[256,128]{1,0:T(8,128)S(1)}, f32[256,128]{1,0:T(8,128)S(1)}, f32[256,128]{1,0:T(8,128)S(1)}) custom-call(f32[512,128]{1,0:T(8,128)S(1)} %get-tuple-element.67.v1_ref, f32[512,128]{1,0:T(8,128)S(1)} %get-tuple-element.68.v_ref, bf16[9,256,256]{2,1,0:T(8,128)(2,1)S(1)} %get-tuple-element.59.w_ref.refs_9_, ...), custom_call_target="tpu_custom_call" | custom-call | flops 1000000000 | bytes 1048576 | tf_op jit(solution)/shard_map/pallas_call | solution.py:24
  12.3 1.5 %collective-permute-start.3 = (f32[256,128]{1,0:T(8,128)S(1)}, f32[256,128]{1,0:T(8,128)S(1)}, u32[]{:S(2)}, u32[]{:S(2)}) collective-permute-start(f32[256,128]{1,0:T(8,128)S(1)} %get-tuple-element.71.wp_ref), channel_id=1, source_target_pairs={{0,8},{8,16},{16,24},{24,0},{1,9},{9,17},{17,25},{25,1},{2,10},{10... | collective-permute-start | bytes 393224 | tf_op jit(solution)/shard_map/ppermute | solution.py:167
  13.9 0.5 %collective-permute-start.4 = (f32[256,128]{1,0:T(8,128)S(1)}, f32[256,128]{1,0:T(8,128)S(1)}, u32[]{:S(2)}, u32[]{:S(2)}) collective-permute-start(f32[256,128]{1,0:T(8,128)S(1)} %get-tuple-element.71.wp_ref), channel_id=1, source_target_pairs={{0,16},{8,24},{16,0},{24,8},{1,17},{9,25},{17,1},{25,9},{2,18},{10... | collective-permute-start | bytes 393224 | tf_op jit(solution)/shard_map/ppermute | solution.py:167
  14.4 2.4 %collective-permute-start.5 = (f32[256,128]{1,0:T(8,128)S(1)}, f32[256,128]{1,0:T(8,128)S(1)}, u32[]{:S(2)}, u32[]{:S(2)}) collective-permute-start(f32[256,128]{1,0:T(8,128)S(1)} %get-tuple-element.71.wp_ref), channel_id=1, source_target_pairs={{0,24},{8,0},{16,8},{24,16},{1,25},{9,1},{17,9},{25,17},{2,26},{10... | collective-permute-start | bytes 393224 | tf_op jit(solution)/shard_map/ppermute | solution.py:167
  16.8 0.0 collective-permute-done.6.re_ref
  16.8 0.3 shard_map.87
  17.1 2.0 %collective-permute-start.7 = (f32[80,128]{1,0:T(8,128)S(1)}, f32[80,128]{1,0:T(8,128)S(1)}, u32[]{:S(2)}, u32[]{:S(2)}) collective-permute-start(f32[80,128]{1,0:T(8,128)S(1)} %shard_map.87), channel_id=1, source_target_pairs={{0,7},{1,2},{2,1},{3,4},{4,3},{5,6},{6,5},{7,0},{8,15},{9,10},{10,... | collective-permute-start | bytes 122888 | tf_op jit(solution)/shard_map/ppermute | solution.py:164
  19.1 0.2 shard_map.94
  19.3 0.1 collective-permute-start.14
  19.4 2.9 %collective-permute-done.7.ro_ref.refs_8_ = f32[80,128]{1,0:T(8,128)S(1)} collective-permute-done((f32[80,128]{1,0:T(8,128)S(1)}, f32[80,128]{1,0:T(8,128)S(1)}, u32[]{:S(2)}, u32[]{:S(2)}) %collective-permute-start.7) | collective-permute-done | bytes 40992 | tf_op jit(solution)/shard_map/ppermute | solution.py:164
  22.4 0.4 shard_map.88
  22.7 0.6 %collective-permute-start.10 = (f32[48,128]{1,0:T(8,128)S(1)}, f32[48,128]{1,0:T(8,128)S(1)}, u32[]{:S(2)}, u32[]{:S(2)}) collective-permute-start(f32[48,128]{1,0:T(8,128)S(1)} %get-tuple-element.75.refs_7_), channel_id=1, source_target_pairs={{0,24},{8,0},{16,8},{24,16},{1,25},{9,1},{17,9},{25,17},{2,26},{10... | collective-permute-start | bytes 73736 | tf_op jit(solution)/shard_map/ppermute | solution.py:167
  23.3 3.3 %collective-permute-done.10.refs_5_ = f32[48,128]{1,0:T(8,128)S(1)} collective-permute-done((f32[48,128]{1,0:T(8,128)S(1)}, f32[48,128]{1,0:T(8,128)S(1)}, u32[]{:S(2)}, u32[]{:S(2)}) %collective-permute-start.10) | collective-permute-done | bytes 24608 | tf_op jit(solution)/shard_map/ppermute | solution.py:167
  26.6 0.5 %collective-permute-start.8 = (f32[48,128]{1,0:T(8,128)S(1)}, f32[48,128]{1,0:T(8,128)S(1)}, u32[]{:S(2)}, u32[]{:S(2)}) collective-permute-start(f32[48,128]{1,0:T(8,128)S(1)} %get-tuple-element.75.refs_7_), channel_id=1, source_target_pairs={{0,8},{8,16},{16,24},{24,0},{1,9},{9,17},{17,25},{25,1},{2,10},{10... | collective-permute-start | bytes 73736 | tf_op jit(solution)/shard_map/ppermute | solution.py:167
  27.2 4.2 %collective-permute-done.8.refs_3_ = f32[48,128]{1,0:T(8,128)S(1)} collective-permute-done((f32[48,128]{1,0:T(8,128)S(1)}, f32[48,128]{1,0:T(8,128)S(1)}, u32[]{:S(2)}, u32[]{:S(2)}) %collective-permute-start.8) | collective-permute-done | bytes 24608 | tf_op jit(solution)/shard_map/ppermute | solution.py:167
  31.3 0.5 %collective-permute-start.9 = (f32[48,128]{1,0:T(8,128)S(1)}, f32[48,128]{1,0:T(8,128)S(1)}, u32[]{:S(2)}, u32[]{:S(2)}) collective-permute-start(f32[48,128]{1,0:T(8,128)S(1)} %get-tuple-element.75.refs_7_), channel_id=1, source_target_pairs={{0,16},{8,24},{16,0},{24,8},{1,17},{9,25},{17,1},{25,9},{2,18},{10... | collective-permute-start | bytes 73736 | tf_op jit(solution)/shard_map/ppermute | solution.py:167
  31.8 0.3 shard_map.89
  32.2 3.0 %collective-permute-done.9.refs_4_ = f32[48,128]{1,0:T(8,128)S(1)} collective-permute-done((f32[48,128]{1,0:T(8,128)S(1)}, f32[48,128]{1,0:T(8,128)S(1)}, u32[]{:S(2)}, u32[]{:S(2)}) %collective-permute-start.9) | collective-permute-done | bytes 24608 | tf_op jit(solution)/shard_map/ppermute | solution.py:167
  35.2 0.0 collective-permute-done.3.refs_0_
  35.2 0.0 collective-permute-done.4.refs_1_
  35.2 0.0 collective-permute-done.5.refs_2_
  35.2 0.6 %shard_map.90 = (f32[256,128]{1,0:T(8,128)S(1)}, f32[256,128]{1,0:T(8,128)S(1)}, f32[64,128]{1,0:T(8,128)S(1)}, f32[32,128]{1,0:T(8,128)S(1)}, f32[32,128]{1,0:T(8,128)S(1)}) custom-call(f32[256,128]{1,0:T(8,128)S(1)} %collective-permute-done.3.refs_0_, f32[256,128]{1,0:T(8,128)S(1)} %collective-permute-done.4.refs_1_, ...), custom_call_target="tpu_custom_call" | custom-call | flops 100000000 | bytes 1048576 | tf_op jit(solution)/shard_map/pallas_call | solution.py:24
  35.8 0.0 collective-permute-start.11
  35.9 0.6 %shard_map.93.g_ref = f32[256,128]{1,0:T(8,128)S(1)} custom-call(f32[256,128]{1,0:T(8,128)S(1)} %get-tuple-element.83.c_ref.c_in, bf16[9,256,256]{2,1,0:T(8,128)(2,1)S(1)} %get-tuple-element.59.w_ref.refs_9_, bf16[1024,256]{1,0:T(8,128)(2,1)S(1)} %get-tuple-element.69.pick_ref), custom_call_target="tpu_custom_call" | custom-call | flops 300000000 | bytes 1048576 | tf_op jit(solution)/shard_map/pallas_call | solution.py:24
  36.5 0.4 shard_map.91.psent_ref
  36.9 0.2 collective-permute-done.11.re_ref
  37.0 0.3 shard_map.92
  37.3 0.4 collective-permute-start.12
  37.7 1.2 %collective-permute-start.13 = (f32[32,128]{1,0:T(8,128)S(1)}, f32[32,128]{1,0:T(8,128)S(1)}, u32[]{:S(2)}, u32[]{:S(2)}) collective-permute-start(f32[32,128]{1,0:T(8,128)S(1)} %get-tuple-element.87), channel_id=1, source_target_pairs={{0,7},{1,2},{2,1},{3,4},{4,3},{5,6},{6,5},{7,0},{8,15},{9,10},{10,... | collective-permute-start | bytes 49160 | tf_op jit(solution)/shard_map/ppermute | solution.py:164
  38.9 0.0 collective-permute-done.14.xb_ref
  38.9 1.9 %shard_map.95.p_ref = f32[512,128]{1,0:T(8,128)S(1)} custom-call(f32[32,128]{1,0:T(8,128)S(1)} %collective-permute-done.11.re_ref, f32[32,128]{1,0:T(8,128)S(1)} %get-tuple-element.82.ro_ref, f32[256,128]{1,0:T(8,128)S(1)} %get-tuple-element.83.c_ref.c_in, f32[256,128]{1,0:T(8,128)S(1)} %get-tuple-element.88.d_in, f32[256,128]{1,0:T(8,128)S(1)} %shard_map.93.g_ref, ...), custom_call_target="tpu_custom_call" | custom-call | flops 2000000000 | bytes 1048576 | tf_op jit(solution)/shard_map/pallas_call | solution.py:24
  40.7 0.0 collective-permute-done.12.re_ref
  40.7 1.9 %collective-permute-done.13.ro_ref = f32[32,128]{1,0:T(8,128)S(1)} collective-permute-done((f32[32,128]{1,0:T(8,128)S(1)}, f32[32,128]{1,0:T(8,128)S(1)}, u32[]{:S(2)}, u32[]{:S(2)}) %collective-permute-start.13) | collective-permute-done | bytes 16416 | tf_op jit(solution)/shard_map/ppermute | solution.py:164
  42.6 1.1 %shard_map.96 = f32[512,128]{1,0:T(8,128)} custom-call(f32[32,128]{1,0:T(8,128)S(1)} %collective-permute-done.12.re_ref, f32[32,128]{1,0:T(8,128)S(1)} %collective-permute-done.13.ro_ref, f32[512,128]{1,0:T(8,128)S(1)} %shard_map.95.p_ref, bf16[9,256,256]{2,1,0:T(8,128)(2,1)S(1)} %get-tuple-element.59.w_ref.refs_9_, ...), custom_call_target="tpu_custom_call" | custom-call | flops 10000000 | bytes 1048576 | tf_op jit(solution)/shard_map/pallas_call | solution.py:24
Async XLA Ops:
  1.3 8.0 %collective-permute-start.2 = (f32[256,128]{1,0:T(8,128)S(1)}, f32[256,128]{1,0:T(8,128)S(1)}, u32[]{:S(2)}, u32[]{:S(2)}) collective-permute-start(f32[256,128]{1,0:T(8,128)S(1)} %get-tuple-element.50.xb_ref), channel_id=1, source_target_pairs={{0,8},{8,16},{16,24},{24,0},{1,9},{9,17},{17,25},{25,1},{2,10},{10... | collective-permute-start | bytes 393224 | tf_op jit(solution)/shard_map/ppermute | solution.py:167
  4.3 5.0 %collective-permute-start.1 = (f32[32,128]{1,0:T(8,128)S(1)}, f32[32,128]{1,0:T(8,128)S(1)}, u32[]{:S(2)}, u32[]{:S(2)}) collective-permute-start(f32[32,128]{1,0:T(8,128)S(1)} %get-tuple-element.49.o0_ref), channel_id=1, source_target_pairs={{0,7},{1,2},{2,1},{3,4},{4,3},{5,6},{6,5},{7,0},{8,15},{9,10},{10,... | collective-permute-start | bytes 49160 | tf_op jit(solution)/shard_map/ppermute | solution.py:164
  7.1 2.2 %collective-permute-start = (f32[32,128]{1,0:T(8,128)S(1)}, f32[32,128]{1,0:T(8,128)S(1)}, u32[]{:S(2)}, u32[]{:S(2)}) collective-permute-start(f32[32,128]{1,0:T(8,128)S(1)} %get-tuple-element.48), channel_id=1, source_target_pairs={{0,1},{1,0},{2,3},{3,2},{4,5},{5,4},{6,7},{7,6},{8,9},{9,8},{10,11... | collective-permute-start | bytes 49160 | tf_op jit(solution)/shard_map/ppermute | solution.py:161
  9.8 7.0 %collective-permute-start.6 = (f32[32,128]{1,0:T(8,128)S(1)}, f32[32,128]{1,0:T(8,128)S(1)}, u32[]{:S(2)}, u32[]{:S(2)}) collective-permute-start(f32[32,128]{1,0:T(8,128)S(1)} %get-tuple-element.72), channel_id=1, source_target_pairs={{0,1},{1,0},{2,3},{3,2},{4,5},{5,4},{6,7},{7,6},{8,9},{9,8},{10,11... | collective-permute-start | bytes 49160 | tf_op jit(solution)/shard_map/ppermute | solution.py:161
  12.3 22.9 %collective-permute-start.3 = (f32[256,128]{1,0:T(8,128)S(1)}, f32[256,128]{1,0:T(8,128)S(1)}, u32[]{:S(2)}, u32[]{:S(2)}) collective-permute-start(f32[256,128]{1,0:T(8,128)S(1)} %get-tuple-element.71.wp_ref), channel_id=1, source_target_pairs={{0,8},{8,16},{16,24},{24,0},{1,9},{9,17},{17,25},{25,1},{2,10},{10... | collective-permute-start | bytes 393224 | tf_op jit(solution)/shard_map/ppermute | solution.py:167
  13.9 21.3 %collective-permute-start.4 = (f32[256,128]{1,0:T(8,128)S(1)}, f32[256,128]{1,0:T(8,128)S(1)}, u32[]{:S(2)}, u32[]{:S(2)}) collective-permute-start(f32[256,128]{1,0:T(8,128)S(1)} %get-tuple-element.71.wp_ref), channel_id=1, source_target_pairs={{0,16},{8,24},{16,0},{24,8},{1,17},{9,25},{17,1},{25,9},{2,18},{10... | collective-permute-start | bytes 393224 | tf_op jit(solution)/shard_map/ppermute | solution.py:167
  14.4 20.8 %collective-permute-start.5 = (f32[256,128]{1,0:T(8,128)S(1)}, f32[256,128]{1,0:T(8,128)S(1)}, u32[]{:S(2)}, u32[]{:S(2)}) collective-permute-start(f32[256,128]{1,0:T(8,128)S(1)} %get-tuple-element.71.wp_ref), channel_id=1, source_target_pairs={{0,24},{8,0},{16,8},{24,16},{1,25},{9,1},{17,9},{25,17},{2,26},{10... | collective-permute-start | bytes 393224 | tf_op jit(solution)/shard_map/ppermute | solution.py:167
  17.1 5.2 %collective-permute-start.7 = (f32[80,128]{1,0:T(8,128)S(1)}, f32[80,128]{1,0:T(8,128)S(1)}, u32[]{:S(2)}, u32[]{:S(2)}) collective-permute-start(f32[80,128]{1,0:T(8,128)S(1)} %shard_map.87), channel_id=1, source_target_pairs={{0,7},{1,2},{2,1},{3,4},{4,3},{5,6},{6,5},{7,0},{8,15},{9,10},{10,... | collective-permute-start | bytes 122888 | tf_op jit(solution)/shard_map/ppermute | solution.py:164
  19.3 19.5 %collective-permute-start.14 = (f32[256,128]{1,0:T(8,128)S(1)}, f32[256,128]{1,0:T(8,128)S(1)}, u32[]{:S(2)}, u32[]{:S(2)}) collective-permute-start(f32[256,128]{1,0:T(8,128)S(1)} %shard_map.94), channel_id=1, source_target_pairs={{0,8},{8,16},{16,24},{24,0},{1,9},{9,17},{17,25},{25,1},{2,10},{10... | collective-permute-start | bytes 393224 | tf_op jit(solution)/shard_map/ppermute | solution.py:167
  22.7 3.9 %collective-permute-start.10 = (f32[48,128]{1,0:T(8,128)S(1)}, f32[48,128]{1,0:T(8,128)S(1)}, u32[]{:S(2)}, u32[]{:S(2)}) collective-permute-start(f32[48,128]{1,0:T(8,128)S(1)} %get-tuple-element.75.refs_7_), channel_id=1, source_target_pairs={{0,24},{8,0},{16,8},{24,16},{1,25},{9,1},{17,9},{25,17},{2,26},{10... | collective-permute-start | bytes 73736 | tf_op jit(solution)/shard_map/ppermute | solution.py:167
  26.6 4.7 %collective-permute-start.8 = (f32[48,128]{1,0:T(8,128)S(1)}, f32[48,128]{1,0:T(8,128)S(1)}, u32[]{:S(2)}, u32[]{:S(2)}) collective-permute-start(f32[48,128]{1,0:T(8,128)S(1)} %get-tuple-element.75.refs_7_), channel_id=1, source_target_pairs={{0,8},{8,16},{16,24},{24,0},{1,9},{9,17},{17,25},{25,1},{2,10},{10... | collective-permute-start | bytes 73736 | tf_op jit(solution)/shard_map/ppermute | solution.py:167
  31.3 3.8 %collective-permute-start.9 = (f32[48,128]{1,0:T(8,128)S(1)}, f32[48,128]{1,0:T(8,128)S(1)}, u32[]{:S(2)}, u32[]{:S(2)}) collective-permute-start(f32[48,128]{1,0:T(8,128)S(1)} %get-tuple-element.75.refs_7_), channel_id=1, source_target_pairs={{0,16},{8,24},{16,0},{24,8},{1,17},{9,25},{17,1},{25,9},{2,18},{10... | collective-permute-start | bytes 73736 | tf_op jit(solution)/shard_map/ppermute | solution.py:167
  35.8 1.2 %collective-permute-start.11 = (f32[32,128]{1,0:T(8,128)S(1)}, f32[32,128]{1,0:T(8,128)S(1)}, u32[]{:S(2)}, u32[]{:S(2)}) collective-permute-start(f32[32,128]{1,0:T(8,128)S(1)} %get-tuple-element.81), channel_id=1, source_target_pairs={{0,1},{1,0},{2,3},{3,2},{4,5},{5,4},{6,7},{7,6},{8,9},{9,8},{10,11... | collective-permute-start | bytes 49160 | tf_op jit(solution)/shard_map/ppermute | solution.py:161
  37.3 3.4 %collective-permute-start.12 = (f32[32,128]{1,0:T(8,128)S(1)}, f32[32,128]{1,0:T(8,128)S(1)}, u32[]{:S(2)}, u32[]{:S(2)}) collective-permute-start(f32[32,128]{1,0:T(8,128)S(1)} %get-tuple-element.86), channel_id=1, source_target_pairs={{0,1},{1,0},{2,3},{3,2},{4,5},{5,4},{6,7},{7,6},{8,9},{9,8},{10,11... | collective-permute-start | bytes 49160 | tf_op jit(solution)/shard_map/ppermute | solution.py:161
  37.7 5.0 %collective-permute-start.13 = (f32[32,128]{1,0:T(8,128)S(1)}, f32[32,128]{1,0:T(8,128)S(1)}, u32[]{:S(2)}, u32[]{:S(2)}) collective-permute-start(f32[32,128]{1,0:T(8,128)S(1)} %get-tuple-element.87), channel_id=1, source_target_pairs={{0,7},{1,2},{2,1},{3,4},{4,3},{5,6},{6,5},{7,0},{8,15},{9,10},{10,... | collective-permute-start | bytes 49160 | tf_op jit(solution)/shard_map/ppermute | solution.py:164

commit v6 on v5

--- a/solution.py
+++ b/solution.py
@@ -417,24 +417,20 @@
     )
     ro1 = over_o(o1)
 
-    def middle(
-        v1_ref, v_ref, w_ref, pick_ref, sig_ref, frac_ref, pa_ref, pb_ref, wp_ref
-    ):
-        sigma = sig_ref[...]
-        frac = frac_ref[...]
+    def middle(v1_ref, v_ref, w_ref, pick_ref, sig_ref, frac_ref, wp_ref):
         va, vb = v1_ref[:elements, :], v1_ref[elements:, :]
-        v0a, v0b = v_ref[:elements, :], v_ref[elements:, :]
-        ca, cb = split(va), split(vb)
-        ga, gb = own_faces(faces, pick_ref, w_ref, [ca, cb])
-        da, db = product(ca, w_ref[W_DIAG]), product(cb, w_ref[W_DIAG])
-        ta = product(ca, w_ref[W_TIME])
-        pa_ref[...] = va + v0a - DAMPING * da + sigma * ga
-        pb_ref[...] = vb + v0b - DAMPING * db + sigma * (ta + gb)
-        wp_ref[...] = (
-            frac * (((v0a + v0b) - DAMPING * (da + db)) / sigma + ta + ga + gb) + vb
-        )
-
-    pa0, pb0, wp = call(middle, [full] * 3, [v1, v0, weights, pick, sigma_all, frac_all], flops=1e9)
+        cut = split(va + vb)
+        near = own_faces(faces, pick_ref, w_ref, [cut])[0]
+        rest = v_ref[:elements, :] + v_ref[elements:, :] - DAMPING * product(cut, w_ref[W_DIAG])
+        rest = rest / sig_ref[...] + product(split(va), w_ref[W_TIME]) + near
+        wp_ref[...] = frac_ref[...] * rest + vb
+
+    (wp,) = call(
+        middle,
+        [full],
+        [v1, v0, weights, pick, sigma_all, frac_all],
+        flops=1e9,
+    )
 
     early_w = [later(wp, a) for a in range(1, groups)]
 
@@ -477,17 +473,21 @@
     x_before = later(x_own, 1)
 
     def rest_kernel(
-        table_ref, pa_ref, pb_ref, wp_ref, v1_ref, q_ref, sig_ref, frac_ref, sent_ref,
+        table_ref, wp_ref, v1_ref, v_ref, w_ref, pick_ref, q_ref, sig_ref, frac_ref, sent_ref,
         pa_out, pb_out, ps_out, c_out,
     ):
+        sigma = sig_ref[...]
         add = spread(q_ref[...], table_ref[...], slabs)
-        a = pa_ref[...] + sig_ref[...] * add[0]
-        b = pb_ref[...] + sig_ref[...] * add[1]
+        va, vb = v1_ref[:elements, :], v1_ref[elements:, :]
+        c_out[...] = wp_ref[...] - vb + frac_ref[...] * (add[0] + add[1])
+        ca, cb = split(va), split(vb)
+        ga, gb = own_faces(faces, pick_ref, w_ref, [ca, cb])
+        a = va + v_ref[:elements, :] - DAMPING * product(ca, w_ref[W_DIAG])
+        a = a + sigma * (ga + add[0])
+        b = vb + v_ref[elements:, :] - DAMPING * product(cb, w_ref[W_DIAG])
+        b = b + sigma * (product(ca, w_ref[W_TIME]) + gb + add[1])
         pa_out[...] = a
         pb_out[...] = b
-        c_out[...] = (
-            wp_ref[...] - v1_ref[(slabs - 1) * elements :, :] + frac_ref[...] * (add[0] + add[1])
-        )
         got = at_sent(sent_ref, [a, b])
         ps_out[:sent, :] = got[0]
         ps_out[sent:, :] = got[1]
@@ -495,8 +495,8 @@
     pa1, pb1, psent2, c_start = call(
         rest_kernel,
         [full, full, ((slabs * sent, width), F32), full],
-        [table1, pa0, pb0, wp, v1, q_all, sigma_all, frac_all, choose],
-        flops=1e8,
+        [table1, wp, v1, v0, weights, pick, q_all, sigma_all, frac_all, choose],
+        flops=1e9,
     )
 
     def recur(*refs):

time: 43.9 us -> 39.6 us (0.902)
  waiting for transfers between devices: 15.5 us -> 6.89 us
  starting transfers between devices: 16.1 us -> 20 us
  Pallas kernels: 12 us -> 12.5 us
    ppermute x8, waiting for transfers between devices: 10.5 us -> 5.77 us  [later(): lax.ppermute(x, 'tm', [(i, (i + by) % groups) for i in range(groups)])]
    ppermute x3, waiting for transfers between devices: 4.86 us -> 0.67 us  [over_o(): return lax.ppermute(x, 'space', swap_o)]
    ppermute x3, starting transfers between devices: 5.96 us -> 8.32 us  [over_o(): return lax.ppermute(x, 'space', swap_o)]
    ppermute x8, starting transfers between devices: 9.2 us -> 10.6 us  [later(): lax.ppermute(x, 'tm', [(i, (i + by) % groups) for i in range(groups)])]
    pallas_call x15, Pallas kernels: 12 us -> 12.5 us  [call(): pl.pallas_call(kernel, out_shape=[jax.ShapeDtypeStruct(s, d) for s, d in...]
  transfers between devices with their start and end apart: 15 -> 15, of which waited for: 6 -> 7; matrix products, arithmetic and copies ran while one was open for 0% -> 0% of each run, Pallas kernels for 21% -> 23%
where the time goes in v6:
time: 39.6 us; the launch traced here: 39.5 us
  starting transfers between devices  20 us (51%)
  Pallas kernels  12.5 us (32%)
  waiting for transfers between devices  6.89 us (17%)
    pallas_call x15, Pallas kernels, call(): pl.pallas_call(kernel, out_shape=[jax.ShapeDtypeStruct(s, d) for s, d in...  12.5 us
    ppermute x8, starting transfers between devices, later(): lax.ppermute(x, 'tm', [(i, (i + by) % groups) for i in range(groups)])  10.6 us
    ppermute x3, starting transfers between devices, over_o(): return lax.ppermute(x, 'space', swap_o)  8.32 us
    ppermute x8, waiting for transfers between devices, later(): lax.ppermute(x, 'tm', [(i, (i + by) % groups) for i in range(groups)])  5.77 us
    ppermute x4, starting transfers between devices, over_e(): return lax.ppermute(x, 'space', swap_e)  1.02 us
  transfers between devices with their start and end apart: 15, of which 7 were waited for; matrix products, arithmetic and copies ran while one was open for 0% of the time, Pallas kernels for 23%

profile of v6, /device:TPU:0, one launch (start us, length us, event | category | flops | bytes accessed | tf_op | source)
XLA Modules:
  0.0 39.5 jit_solution(14796727333080122989)
XLA Ops:
  0.0 1.3 %shard_map.82 = (f32[32,128]{1,0:T(8,128)S(1)}, f32[32,128]{1,0:T(8,128)S(1)}, f32[256,128]{1,0:T(8,128)S(1)}, f32[256,128]{1,0:T(8,128)S(1)}, f32[256,128]{1,0:...) custom-call(f32[512,128]{1,0:T(8,128)} %bitcast.5, f32[1,256]{1,0:T(1,128)} %bitcast.8, ...), custom_call_target="tpu_custom_call" | custom-call | flops 10000000 | bytes 1048576 | tf_op jit(solution)/shard_map/pallas_call | solution.py:24
  1.3 0.6 %collective-permute-start = (f32[32,128]{1,0:T(8,128)S(1)}, f32[32,128]{1,0:T(8,128)S(1)}, u32[]{:S(2)}, u32[]{:S(2)}) collective-permute-start(f32[32,128]{1,0:T(8,128)S(1)} %get-tuple-element.45), channel_id=1, source_target_pairs={{0,1},{1,0},{2,3},{3,2},{4,5},{5,4},{6,7},{7,6},{8,9},{9,8},{10,11... | collective-permute-start | bytes 49160 | tf_op jit(solution)/shard_map/ppermute | solution.py:161
  1.9 4.7 %collective-permute-start.1 = (f32[32,128]{1,0:T(8,128)S(1)}, f32[32,128]{1,0:T(8,128)S(1)}, u32[]{:S(2)}, u32[]{:S(2)}) collective-permute-start(f32[32,128]{1,0:T(8,128)S(1)} %get-tuple-element.46.o0_ref), channel_id=1, source_target_pairs={{0,7},{1,2},{2,1},{3,4},{4,3},{5,6},{6,5},{7,0},{8,15},{9,10},{10,... | collective-permute-start | bytes 49160 | tf_op jit(solution)/shard_map/ppermute | solution.py:164
  6.6 1.5 %collective-permute-start.2 = (f32[256,128]{1,0:T(8,128)S(1)}, f32[256,128]{1,0:T(8,128)S(1)}, u32[]{:S(2)}, u32[]{:S(2)}) collective-permute-start(f32[256,128]{1,0:T(8,128)S(1)} %get-tuple-element.47.xb_ref), channel_id=1, source_target_pairs={{0,8},{8,16},{16,24},{24,0},{1,9},{9,17},{17,25},{25,1},{2,10},{10... | collective-permute-start | bytes 393224 | tf_op jit(solution)/shard_map/ppermute | solution.py:167
  8.1 2.2 %shard_map.83 = (f32[512,128]{1,0:T(8,128)S(1)}, f32[512,128]{1,0:T(8,128)S(1)}, f32[64,128]{1,0:T(8,128)S(1)}, f32[32,128]{1,0:T(8,128)S(1)}, f32[32,128]{1,0:T...) custom-call(f32[256,128]{1,0:T(8,128)S(1)} %get-tuple-element.48.xa_, ...), custom_call_target="tpu_custom_call" | custom-call | flops 2000000000 | bytes 1048576 | tf_op jit(solution)/shard_map/pallas_call | solution.py:24
  10.3 0.0 collective-permute-done.re_ref
  10.3 0.0 collective-permute-done.1.ro_ref
  10.3 2.2 %collective-permute-done.2.b_ref = f32[256,128]{1,0:T(8,128)S(1)} collective-permute-done((f32[256,128]{1,0:T(8,128)S(1)}, f32[256,128]{1,0:T(8,128)S(1)}, u32[]{:S(2)}, u32[]{:S(2)}) %collective-permute-start.2) | collective-permute-done | bytes 131104 | tf_op jit(solution)/shard_map/ppermute | solution.py:167
  12.4 0.5 %shard_map.84 = (f32[32,128]{1,0:T(8,128)S(1)}, f32[32,128]{1,0:T(8,128)S(1)}) custom-call(f32[32,128]{1,0:T(8,128)S(1)} %collective-permute-done.re_ref, f32[32,128]{1,0:T(8,128)S(1)} %collective-permute-done.1.ro_ref, f32[256,128]{1,0:T(8,128)S(1)} %collective-permute-done.2.b_ref, f32[64,128]{1,0:T(8,128)S(1)} %get-tuple-element.54.psent_ref, ...), custom_call_target="tpu_custom_call" | custom-call | flops 10000000 | bytes 1048576 | tf_op jit(solution)/shard_map/pallas_call | solution.py:24
  12.9 0.1 collective-permute-start.6
  13.0 0.9 %shard_map.85 = (f32[512,128]{1,0:T(8,128)S(1)}, f32[16,128]{1,0:T(8,128)S(1)}) custom-call(f32[32,128]{1,0:T(8,128)S(1)} %collective-permute-done.re_ref, f32[32,128]{1,0:T(8,128)S(1)} %collective-permute-done.1.ro_ref, f32[256,128]{1,0:T(8,128)S(1)} %collective-permute-done.2.b_ref, f32[512,128]{1,0:T(8,128)S(1)} %get-tuple-element.53.part_ref, ...), custom_call_target="tpu_custom_call" | custom-call | flops 200000000 | bytes 1048576 | tf_op jit(solution)/shard_map/pallas_call | solution.py:24
  13.9 0.3 collective-permute-done.6.re_ref
  14.2 0.3 shard_map.87
  14.5 0.7 %collective-permute-start.7 = (f32[80,128]{1,0:T(8,128)S(1)}, f32[80,128]{1,0:T(8,128)S(1)}, u32[]{:S(2)}, u32[]{:S(2)}) collective-permute-start(f32[80,128]{1,0:T(8,128)S(1)} %shard_map.87), channel_id=1, source_target_pairs={{0,7},{1,2},{2,1},{3,4},{4,3},{5,6},{6,5},{7,0},{8,15},{9,10},{10,... | collective-permute-start | bytes 122888 | tf_op jit(solution)/shard_map/ppermute | solution.py:164
  15.2 0.6 %shard_map.86.wp_ref = f32[256,128]{1,0:T(8,128)S(1)} custom-call(f32[512,128]{1,0:T(8,128)S(1)} %get-tuple-element.64.v1_ref, f32[512,128]{1,0:T(8,128)S(1)} %get-tuple-element.65.v_ref, bf16[9,256,256]{2,1,0:T(8,128)(2,1)S(1)} %get-tuple-element.56.w_ref.refs_9_, bf16[1024,256]{1,0:T(8,128)(2,1)S(1)} %get-tuple-element.66.pick_ref, ...), custom_call_target="tpu_custom_call" | custom-call | flops 1000000000 | bytes 1048576 | tf_op jit(solution)/shard_map/pallas_call | solution.py:24
  15.7 1.6 %collective-permute-start.5 = (f32[256,128]{1,0:T(8,128)S(1)}, f32[256,128]{1,0:T(8,128)S(1)}, u32[]{:S(2)}, u32[]{:S(2)}) collective-permute-start(f32[256,128]{1,0:T(8,128)S(1)} %shard_map.86.wp_ref), channel_id=1, source_target_pairs={{0,24},{8,0},{16,8},{24,16},{1,25},{9,1},{17,9},{25,17},{2,26},{10... | collective-permute-start | bytes 393224 | tf_op jit(solution)/shard_map/ppermute | solution.py:167
  17.3 0.5 %collective-permute-start.4 = (f32[256,128]{1,0:T(8,128)S(1)}, f32[256,128]{1,0:T(8,128)S(1)}, u32[]{:S(2)}, u32[]{:S(2)}) collective-permute-start(f32[256,128]{1,0:T(8,128)S(1)} %shard_map.86.wp_ref), channel_id=1, source_target_pairs={{0,16},{8,24},{16,0},{24,8},{1,17},{9,25},{17,1},{25,9},{2,18},{10... | collective-permute-start | bytes 393224 | tf_op jit(solution)/shard_map/ppermute | solution.py:167
  17.8 1.5 %collective-permute-start.3 = (f32[256,128]{1,0:T(8,128)S(1)}, f32[256,128]{1,0:T(8,128)S(1)}, u32[]{:S(2)}, u32[]{:S(2)}) collective-permute-start(f32[256,128]{1,0:T(8,128)S(1)} %shard_map.86.wp_ref), channel_id=1, source_target_pairs={{0,8},{8,16},{16,24},{24,0},{1,9},{9,17},{17,25},{25,1},{2,10},{10... | collective-permute-start | bytes 393224 | tf_op jit(solution)/shard_map/ppermute | solution.py:167
  19.3 0.4 %collective-permute-done.7.ro_ref.refs_8_ = f32[80,128]{1,0:T(8,128)S(1)} collective-permute-done((f32[80,128]{1,0:T(8,128)S(1)}, f32[80,128]{1,0:T(8,128)S(1)}, u32[]{:S(2)}, u32[]{:S(2)}) %collective-permute-start.7) | collective-permute-done | bytes 40992 | tf_op jit(solution)/shard_map/ppermute | solution.py:164
  19.7 0.4 shard_map.88
  20.1 1.6 %collective-permute-start.10 = (f32[48,128]{1,0:T(8,128)S(1)}, f32[48,128]{1,0:T(8,128)S(1)}, u32[]{:S(2)}, u32[]{:S(2)}) collective-permute-start(f32[48,128]{1,0:T(8,128)S(1)} %get-tuple-element.71.refs_7_), channel_id=1, source_target_pairs={{0,24},{8,0},{16,8},{24,16},{1,25},{9,1},{17,9},{25,17},{2,26},{10... | collective-permute-start | bytes 73736 | tf_op jit(solution)/shard_map/ppermute | solution.py:167
  21.7 1.0 %collective-permute-start.9 = (f32[48,128]{1,0:T(8,128)S(1)}, f32[48,128]{1,0:T(8,128)S(1)}, u32[]{:S(2)}, u32[]{:S(2)}) collective-permute-start(f32[48,128]{1,0:T(8,128)S(1)} %get-tuple-element.71.refs_7_), channel_id=1, source_target_pairs={{0,16},{8,24},{16,0},{24,8},{1,17},{9,25},{17,1},{25,9},{2,18},{10... | collective-permute-start | bytes 73736 | tf_op jit(solution)/shard_map/ppermute | solution.py:167
  22.7 0.2 shard_map.94
  22.9 1.2 %collective-permute-done.10.refs_5_ = f32[48,128]{1,0:T(8,128)S(1)} collective-permute-done((f32[48,128]{1,0:T(8,128)S(1)}, f32[48,128]{1,0:T(8,128)S(1)}, u32[]{:S(2)}, u32[]{:S(2)}) %collective-permute-start.10) | collective-permute-done | bytes 24608 | tf_op jit(solution)/shard_map/ppermute | solution.py:167
  24.1 1.9 %collective-permute-start.14 = (f32[256,128]{1,0:T(8,128)S(1)}, f32[256,128]{1,0:T(8,128)S(1)}, u32[]{:S(2)}, u32[]{:S(2)}) collective-permute-start(f32[256,128]{1,0:T(8,128)S(1)} %shard_map.94), channel_id=1, source_target_pairs={{0,8},{8,16},{16,24},{24,0},{1,9},{9,17},{17,25},{25,1},{2,10},{10... | collective-permute-start | bytes 393224 | tf_op jit(solution)/shard_map/ppermute | solution.py:167
  26.0 0.0 collective-permute-done.9.refs_4_
  26.0 1.1 %collective-permute-start.8 = (f32[48,128]{1,0:T(8,128)S(1)}, f32[48,128]{1,0:T(8,128)S(1)}, u32[]{:S(2)}, u32[]{:S(2)}) collective-permute-start(f32[48,128]{1,0:T(8,128)S(1)} %get-tuple-element.71.refs_7_), channel_id=1, source_target_pairs={{0,8},{8,16},{16,24},{24,0},{1,9},{9,17},{17,25},{25,1},{2,10},{10... | collective-permute-start | bytes 73736 | tf_op jit(solution)/shard_map/ppermute | solution.py:167
  27.1 1.3 %shard_map.89 = (f32[256,128]{1,0:T(8,128)S(1)}, f32[256,128]{1,0:T(8,128)S(1)}, f32[64,128]{1,0:T(8,128)S(1)}, f32[256,128]{1,0:T(8,128)S(1)}) custom-call(bf16[128,512]{1,0:T(8,128)(2,1)S(1)} %get-tuple-element.72.table_ref, f32[256,128]{1,0:T(8,128)S(1)} %shard_map.86.wp_ref, f32[512,128]{1,0:T(8,128)S(1)} %get-tuple-element.64.v1_ref, ...), custom_call_target="tpu_custom_call" | custom-call | flops 1000000000 | bytes 1048576 | tf_op jit(solution)/shard_map/pallas_call | solution.py:24
  28.3 2.4 %collective-permute-done.8.refs_3_ = f32[48,128]{1,0:T(8,128)S(1)} collective-permute-done((f32[48,128]{1,0:T(8,128)S(1)}, f32[48,128]{1,0:T(8,128)S(1)}, u32[]{:S(2)}, u32[]{:S(2)}) %collective-permute-start.8) | collective-permute-done | bytes 24608 | tf_op jit(solution)/shard_map/ppermute | solution.py:167
  30.7 0.0 collective-permute-done.5.refs_2_
  30.7 0.0 collective-permute-done.4.refs_1_
  30.7 0.0 collective-permute-done.3.refs_0_
  30.7 0.6 %shard_map.90 = (f32[256,128]{1,0:T(8,128)S(1)}, f32[256,128]{1,0:T(8,128)S(1)}, f32[64,128]{1,0:T(8,128)S(1)}, f32[32,128]{1,0:T(8,128)S(1)}, f32[32,128]{1,0:T(8,128)S(1)}) custom-call(f32[256,128]{1,0:T(8,128)S(1)} %collective-permute-done.3.refs_0_, f32[256,128]{1,0:T(8,128)S(1)} %collective-permute-done.4.refs_1_, ...), custom_call_target="tpu_custom_call" | custom-call | flops 100000000 | bytes 1048576 | tf_op jit(solution)/shard_map/pallas_call | solution.py:24
  31.4 0.0 collective-permute-start.11
  31.4 0.6 %shard_map.93.g_ref = f32[256,128]{1,0:T(8,128)S(1)} custom-call(f32[256,128]{1,0:T(8,128)S(1)} %get-tuple-element.77.c_ref.c_in, bf16[9,256,256]{2,1,0:T(8,128)(2,1)S(1)} %get-tuple-element.56.w_ref.refs_9_, bf16[1024,256]{1,0:T(8,128)(2,1)S(1)} %get-tuple-element.66.pick_ref), custom_call_target="tpu_custom_call" | custom-call | flops 300000000 | bytes 1048576 | tf_op jit(solution)/shard_map/pallas_call | solution.py:24
  32.0 0.4 shard_map.91.psent_ref
  32.4 0.2 collective-permute-done.11.re_ref
  32.6 0.3 shard_map.92
  32.9 0.4 collective-permute-start.12
  33.2 3.0 %collective-permute-start.13 = (f32[32,128]{1,0:T(8,128)S(1)}, f32[32,128]{1,0:T(8,128)S(1)}, u32[]{:S(2)}, u32[]{:S(2)}) collective-permute-start(f32[32,128]{1,0:T(8,128)S(1)} %get-tuple-element.81), channel_id=1, source_target_pairs={{0,7},{1,2},{2,1},{3,4},{4,3},{5,6},{6,5},{7,0},{8,15},{9,10},{10,... | collective-permute-start | bytes 49160 | tf_op jit(solution)/shard_map/ppermute | solution.py:164
  36.2 0.0 collective-permute-done.14.xb_ref
  36.2 1.8 %shard_map.95.p_ref = f32[512,128]{1,0:T(8,128)S(1)} custom-call(f32[32,128]{1,0:T(8,128)S(1)} %collective-permute-done.11.re_ref, f32[32,128]{1,0:T(8,128)S(1)} %get-tuple-element.76.ro_ref, f32[256,128]{1,0:T(8,128)S(1)} %get-tuple-element.77.c_ref.c_in, f32[256,128]{1,0:T(8,128)S(1)} %get-tuple-element.82.d_in, f32[256,128]{1,0:T(8,128)S(1)} %shard_map.93.g_ref, ...), custom_call_target="tpu_custom_call" | custom-call | flops 2000000000 | bytes 1048576 | tf_op jit(solution)/shard_map/pallas_call | solution.py:24
  38.1 0.0 collective-permute-done.12.re_ref
  38.1 0.3 collective-permute-done.13.ro_ref
  38.3 1.1 %shard_map.96 = f32[512,128]{1,0:T(8,128)} custom-call(f32[32,128]{1,0:T(8,128)S(1)} %collective-permute-done.12.re_ref, f32[32,128]{1,0:T(8,128)S(1)} %collective-permute-done.13.ro_ref, f32[512,128]{1,0:T(8,128)S(1)} %shard_map.95.p_ref, bf16[9,256,256]{2,1,0:T(8,128)(2,1)S(1)} %get-tuple-element.56.w_ref.refs_9_, ...), custom_call_target="tpu_custom_call" | custom-call | flops 10000000 | bytes 1048576 | tf_op jit(solution)/shard_map/pallas_call | solution.py:24
Async XLA Ops:
  1.3 9.0 %collective-permute-start = (f32[32,128]{1,0:T(8,128)S(1)}, f32[32,128]{1,0:T(8,128)S(1)}, u32[]{:S(2)}, u32[]{:S(2)}) collective-permute-start(f32[32,128]{1,0:T(8,128)S(1)} %get-tuple-element.45), channel_id=1, source_target_pairs={{0,1},{1,0},{2,3},{3,2},{4,5},{5,4},{6,7},{7,6},{8,9},{9,8},{10,11... | collective-permute-start | bytes 49160 | tf_op jit(solution)/shard_map/ppermute | solution.py:161
  1.9 8.4 %collective-permute-start.1 = (f32[32,128]{1,0:T(8,128)S(1)}, f32[32,128]{1,0:T(8,128)S(1)}, u32[]{:S(2)}, u32[]{:S(2)}) collective-permute-start(f32[32,128]{1,0:T(8,128)S(1)} %get-tuple-element.46.o0_ref), channel_id=1, source_target_pairs={{0,7},{1,2},{2,1},{3,4},{4,3},{5,6},{6,5},{7,0},{8,15},{9,10},{10,... | collective-permute-start | bytes 49160 | tf_op jit(solution)/shard_map/ppermute | solution.py:164
  6.6 5.9 %collective-permute-start.2 = (f32[256,128]{1,0:T(8,128)S(1)}, f32[256,128]{1,0:T(8,128)S(1)}, u32[]{:S(2)}, u32[]{:S(2)}) collective-permute-start(f32[256,128]{1,0:T(8,128)S(1)} %get-tuple-element.47.xb_ref), channel_id=1, source_target_pairs={{0,8},{8,16},{16,24},{24,0},{1,9},{9,17},{17,25},{25,1},{2,10},{10... | collective-permute-start | bytes 393224 | tf_op jit(solution)/shard_map/ppermute | solution.py:167
  12.9 1.2 %collective-permute-start.6 = (f32[32,128]{1,0:T(8,128)S(1)}, f32[32,128]{1,0:T(8,128)S(1)}, u32[]{:S(2)}, u32[]{:S(2)}) collective-permute-start(f32[32,128]{1,0:T(8,128)S(1)} %get-tuple-element.68), channel_id=1, source_target_pairs={{0,1},{1,0},{2,3},{3,2},{4,5},{5,4},{6,7},{7,6},{8,9},{9,8},{10,11... | collective-permute-start | bytes 49160 | tf_op jit(solution)/shard_map/ppermute | solution.py:161
  14.5 5.2 %collective-permute-start.7 = (f32[80,128]{1,0:T(8,128)S(1)}, f32[80,128]{1,0:T(8,128)S(1)}, u32[]{:S(2)}, u32[]{:S(2)}) collective-permute-start(f32[80,128]{1,0:T(8,128)S(1)} %shard_map.87), channel_id=1, source_target_pairs={{0,7},{1,2},{2,1},{3,4},{4,3},{5,6},{6,5},{7,0},{8,15},{9,10},{10,... | collective-permute-start | bytes 122888 | tf_op jit(solution)/shard_map/ppermute | solution.py:164
  15.7 15.0 %collective-permute-start.5 = (f32[256,128]{1,0:T(8,128)S(1)}, f32[256,128]{1,0:T(8,128)S(1)}, u32[]{:S(2)}, u32[]{:S(2)}) collective-permute-start(f32[256,128]{1,0:T(8,128)S(1)} %shard_map.86.wp_ref), channel_id=1, source_target_pairs={{0,24},{8,0},{16,8},{24,16},{1,25},{9,1},{17,9},{25,17},{2,26},{10... | collective-permute-start | bytes 393224 | tf_op jit(solution)/shard_map/ppermute | solution.py:167
  17.3 13.4 %collective-permute-start.4 = (f32[256,128]{1,0:T(8,128)S(1)}, f32[256,128]{1,0:T(8,128)S(1)}, u32[]{:S(2)}, u32[]{:S(2)}) collective-permute-start(f32[256,128]{1,0:T(8,128)S(1)} %shard_map.86.wp_ref), channel_id=1, source_target_pairs={{0,16},{8,24},{16,0},{24,8},{1,17},{9,25},{17,1},{25,9},{2,18},{10... | collective-permute-start | bytes 393224 | tf_op jit(solution)/shard_map/ppermute | solution.py:167
  17.8 12.9 %collective-permute-start.3 = (f32[256,128]{1,0:T(8,128)S(1)}, f32[256,128]{1,0:T(8,128)S(1)}, u32[]{:S(2)}, u32[]{:S(2)}) collective-permute-start(f32[256,128]{1,0:T(8,128)S(1)} %shard_map.86.wp_ref), channel_id=1, source_target_pairs={{0,8},{8,16},{16,24},{24,0},{1,9},{9,17},{17,25},{25,1},{2,10},{10... | collective-permute-start | bytes 393224 | tf_op jit(solution)/shard_map/ppermute | solution.py:167
  20.1 4.0 %collective-permute-start.10 = (f32[48,128]{1,0:T(8,128)S(1)}, f32[48,128]{1,0:T(8,128)S(1)}, u32[]{:S(2)}, u32[]{:S(2)}) collective-permute-start(f32[48,128]{1,0:T(8,128)S(1)} %get-tuple-element.71.refs_7_), channel_id=1, source_target_pairs={{0,24},{8,0},{16,8},{24,16},{1,25},{9,1},{17,9},{25,17},{2,26},{10... | collective-permute-start | bytes 73736 | tf_op jit(solution)/shard_map/ppermute | solution.py:167
  21.7 4.3 %collective-permute-start.9 = (f32[48,128]{1,0:T(8,128)S(1)}, f32[48,128]{1,0:T(8,128)S(1)}, u32[]{:S(2)}, u32[]{:S(2)}) collective-permute-start(f32[48,128]{1,0:T(8,128)S(1)} %get-tuple-element.71.refs_7_), channel_id=1, source_target_pairs={{0,16},{8,24},{16,0},{24,8},{1,17},{9,25},{17,1},{25,9},{2,18},{10... | collective-permute-start | bytes 73736 | tf_op jit(solution)/shard_map/ppermute | solution.py:167
  24.1 12.1 %collective-permute-start.14 = (f32[256,128]{1,0:T(8,128)S(1)}, f32[256,128]{1,0:T(8,128)S(1)}, u32[]{:S(2)}, u32[]{:S(2)}) collective-permute-start(f32[256,128]{1,0:T(8,128)S(1)} %shard_map.94), channel_id=1, source_target_pairs={{0,8},{8,16},{16,24},{24,0},{1,9},{9,17},{17,25},{25,1},{2,10},{10... | collective-permute-start | bytes 393224 | tf_op jit(solution)/shard_map/ppermute | solution.py:167
  26.0 4.7 %collective-permute-start.8 = (f32[48,128]{1,0:T(8,128)S(1)}, f32[48,128]{1,0:T(8,128)S(1)}, u32[]{:S(2)}, u32[]{:S(2)}) collective-permute-start(f32[48,128]{1,0:T(8,128)S(1)} %get-tuple-element.71.refs_7_), channel_id=1, source_target_pairs={{0,8},{8,16},{16,24},{24,0},{1,9},{9,17},{17,25},{25,1},{2,10},{10... | collective-permute-start | bytes 73736 | tf_op jit(solution)/shard_map/ppermute | solution.py:167
  31.4 1.2 %collective-permute-start.11 = (f32[32,128]{1,0:T(8,128)S(1)}, f32[32,128]{1,0:T(8,128)S(1)}, u32[]{:S(2)}, u32[]{:S(2)}) collective-permute-start(f32[32,128]{1,0:T(8,128)S(1)} %get-tuple-element.75), channel_id=1, source_target_pairs={{0,1},{1,0},{2,3},{3,2},{4,5},{5,4},{6,7},{7,6},{8,9},{9,8},{10,11... | collective-permute-start | bytes 49160 | tf_op jit(solution)/shard_map/ppermute | solution.py:161
  32.9 5.2 %collective-permute-start.12 = (f32[32,128]{1,0:T(8,128)S(1)}, f32[32,128]{1,0:T(8,128)S(1)}, u32[]{:S(2)}, u32[]{:S(2)}) collective-permute-start(f32[32,128]{1,0:T(8,128)S(1)} %get-tuple-element.80), channel_id=1, source_target_pairs={{0,1},{1,0},{2,3},{3,2},{4,5},{5,4},{6,7},{7,6},{8,9},{9,8},{10,11... | collective-permute-start | bytes 49160 | tf_op jit(solution)/shard_map/ppermute | solution.py:161
  33.2 5.1 %collective-permute-start.13 = (f32[32,128]{1,0:T(8,128)S(1)}, f32[32,128]{1,0:T(8,128)S(1)}, u32[]{:S(2)}, u32[]{:S(2)}) collective-permute-start(f32[32,128]{1,0:T(8,128)S(1)} %get-tuple-element.81), channel_id=1, source_target_pairs={{0,7},{1,2},{2,1},{3,4},{4,3},{5,6},{6,5},{7,0},{8,15},{9,10},{10,... | collective-permute-start | bytes 49160 | tf_op jit(solution)/shard_map/ppermute | solution.py:164

commit v7 on v6

--- a/solution.py
+++ b/solution.py
@@ -173,6 +173,13 @@
             term = dot(picked, w_ref[W_FACE + f])
             near = term if near is None else near + term
         return halves(near)
+
+    def unpacked(block):
+        even = lax.axis_index("space") % 2 == 0
+        low = lax.broadcasted_iota(jnp.int32, block.shape, 1) % sent < halo
+        kept = jnp.where(low, jnp.where(even, 0.0, 1.0), jnp.where(even, 1.0, 0.0))
+        factor = jnp.where(even, block[:, :1], block[:, halo : halo + 1])
+        return (block * kept).astype(BF16), jnp.broadcast_to(factor, (halo, width))
 
     def sent_at(send_ref, i):
         first = jnp.where(lax.axis_index("space") % 2 == 0, halo, 0)
@@ -319,7 +326,7 @@
         near_half = lax.broadcasted_iota(jnp.int32, (halo, far), 1) % sent < halo
         even = lax.axis_index("space") % 2 == 0
         kept = jnp.where(near_half, jnp.where(even, 1.0, 0.0), jnp.where(even, 0.0, 1.0))
-        qo_ref[...] = qs[halo:] * kept
+        qo_ref[...] = qs[halo:] * kept + got[slabs + 1][halo:] * (1.0 - kept)
 
     (
         v0, part1, psent1, sig_sent, frac_sent, weights, pick, pick_sent, q_all, q_sent, q_o, choose,
@@ -406,12 +413,11 @@
         frac = fracs_ref[halo:, :]
         o_ref[: slabs * halo, :] = vo_ref[...]
         o_ref[slabs * halo : (slabs + 1) * halo, :] = wo_ref[...] + frac * add
-        o_ref[(slabs + 1) * halo : (slabs + 2) * halo, :] = qo_ref[...]
-        o_ref[(slabs + 2) * halo :, :] = frac
+        o_ref[(slabs + 1) * halo :, :] = qo_ref[...]
 
     (o1,) = call(
         edge_w,
-        [(((slabs + 3) * halo, width), F32)],
+        [(((slabs + 2) * halo, width), F32)],
         [re1, w_part, vo, weights, q_sent, frac_sent, q_o],
         flops=1e7,
     )
@@ -453,14 +459,9 @@
         even = lax.axis_index("space") % 2 == 0
         w_out[:halo, :] = jnp.where(even, late[halo:], late[:halo])
         w_out[halo:sent, :] = jnp.where(even, late[:halo], late[halo:])
-        mine = spread(
-            ro_ref[(slabs + 1) * halo : (slabs + 2) * halo, :].astype(BF16),
-            table[:, slabs * lanes :],
-            1,
-        )[0]
-        w_out[sent:, :] = (
-            ro_ref[slabs * halo : (slabs + 1) * halo, :] + ro_ref[(slabs + 2) * halo :, :] * mine
-        )
+        chosen, factor = unpacked(ro_ref[(slabs + 1) * halo :, :])
+        mine = spread(chosen, table[:, slabs * lanes :], 1)[0]
+        w_out[sent:, :] = ro_ref[slabs * halo : (slabs + 1) * halo, :] + factor * mine
         table_ref[...] = table[:, : slabs * lanes]
 
     w_late, table1 = call(
@@ -510,19 +511,20 @@
             jnp.concatenate([x[...] + fix, y[sent:, :]], axis=0)
             for x, y, fix in zip(earlies, lates, fixes)
         ]
-        frac = jnp.concatenate([frac_ref[...], ro_ref[(slabs + 2) * halo :, :]], axis=0)
+        frac = jnp.concatenate(
+            [frac_ref[...], unpacked(ro_ref[(slabs + 1) * halo :, :])[1]], axis=0
+        )
         c = jnp.concatenate(
             [c0_ref[...], late_ref[sent:, :] - ro_ref[(slabs - 1) * halo : slabs * halo, :]], axis=0
         )
         d = time_mask(olds[0])
         power = frac
         for a in range(1, groups):
-            cut = split(time_mask(power * olds[a - 1], a))
-            c = c + product(cut, w_ref[W_TIME + a - 1])
-            if a < groups - 1:
-                cut = split(time_mask(power * olds[a], a + 1))
-                d = d + product(cut, w_ref[W_TIME + a - 1])
+            cut = split(time_mask(olds[a - 1], a))
+            if a > 1:
+                d = d + power * product(cut, w_ref[W_TIME + a - 2])
                 power = power * frac
+            c = c + power * product(cut, w_ref[W_TIME + a - 1])
         c_ref[...] = c[:elements]
         d_ref[...] = d[:elements]
         oh_ref[:halo, :] = c[elements:]

time: 39.6 us -> 39.6 us (level)
  no operation moved by 1% of the time
where the time goes in v7:
time: 39.6 us; the launch traced here: 39.4 us
  starting transfers between devices  20 us (51%)
  Pallas kernels  12.5 us (32%)
  waiting for transfers between devices  6.87 us (17%)
    pallas_call x15, Pallas kernels, call(): pl.pallas_call(kernel, out_shape=[jax.ShapeDtypeStruct(s, d) for s, d in...  12.5 us
    ppermute x8, starting transfers between devices, later(): lax.ppermute(x, 'tm', [(i, (i + by) % groups) for i in range(groups)])  10.7 us
    ppermute x3, starting transfers between devices, over_o(): return lax.ppermute(x, 'space', swap_o)  8.25 us
    ppermute x8, waiting for transfers between devices, later(): lax.ppermute(x, 'tm', [(i, (i + by) % groups) for i in range(groups)])  5.84 us
    ppermute x4, starting transfers between devices, over_e(): return lax.ppermute(x, 'space', swap_e)  1.02 us
  transfers between devices with their start and end apart: 15, of which 7 were waited for; matrix products, arithmetic and copies ran while one was open for 0% of the time, Pallas kernels for 23%

profile of v7, /device:TPU:0, one launch (start us, length us, event | category | flops | bytes accessed | tf_op | source)
XLA Modules:
  0.0 39.4 jit_solution(1100912381632408571)
XLA Ops:
  0.0 1.3 %shard_map.82 = (f32[32,128]{1,0:T(8,128)S(1)}, f32[32,128]{1,0:T(8,128)S(1)}, f32[256,128]{1,0:T(8,128)S(1)}, f32[256,128]{1,0:T(8,128)S(1)}, f32[256,128]{1,0:...) custom-call(f32[512,128]{1,0:T(8,128)} %bitcast.5, f32[1,256]{1,0:T(1,128)} %bitcast.8, ...), custom_call_target="tpu_custom_call" | custom-call | flops 10000000 | bytes 1048576 | tf_op jit(solution)/shard_map/pallas_call | solution.py:24
  1.3 0.6 %collective-permute-start = (f32[32,128]{1,0:T(8,128)S(1)}, f32[32,128]{1,0:T(8,128)S(1)}, u32[]{:S(2)}, u32[]{:S(2)}) collective-permute-start(f32[32,128]{1,0:T(8,128)S(1)} %get-tuple-element.45), channel_id=1, source_target_pairs={{0,1},{1,0},{2,3},{3,2},{4,5},{5,4},{6,7},{7,6},{8,9},{9,8},{10,11... | collective-permute-start | bytes 49160 | tf_op jit(solution)/shard_map/ppermute | solution.py:161
  1.9 4.7 %collective-permute-start.1 = (f32[32,128]{1,0:T(8,128)S(1)}, f32[32,128]{1,0:T(8,128)S(1)}, u32[]{:S(2)}, u32[]{:S(2)}) collective-permute-start(f32[32,128]{1,0:T(8,128)S(1)} %get-tuple-element.46.o0_ref), channel_id=1, source_target_pairs={{0,7},{1,2},{2,1},{3,4},{4,3},{5,6},{6,5},{7,0},{8,15},{9,10},{10,... | collective-permute-start | bytes 49160 | tf_op jit(solution)/shard_map/ppermute | solution.py:164
  6.6 1.5 %collective-permute-start.2 = (f32[256,128]{1,0:T(8,128)S(1)}, f32[256,128]{1,0:T(8,128)S(1)}, u32[]{:S(2)}, u32[]{:S(2)}) collective-permute-start(f32[256,128]{1,0:T(8,128)S(1)} %get-tuple-element.47.xb_ref), channel_id=1, source_target_pairs={{0,8},{8,16},{16,24},{24,0},{1,9},{9,17},{17,25},{25,1},{2,10},{10... | collective-permute-start | bytes 393224 | tf_op jit(solution)/shard_map/ppermute | solution.py:167
  8.1 2.2 %shard_map.83 = (f32[512,128]{1,0:T(8,128)S(1)}, f32[512,128]{1,0:T(8,128)S(1)}, f32[64,128]{1,0:T(8,128)S(1)}, f32[32,128]{1,0:T(8,128)S(1)}, f32[32,128]{1,0:T...) custom-call(f32[256,128]{1,0:T(8,128)S(1)} %get-tuple-element.48.xa_, ...), custom_call_target="tpu_custom_call" | custom-call | flops 2000000000 | bytes 1048576 | tf_op jit(solution)/shard_map/pallas_call | solution.py:24
  10.3 0.0 collective-permute-done.re_ref
  10.3 0.0 collective-permute-done.1.ro_ref
  10.3 2.2 %collective-permute-done.2.b_ref = f32[256,128]{1,0:T(8,128)S(1)} collective-permute-done((f32[256,128]{1,0:T(8,128)S(1)}, f32[256,128]{1,0:T(8,128)S(1)}, u32[]{:S(2)}, u32[]{:S(2)}) %collective-permute-start.2) | collective-permute-done | bytes 131104 | tf_op jit(solution)/shard_map/ppermute | solution.py:167
  12.4 0.5 %shard_map.84 = (f32[32,128]{1,0:T(8,128)S(1)}, f32[32,128]{1,0:T(8,128)S(1)}) custom-call(f32[32,128]{1,0:T(8,128)S(1)} %collective-permute-done.re_ref, f32[32,128]{1,0:T(8,128)S(1)} %collective-permute-done.1.ro_ref, f32[256,128]{1,0:T(8,128)S(1)} %collective-permute-done.2.b_ref, f32[64,128]{1,0:T(8,128)S(1)} %get-tuple-element.54.psent_ref, ...), custom_call_target="tpu_custom_call" | custom-call | flops 10000000 | bytes 1048576 | tf_op jit(solution)/shard_map/pallas_call | solution.py:24
  12.9 0.1 collective-permute-start.6
  13.0 0.9 %shard_map.85 = (f32[512,128]{1,0:T(8,128)S(1)}, f32[16,128]{1,0:T(8,128)S(1)}) custom-call(f32[32,128]{1,0:T(8,128)S(1)} %collective-permute-done.re_ref, f32[32,128]{1,0:T(8,128)S(1)} %collective-permute-done.1.ro_ref, f32[256,128]{1,0:T(8,128)S(1)} %collective-permute-done.2.b_ref, f32[512,128]{1,0:T(8,128)S(1)} %get-tuple-element.53.part_ref, ...), custom_call_target="tpu_custom_call" | custom-call | flops 200000000 | bytes 1048576 | tf_op jit(solution)/shard_map/pallas_call | solution.py:24
  13.9 0.3 collective-permute-done.6.re_ref
  14.2 0.3 shard_map.87
  14.5 0.7 %collective-permute-start.7 = (f32[64,128]{1,0:T(8,128)S(1)}, f32[64,128]{1,0:T(8,128)S(1)}, u32[]{:S(2)}, u32[]{:S(2)}) collective-permute-start(f32[64,128]{1,0:T(8,128)S(1)} %shard_map.87), channel_id=1, source_target_pairs={{0,7},{1,2},{2,1},{3,4},{4,3},{5,6},{6,5},{7,0},{8,15},{9,10},{10,... | collective-permute-start | bytes 98312 | tf_op jit(solution)/shard_map/ppermute | solution.py:164
  15.2 0.6 %shard_map.86.wp_ref = f32[256,128]{1,0:T(8,128)S(1)} custom-call(f32[512,128]{1,0:T(8,128)S(1)} %get-tuple-element.64.v1_ref, f32[512,128]{1,0:T(8,128)S(1)} %get-tuple-element.65.v_ref, bf16[9,256,256]{2,1,0:T(8,128)(2,1)S(1)} %get-tuple-element.56.w_ref.refs_9_, bf16[1024,256]{1,0:T(8,128)(2,1)S(1)} %get-tuple-element.66.pick_ref, ...), custom_call_target="tpu_custom_call" | custom-call | flops 1000000000 | bytes 1048576 | tf_op jit(solution)/shard_map/pallas_call | solution.py:24
  15.7 1.6 %collective-permute-start.5 = (f32[256,128]{1,0:T(8,128)S(1)}, f32[256,128]{1,0:T(8,128)S(1)}, u32[]{:S(2)}, u32[]{:S(2)}) collective-permute-start(f32[256,128]{1,0:T(8,128)S(1)} %shard_map.86.wp_ref), channel_id=1, source_target_pairs={{0,24},{8,0},{16,8},{24,16},{1,25},{9,1},{17,9},{25,17},{2,26},{10... | collective-permute-start | bytes 393224 | tf_op jit(solution)/shard_map/ppermute | solution.py:167
  17.3 0.5 %collective-permute-start.4 = (f32[256,128]{1,0:T(8,128)S(1)}, f32[256,128]{1,0:T(8,128)S(1)}, u32[]{:S(2)}, u32[]{:S(2)}) collective-permute-start(f32[256,128]{1,0:T(8,128)S(1)} %shard_map.86.wp_ref), channel_id=1, source_target_pairs={{0,16},{8,24},{16,0},{24,8},{1,17},{9,25},{17,1},{25,9},{2,18},{10... | collective-permute-start | bytes 393224 | tf_op jit(solution)/shard_map/ppermute | solution.py:167
  17.8 1.5 %collective-permute-start.3 = (f32[256,128]{1,0:T(8,128)S(1)}, f32[256,128]{1,0:T(8,128)S(1)}, u32[]{:S(2)}, u32[]{:S(2)}) collective-permute-start(f32[256,128]{1,0:T(8,128)S(1)} %shard_map.86.wp_ref), channel_id=1, source_target_pairs={{0,8},{8,16},{16,24},{24,0},{1,9},{9,17},{17,25},{25,1},{2,10},{10... | collective-permute-start | bytes 393224 | tf_op jit(solution)/shard_map/ppermute | solution.py:167
  19.3 0.3 collective-permute-done.7.ro_ref.refs_8_
  19.6 0.4 shard_map.88
  20.0 1.6 %collective-permute-start.10 = (f32[48,128]{1,0:T(8,128)S(1)}, f32[48,128]{1,0:T(8,128)S(1)}, u32[]{:S(2)}, u32[]{:S(2)}) collective-permute-start(f32[48,128]{1,0:T(8,128)S(1)} %get-tuple-element.71.refs_7_), channel_id=1, source_target_pairs={{0,24},{8,0},{16,8},{24,16},{1,25},{9,1},{17,9},{25,17},{2,26},{10... | collective-permute-start | bytes 73736 | tf_op jit(solution)/shard_map/ppermute | solution.py:167
  21.6 1.1 %collective-permute-start.9 = (f32[48,128]{1,0:T(8,128)S(1)}, f32[48,128]{1,0:T(8,128)S(1)}, u32[]{:S(2)}, u32[]{:S(2)}) collective-permute-start(f32[48,128]{1,0:T(8,128)S(1)} %get-tuple-element.71.refs_7_), channel_id=1, source_target_pairs={{0,16},{8,24},{16,0},{24,8},{1,17},{9,25},{17,1},{25,9},{2,18},{10... | collective-permute-start | bytes 73736 | tf_op jit(solution)/shard_map/ppermute | solution.py:167
  22.7 0.2 shard_map.94
  22.9 1.2 %collective-permute-done.10.refs_5_ = f32[48,128]{1,0:T(8,128)S(1)} collective-permute-done((f32[48,128]{1,0:T(8,128)S(1)}, f32[48,128]{1,0:T(8,128)S(1)}, u32[]{:S(2)}, u32[]{:S(2)}) %collective-permute-start.10) | collective-permute-done | bytes 24608 | tf_op jit(solution)/shard_map/ppermute | solution.py:167
  24.1 1.9 %collective-permute-start.14 = (f32[256,128]{1,0:T(8,128)S(1)}, f32[256,128]{1,0:T(8,128)S(1)}, u32[]{:S(2)}, u32[]{:S(2)}) collective-permute-start(f32[256,128]{1,0:T(8,128)S(1)} %shard_map.94), channel_id=1, source_target_pairs={{0,8},{8,16},{16,24},{24,0},{1,9},{9,17},{17,25},{25,1},{2,10},{10... | collective-permute-start | bytes 393224 | tf_op jit(solution)/shard_map/ppermute | solution.py:167
  26.1 0.0 collective-permute-done.9.refs_4_
  26.1 1.0 %collective-permute-start.8 = (f32[48,128]{1,0:T(8,128)S(1)}, f32[48,128]{1,0:T(8,128)S(1)}, u32[]{:S(2)}, u32[]{:S(2)}) collective-permute-start(f32[48,128]{1,0:T(8,128)S(1)} %get-tuple-element.71.refs_7_), channel_id=1, source_target_pairs={{0,8},{8,16},{16,24},{24,0},{1,9},{9,17},{17,25},{25,1},{2,10},{10... | collective-permute-start | bytes 73736 | tf_op jit(solution)/shard_map/ppermute | solution.py:167
  27.1 1.3 %shard_map.89 = (f32[256,128]{1,0:T(8,128)S(1)}, f32[256,128]{1,0:T(8,128)S(1)}, f32[64,128]{1,0:T(8,128)S(1)}, f32[256,128]{1,0:T(8,128)S(1)}) custom-call(bf16[128,512]{1,0:T(8,128)(2,1)S(1)} %get-tuple-element.72.table_ref, f32[256,128]{1,0:T(8,128)S(1)} %shard_map.86.wp_ref, f32[512,128]{1,0:T(8,128)S(1)} %get-tuple-element.64.v1_ref, ...), custom_call_target="tpu_custom_call" | custom-call | flops 1000000000 | bytes 1048576 | tf_op jit(solution)/shard_map/pallas_call | solution.py:24
  28.3 2.5 %collective-permute-done.8.refs_3_ = f32[48,128]{1,0:T(8,128)S(1)} collective-permute-done((f32[48,128]{1,0:T(8,128)S(1)}, f32[48,128]{1,0:T(8,128)S(1)}, u32[]{:S(2)}, u32[]{:S(2)}) %collective-permute-start.8) | collective-permute-done | bytes 24608 | tf_op jit(solution)/shard_map/ppermute | solution.py:167
  30.8 0.0 collective-permute-done.5.refs_2_
  30.8 0.0 collective-permute-done.4.refs_1_
  30.8 0.0 collective-permute-done.3.refs_0_
  30.8 0.6 %shard_map.90 = (f32[256,128]{1,0:T(8,128)S(1)}, f32[256,128]{1,0:T(8,128)S(1)}, f32[64,128]{1,0:T(8,128)S(1)}, f32[32,128]{1,0:T(8,128)S(1)}, f32[32,128]{1,0:T(8,128)S(1)}) custom-call(f32[256,128]{1,0:T(8,128)S(1)} %collective-permute-done.3.refs_0_, f32[256,128]{1,0:T(8,128)S(1)} %collective-permute-done.4.refs_1_, ...), custom_call_target="tpu_custom_call" | custom-call | flops 100000000 | bytes 1048576 | tf_op jit(solution)/shard_map/pallas_call | solution.py:24
  31.4 0.0 collective-permute-start.11
  31.5 0.6 %shard_map.93.g_ref = f32[256,128]{1,0:T(8,128)S(1)} custom-call(f32[256,128]{1,0:T(8,128)S(1)} %get-tuple-element.77.c_ref.c_in, bf16[9,256,256]{2,1,0:T(8,128)(2,1)S(1)} %get-tuple-element.56.w_ref.refs_9_, bf16[1024,256]{1,0:T(8,128)(2,1)S(1)} %get-tuple-element.66.pick_ref), custom_call_target="tpu_custom_call" | custom-call | flops 300000000 | bytes 1048576 | tf_op jit(solution)/shard_map/pallas_call | solution.py:24
  32.1 0.4 shard_map.91.psent_ref
  32.5 0.2 collective-permute-done.11.re_ref
  32.6 0.3 shard_map.92
  32.9 0.4 collective-permute-start.12
  33.3 2.9 %collective-permute-start.13 = (f32[32,128]{1,0:T(8,128)S(1)}, f32[32,128]{1,0:T(8,128)S(1)}, u32[]{:S(2)}, u32[]{:S(2)}) collective-permute-start(f32[32,128]{1,0:T(8,128)S(1)} %get-tuple-element.81), channel_id=1, source_target_pairs={{0,7},{1,2},{2,1},{3,4},{4,3},{5,6},{6,5},{7,0},{8,15},{9,10},{10,... | collective-permute-start | bytes 49160 | tf_op jit(solution)/shard_map/ppermute | solution.py:164
  36.2 0.0 collective-permute-done.14.xb_ref
  36.2 1.9 %shard_map.95.p_ref = f32[512,128]{1,0:T(8,128)S(1)} custom-call(f32[32,128]{1,0:T(8,128)S(1)} %collective-permute-done.11.re_ref, f32[32,128]{1,0:T(8,128)S(1)} %get-tuple-element.76.ro_ref, f32[256,128]{1,0:T(8,128)S(1)} %get-tuple-element.77.c_ref.c_in, f32[256,128]{1,0:T(8,128)S(1)} %get-tuple-element.82.d_in, f32[256,128]{1,0:T(8,128)S(1)} %shard_map.93.g_ref, ...), custom_call_target="tpu_custom_call" | custom-call | flops 2000000000 | bytes 1048576 | tf_op jit(solution)/shard_map/pallas_call | solution.py:24
  38.0 0.0 collective-permute-done.12.re_ref
  38.0 0.3 collective-permute-done.13.ro_ref
  38.3 1.1 %shard_map.96 = f32[512,128]{1,0:T(8,128)} custom-call(f32[32,128]{1,0:T(8,128)S(1)} %collective-permute-done.12.re_ref, f32[32,128]{1,0:T(8,128)S(1)} %collective-permute-done.13.ro_ref, f32[512,128]{1,0:T(8,128)S(1)} %shard_map.95.p_ref, bf16[9,256,256]{2,1,0:T(8,128)(2,1)S(1)} %get-tuple-element.56.w_ref.refs_9_, ...), custom_call_target="tpu_custom_call" | custom-call | flops 10000000 | bytes 1048576 | tf_op jit(solution)/shard_map/pallas_call | solution.py:24
Async XLA Ops:
  1.3 9.0 %collective-permute-start = (f32[32,128]{1,0:T(8,128)S(1)}, f32[32,128]{1,0:T(8,128)S(1)}, u32[]{:S(2)}, u32[]{:S(2)}) collective-permute-start(f32[32,128]{1,0:T(8,128)S(1)} %get-tuple-element.45), channel_id=1, source_target_pairs={{0,1},{1,0},{2,3},{3,2},{4,5},{5,4},{6,7},{7,6},{8,9},{9,8},{10,11... | collective-permute-start | bytes 49160 | tf_op jit(solution)/shard_map/ppermute | solution.py:161
  1.9 8.4 %collective-permute-start.1 = (f32[32,128]{1,0:T(8,128)S(1)}, f32[32,128]{1,0:T(8,128)S(1)}, u32[]{:S(2)}, u32[]{:S(2)}) collective-permute-start(f32[32,128]{1,0:T(8,128)S(1)} %get-tuple-element.46.o0_ref), channel_id=1, source_target_pairs={{0,7},{1,2},{2,1},{3,4},{4,3},{5,6},{6,5},{7,0},{8,15},{9,10},{10,... | collective-permute-start | bytes 49160 | tf_op jit(solution)/shard_map/ppermute | solution.py:164
  6.6 5.9 %collective-permute-start.2 = (f32[256,128]{1,0:T(8,128)S(1)}, f32[256,128]{1,0:T(8,128)S(1)}, u32[]{:S(2)}, u32[]{:S(2)}) collective-permute-start(f32[256,128]{1,0:T(8,128)S(1)} %get-tuple-element.47.xb_ref), channel_id=1, source_target_pairs={{0,8},{8,16},{16,24},{24,0},{1,9},{9,17},{17,25},{25,1},{2,10},{10... | collective-permute-start | bytes 393224 | tf_op jit(solution)/shard_map/ppermute | solution.py:167
  12.9 1.2 %collective-permute-start.6 = (f32[32,128]{1,0:T(8,128)S(1)}, f32[32,128]{1,0:T(8,128)S(1)}, u32[]{:S(2)}, u32[]{:S(2)}) collective-permute-start(f32[32,128]{1,0:T(8,128)S(1)} %get-tuple-element.68), channel_id=1, source_target_pairs={{0,1},{1,0},{2,3},{3,2},{4,5},{5,4},{6,7},{7,6},{8,9},{9,8},{10,11... | collective-permute-start | bytes 49160 | tf_op jit(solution)/shard_map/ppermute | solution.py:161
  14.5 5.1 %collective-permute-start.7 = (f32[64,128]{1,0:T(8,128)S(1)}, f32[64,128]{1,0:T(8,128)S(1)}, u32[]{:S(2)}, u32[]{:S(2)}) collective-permute-start(f32[64,128]{1,0:T(8,128)S(1)} %shard_map.87), channel_id=1, source_target_pairs={{0,7},{1,2},{2,1},{3,4},{4,3},{5,6},{6,5},{7,0},{8,15},{9,10},{10,... | collective-permute-start | bytes 98312 | tf_op jit(solution)/shard_map/ppermute | solution.py:164
  15.7 15.1 %collective-permute-start.5 = (f32[256,128]{1,0:T(8,128)S(1)}, f32[256,128]{1,0:T(8,128)S(1)}, u32[]{:S(2)}, u32[]{:S(2)}) collective-permute-start(f32[256,128]{1,0:T(8,128)S(1)} %shard_map.86.wp_ref), channel_id=1, source_target_pairs={{0,24},{8,0},{16,8},{24,16},{1,25},{9,1},{17,9},{25,17},{2,26},{10... | collective-permute-start | bytes 393224 | tf_op jit(solution)/shard_map/ppermute | solution.py:167
  17.3 13.5 %collective-permute-start.4 = (f32[256,128]{1,0:T(8,128)S(1)}, f32[256,128]{1,0:T(8,128)S(1)}, u32[]{:S(2)}, u32[]{:S(2)}) collective-permute-start(f32[256,128]{1,0:T(8,128)S(1)} %shard_map.86.wp_ref), channel_id=1, source_target_pairs={{0,16},{8,24},{16,0},{24,8},{1,17},{9,25},{17,1},{25,9},{2,18},{10... | collective-permute-start | bytes 393224 | tf_op jit(solution)/shard_map/ppermute | solution.py:167
  17.8 13.0 %collective-permute-start.3 = (f32[256,128]{1,0:T(8,128)S(1)}, f32[256,128]{1,0:T(8,128)S(1)}, u32[]{:S(2)}, u32[]{:S(2)}) collective-permute-start(f32[256,128]{1,0:T(8,128)S(1)} %shard_map.86.wp_ref), channel_id=1, source_target_pairs={{0,8},{8,16},{16,24},{24,0},{1,9},{9,17},{17,25},{25,1},{2,10},{10... | collective-permute-start | bytes 393224 | tf_op jit(solution)/shard_map/ppermute | solution.py:167
  20.0 4.1 %collective-permute-start.10 = (f32[48,128]{1,0:T(8,128)S(1)}, f32[48,128]{1,0:T(8,128)S(1)}, u32[]{:S(2)}, u32[]{:S(2)}) collective-permute-start(f32[48,128]{1,0:T(8,128)S(1)} %get-tuple-element.71.refs_7_), channel_id=1, source_target_pairs={{0,24},{8,0},{16,8},{24,16},{1,25},{9,1},{17,9},{25,17},{2,26},{10... | collective-permute-start | bytes 73736 | tf_op jit(solution)/shard_map/ppermute | solution.py:167
  21.6 4.5 %collective-permute-start.9 = (f32[48,128]{1,0:T(8,128)S(1)}, f32[48,128]{1,0:T(8,128)S(1)}, u32[]{:S(2)}, u32[]{:S(2)}) collective-permute-start(f32[48,128]{1,0:T(8,128)S(1)} %get-tuple-element.71.refs_7_), channel_id=1, source_target_pairs={{0,16},{8,24},{16,0},{24,8},{1,17},{9,25},{17,1},{25,9},{2,18},{10... | collective-permute-start | bytes 73736 | tf_op jit(solution)/shard_map/ppermute | solution.py:167
  24.1 12.0 %collective-permute-start.14 = (f32[256,128]{1,0:T(8,128)S(1)}, f32[256,128]{1,0:T(8,128)S(1)}, u32[]{:S(2)}, u32[]{:S(2)}) collective-permute-start(f32[256,128]{1,0:T(8,128)S(1)} %shard_map.94), channel_id=1, source_target_pairs={{0,8},{8,16},{16,24},{24,0},{1,9},{9,17},{17,25},{25,1},{2,10},{10... | collective-permute-start | bytes 393224 | tf_op jit(solution)/shard_map/ppermute | solution.py:167
  26.1 4.7 %collective-permute-start.8 = (f32[48,128]{1,0:T(8,128)S(1)}, f32[48,128]{1,0:T(8,128)S(1)}, u32[]{:S(2)}, u32[]{:S(2)}) collective-permute-start(f32[48,128]{1,0:T(8,128)S(1)} %get-tuple-element.71.refs_7_), channel_id=1, source_target_pairs={{0,8},{8,16},{16,24},{24,0},{1,9},{9,17},{17,25},{25,1},{2,10},{10... | collective-permute-start | bytes 73736 | tf_op jit(solution)/shard_map/ppermute | solution.py:167
  31.4 1.2 %collective-permute-start.11 = (f32[32,128]{1,0:T(8,128)S(1)}, f32[32,128]{1,0:T(8,128)S(1)}, u32[]{:S(2)}, u32[]{:S(2)}) collective-permute-start(f32[32,128]{1,0:T(8,128)S(1)} %get-tuple-element.75), channel_id=1, source_target_pairs={{0,1},{1,0},{2,3},{3,2},{4,5},{5,4},{6,7},{7,6},{8,9},{9,8},{10,11... | collective-permute-start | bytes 49160 | tf_op jit(solution)/shard_map/ppermute | solution.py:161
  32.9 5.1 %collective-permute-start.12 = (f32[32,128]{1,0:T(8,128)S(1)}, f32[32,128]{1,0:T(8,128)S(1)}, u32[]{:S(2)}, u32[]{:S(2)}) collective-permute-start(f32[32,128]{1,0:T(8,128)S(1)} %get-tuple-element.80), channel_id=1, source_target_pairs={{0,1},{1,0},{2,3},{3,2},{4,5},{5,4},{6,7},{7,6},{8,9},{9,8},{10,11... | collective-permute-start | bytes 49160 | tf_op jit(solution)/shard_map/ppermute | solution.py:161
  33.3 5.0 %collective-permute-start.13 = (f32[32,128]{1,0:T(8,128)S(1)}, f32[32,128]{1,0:T(8,128)S(1)}, u32[]{:S(2)}, u32[]{:S(2)}) collective-permute-start(f32[32,128]{1,0:T(8,128)S(1)} %get-tuple-element.81), channel_id=1, source_target_pairs={{0,7},{1,2},{2,1},{3,4},{4,3},{5,6},{6,5},{7,0},{8,15},{9,10},{10,... | collective-permute-start | bytes 49160 | tf_op jit(solution)/shard_map/ppermute | solution.py:164
